TPU v7x, 32 devices: a whole 2x2x4 slice. The times are simulated.
32 devices in a mesh: ctx: 8 (over z, x), tp: 4 (over y, core).
Axes of the slice: x: 2, y: 2, z: 4, core: 2. Of those that a mesh axis runs over, the one named last changes fastest.
Arguments:
- layer_input: bfloat16 [4096, 1536], P('ctx'), may hold values from -6 to 6
- segment_ids: int32 [4096], P('ctx'), may hold values from 0 to 3, as said below
- positions: int32 [4096], P('ctx'), may hold values from 0 to 4095, as said below
- attn_gain: bfloat16 [1536], replicated, may hold values from 0.5 to 1.5
- q_weight: bfloat16 [1536, 1536], P(None, 'tp'), may hold values from -0.15625 to 0.15625
- q_bias: bfloat16 [12, 128], P('tp'), may hold values from -3 to 3
- kv_weight: bfloat16 [1536, 512], replicated, may hold values from -0.15625 to 0.15625
- kv_bias: bfloat16 [512], replicated, may hold values from -0.59765625 to 0.59765625
- o_weight: bfloat16 [1536, 1536], P('tp'), may hold values from -1 to 1
- mlp_gain: bfloat16 [1536], replicated, may hold values from 0.5 to 1.5
- gate_weight: bfloat16 [1536, 8960], P(None, 'tp'), may hold values from -0.15625 to 0.15625
- up_weight: bfloat16 [1536, 8960], P(None, 'tp'), may hold values from -0.15625 to 0.15625
- down_weight: bfloat16 [8960, 1536], P('tp'), may hold values from -0.0625 to 0.0625
- cotangent: bfloat16 [4096, 1536], P('ctx'), may hold values from -6 to 6
Outputs:
- layer_output: bfloat16 [4096, 1536], P('ctx')
- dx: float32 [4096, 1536], P('ctx')
- g_attn_gain: float32 [1536], P('ctx')
- g_q_weight: float32 [1536, 1536], P('ctx', 'tp')
- g_q_bias: float32 [12, 128], P('tp', 'ctx')
- g_kv_weight: float32 [1536, 512], P(('ctx', 'tp'))
- g_kv_bias: float32 [512], P(('ctx', 'tp'))
- g_o_weight: float32 [1536, 1536], P('tp', 'ctx')
- g_mlp_gain: float32 [1536], P('ctx')
- g_gate_weight: float32 [1536, 8960], P('ctx', 'tp')
- g_up_weight: float32 [1536, 8960], P('ctx', 'tp')
- g_down_weight: float32 [8960, 1536], P('tp', 'ctx')
Inputs may be any that keep to these rules, and one draw needn't show every extreme that they name: `segment_ids`: segment ids never fall along the row and number four documents: document 0 and documents 2 and 3 hold 1 to 128 tokens each, document 1 holds all the others. Within a document the positions rise by one from token to token; document 0 starts at 0, documents 2 and 3 at an offset below 1024, and the positions of document 1 end at 4095.
All inputs are finite; a program needn't handle non-finite values.
Results may differ from a plain program's by a relative error of at most 0.02.
Values may be sent and summed in bfloat16 or wider, within the bound.
No kernel may reach another device: no remote copies, remote signals or barrier semaphores. Data moves between devices by JAX's collectives and lax.ppermute only.
A program may use at most 192 MiB of HBM per device.

v0:
```python
import math

import jax
import jax.numpy as jnp
from jax import lax
from jax.sharding import PartitionSpec as P

KEY_BLOCK = 1024


rms_eps = 1e-06
rope_base = 1000000.0
masked_score = -1000000000.0


def rms_norm(values, gain):
    factor = lax.rsqrt(jnp.mean(values * values, axis=-1, keepdims=True) + rms_eps)
    return values * factor * gain


def rotate(values, positions):
    half_width = values.shape[-1] // 2
    steps_up = jnp.arange(half_width, dtype=jnp.float32)
    freqs = rope_base ** (-2.0 * steps_up / values.shape[-1])
    angles = positions.astype(jnp.float32)[:, None] * freqs[None, :]
    cosine = jnp.cos(angles)[:, None, :]
    sine = jnp.sin(angles)[:, None, :]
    first_half = values[..., :half_width]
    second_half = values[..., half_width:]
    return jnp.concatenate(
        [first_half * cosine - second_half * sine, second_half * cosine + first_half * sine],
        axis=-1,
    )


def block_rows(count):
    return math.gcd(count, KEY_BLOCK)


def block_weights(query_rot, query_seg, first_query, keys, key_seg, first_key):
    scores = jnp.einsum(
        "qhd,kd->qhk", query_rot, keys, preferred_element_type=jnp.float32
    ) * keys.shape[-1] ** (-0.5)
    key_index = first_key + jnp.arange(keys.shape[0], dtype=jnp.int32)
    query_index = first_query + jnp.arange(query_rot.shape[0], dtype=jnp.int32)
    allowed = (key_index[None, :] <= query_index[:, None]) & (
        key_seg[None, :] == query_seg[:, None]
    )
    return jnp.exp(jnp.where(allowed[:, None, :], scores, masked_score))


def forward_step(state, piece, first_key, query_rot, query_seg, first_query):
    keys, values, key_seg = piece
    last_query = first_query + query_rot.shape[0] - 1

    def forward_compute(current):
        totals, weighted = current
        weights = block_weights(query_rot, query_seg, first_query, keys, key_seg, first_key)
        totals = totals + jnp.sum(weights, axis=-1)
        weighted = weighted + jnp.einsum(
            "qhk,kd->qhd", weights.astype(jnp.bfloat16), values, preferred_element_type=jnp.float32
        )
        return (totals, weighted)

    def keep(current):
        return current

    return lax.cond(first_key > last_query, keep, forward_compute, state)


def fold_blocks(step, state, pieces):
    count = pieces[0].shape[0]
    size = block_rows(count)
    split = tuple((member.reshape((count // size, size) + member.shape[1:]) for member in pieces))

    def advance(current, block_item):
        block_number, block_pieces = block_item
        return (step(current, block_pieces, block_number * size), None)

    state, _ = lax.scan(advance, state, (jnp.arange(count // size, dtype=jnp.int32), split))
    return state


def backward_step(
    d_query_rot, block_item, query_rot, query_seg, first_query, d_weighted, delta, size
):
    block_number, keys, values, key_seg = block_item
    first_key = block_number * size
    last_query = first_query + query_rot.shape[0] - 1
    scale = keys.shape[-1] ** (-0.5)

    def backward_compute(current):
        weights = block_weights(query_rot, query_seg, first_query, keys, key_seg, first_key)
        d_probs = jnp.einsum("qhd,kd->qhk", d_weighted, values, preferred_element_type=jnp.float32)
        d_scores = (weights * (d_probs - delta[:, :, None])).astype(jnp.bfloat16)
        current = (
            current
            + jnp.einsum("qhk,kd->qhd", d_scores, keys, preferred_element_type=jnp.float32) * scale
        )
        d_keys = (
            jnp.einsum("qhk,qhd->kd", d_scores, query_rot, preferred_element_type=jnp.float32)
            * scale
        )
        d_values = jnp.einsum(
            "qhk,qhd->kd",
            weights.astype(jnp.bfloat16),
            d_weighted,
            preferred_element_type=jnp.float32,
        )
        return (current, jnp.concatenate([d_keys, d_values], axis=-1))

    def skip(current):
        return (current, jnp.zeros((keys.shape[0], 2 * keys.shape[1]), jnp.float32))

    return lax.cond(first_key > last_query, skip, backward_compute, d_query_rot)


def swiglu(gate_in, up_in):
    return jax.nn.silu(gate_in) * up_in


def per_device(
    layer_input,
    segment_ids,
    positions,
    attn_gain,
    q_weight,
    q_bias,
    kv_weight,
    kv_bias,
    o_weight,
    mlp_gain,
    gate_weight,
    up_weight,
    down_weight,
    cotangent,
):
    tok_rows, model_width = layer_input.shape
    local_heads, head_dim = q_bias.shape
    kv_heads = kv_bias.shape[0] // (2 * head_dim)
    sharing = local_heads * lax.axis_size("tp") // kv_heads
    kv_head = lax.axis_index("tp") * local_heads // sharing
    first_query = lax.axis_index("ctx") * tok_rows
    key_start = kv_head * head_dim
    value_start = key_start + kv_heads * head_dim
    inputs = layer_input.astype(jnp.float32)
    attn_gain_f = attn_gain.astype(jnp.float32)
    normed = rms_norm(inputs, attn_gain_f).astype(jnp.bfloat16)
    query = jnp.dot(normed, q_weight, preferred_element_type=jnp.float32) + q_bias.astype(
        jnp.float32
    ).reshape(-1)
    query_rot = rotate(query.reshape(tok_rows, local_heads, head_dim), positions).astype(
        jnp.bfloat16
    )
    key_cols = lax.dynamic_slice_in_dim(kv_weight, key_start, head_dim, 1)
    value_cols = lax.dynamic_slice_in_dim(kv_weight, value_start, head_dim, 1)
    both_cols = jnp.concatenate([key_cols, value_cols], axis=1)
    bias_full = kv_bias.astype(jnp.float32)
    both_bias = jnp.concatenate(
        [
            lax.dynamic_slice_in_dim(bias_full, key_start, head_dim, 0),
            lax.dynamic_slice_in_dim(bias_full, value_start, head_dim, 0),
        ]
    )
    key_value = jnp.dot(normed, both_cols, preferred_element_type=jnp.float32) + both_bias
    key_rot = rotate(key_value[:, None, :head_dim], positions)[:, 0, :].astype(jnp.bfloat16)
    value_low = key_value[:, head_dim:].astype(jnp.bfloat16)

    def forward_fold(state, piece):

        def step(current, block_pieces, block_first):
            return forward_step(
                current, block_pieces, block_first, query_rot, segment_ids, first_query
            )

        return fold_blocks(step, state, piece)

    start_state = (
        jnp.zeros((tok_rows, local_heads), jnp.float32),
        jnp.zeros((tok_rows, local_heads, head_dim), jnp.float32),
    )
    totals, weighted = forward_fold(
        start_state,
        (
            lax.all_gather(key_rot, "ctx", axis=0, tiled=True),
            lax.all_gather(value_low, "ctx", axis=0, tiled=True),
            lax.all_gather(segment_ids, "ctx", axis=0, tiled=True),
        ),
    )
    attended = weighted / totals[:, :, None]
    attended_low = attended.astype(jnp.bfloat16).reshape(tok_rows, local_heads * head_dim)
    attn_part = jnp.dot(attended_low, o_weight, preferred_element_type=jnp.float32)
    hidden_in = inputs + lax.psum(attn_part, "tp")
    mlp_gain_f = mlp_gain.astype(jnp.float32)
    normed_two = rms_norm(hidden_in, mlp_gain_f).astype(jnp.bfloat16)
    gate = jnp.dot(normed_two, gate_weight, preferred_element_type=jnp.float32)
    up_proj = jnp.dot(normed_two, up_weight, preferred_element_type=jnp.float32)
    hidden_f, swiglu_pull = jax.vjp(swiglu, gate, up_proj)
    hidden = hidden_f.astype(jnp.bfloat16)
    mlp_part = jnp.dot(hidden, down_weight, preferred_element_type=jnp.float32)
    output = (hidden_in + lax.psum(mlp_part.astype(jnp.bfloat16), "tp").astype(jnp.float32)).astype(
        jnp.bfloat16
    )
    d_output = cotangent.astype(jnp.float32)
    d_hidden = jnp.einsum("td,fd->tf", cotangent, down_weight, preferred_element_type=jnp.float32)
    d_gate, d_up = swiglu_pull(d_hidden)
    d_gate = d_gate.astype(jnp.bfloat16)
    d_up = d_up.astype(jnp.bfloat16)
    g_down = jnp.einsum("tf,td->fd", hidden, cotangent, preferred_element_type=jnp.float32)
    g_gate = jnp.einsum("td,tf->df", normed_two, d_gate, preferred_element_type=jnp.float32)
    g_up = jnp.einsum("td,tf->df", normed_two, d_up, preferred_element_type=jnp.float32)
    d_normed_two = jnp.einsum(
        "tf,df->td", d_gate, gate_weight, preferred_element_type=jnp.float32
    ) + jnp.einsum("tf,df->td", d_up, up_weight, preferred_element_type=jnp.float32)
    d_normed_two = lax.psum(d_normed_two, "tp")
    _, norm_two_pull = jax.vjp(rms_norm, hidden_in, mlp_gain_f)
    d_norm_in, g_mlp_gain = norm_two_pull(d_normed_two)
    d_hidden_in = d_output + d_norm_in
    d_attn = d_hidden_in.astype(jnp.bfloat16)
    g_o = jnp.einsum("tc,td->cd", attended_low, d_attn, preferred_element_type=jnp.float32)
    d_attended = jnp.einsum(
        "td,cd->tc", d_attn, o_weight, preferred_element_type=jnp.float32
    ).reshape(tok_rows, local_heads, head_dim)
    d_weighted = (d_attended / totals[:, :, None]).astype(jnp.bfloat16)
    delta = jnp.sum(d_attended * attended, axis=-1) / totals
    full_keys = (
        lax.all_gather(key_rot, "ctx", axis=0, tiled=True),
        lax.all_gather(value_low, "ctx", axis=0, tiled=True),
        lax.all_gather(segment_ids, "ctx", axis=0, tiled=True),
    )
    all_key_rot, all_values, all_seg = full_keys
    key_count = all_key_rot.shape[0]
    size = block_rows(key_count)
    blocks = key_count // size

    def backward_scan(current, block_item):
        return backward_step(
            current, block_item, query_rot, segment_ids, first_query, d_weighted, delta, size
        )

    scan_items = (
        jnp.arange(blocks, dtype=jnp.int32),
        all_key_rot.reshape(blocks, size, head_dim),
        all_values.reshape(blocks, size, head_dim),
        all_seg.reshape(blocks, size),
    )
    d_query_rot, key_grads = lax.scan(
        backward_scan, jnp.zeros((tok_rows, local_heads, head_dim), jnp.float32), scan_items
    )
    own_grads = lax.psum_scatter(
        key_grads.reshape(key_count, 2 * head_dim).astype(jnp.bfloat16),
        "ctx",
        scatter_dimension=0,
        tiled=True,
    ).astype(jnp.float32)
    d_query = (
        rotate(d_query_rot, -positions)
        .astype(jnp.bfloat16)
        .reshape(tok_rows, local_heads * head_dim)
    )
    d_key = rotate(own_grads[:, None, :head_dim], -positions)[:, 0, :].astype(jnp.bfloat16)
    d_value = own_grads[:, head_dim:].astype(jnp.bfloat16)
    d_both = jnp.concatenate([d_key, d_value], axis=1)
    g_q = jnp.einsum("td,tc->dc", normed, d_query, preferred_element_type=jnp.float32)
    g_q_bias = jnp.sum(d_query.astype(jnp.float32), axis=0).reshape(local_heads, head_dim)
    g_both = jnp.einsum("td,tc->dc", normed, d_both, preferred_element_type=jnp.float32)
    g_both_bias = jnp.sum(d_both.astype(jnp.float32), axis=0)
    g_kv = jnp.zeros((model_width, kv_bias.shape[0]), jnp.float32)
    g_kv = lax.dynamic_update_slice_in_dim(g_kv, g_both[:, :head_dim], key_start, 1)
    g_kv = lax.dynamic_update_slice_in_dim(g_kv, g_both[:, head_dim:], value_start, 1)
    g_kv_bias = jnp.zeros((kv_bias.shape[0],), jnp.float32)
    g_kv_bias = lax.dynamic_update_slice_in_dim(g_kv_bias, g_both_bias[:head_dim], key_start, 0)
    g_kv_bias = lax.dynamic_update_slice_in_dim(g_kv_bias, g_both_bias[head_dim:], value_start, 0)
    d_normed = jnp.einsum(
        "tc,dc->td", d_query, q_weight, preferred_element_type=jnp.float32
    ) + jnp.einsum("tc,dc->td", d_both, both_cols, preferred_element_type=jnp.float32)
    d_normed = lax.psum(d_normed.astype(jnp.bfloat16), "tp").astype(jnp.float32)
    _, norm_one_pull = jax.vjp(rms_norm, inputs, attn_gain_f)
    d_norm_one, g_attn_gain = norm_one_pull(d_normed)
    d_inputs = d_hidden_in + d_norm_one
    kv_sent = (
        lax.psum_scatter(g_kv, ("ctx", "tp"), scatter_dimension=0, tiled=True),
        lax.psum_scatter(g_kv_bias, ("ctx", "tp"), scatter_dimension=0, tiled=True),
    )
    every_grad = (
        lax.psum_scatter(
            g_attn_gain.astype(jnp.bfloat16), "ctx", scatter_dimension=0, tiled=True
        ).astype(jnp.float32),
        lax.psum_scatter(g_q.astype(jnp.bfloat16), "ctx", scatter_dimension=0, tiled=True).astype(
            jnp.float32
        ),
        lax.psum_scatter(
            g_q_bias.astype(jnp.bfloat16), "ctx", scatter_dimension=1, tiled=True
        ).astype(jnp.float32),
        lax.psum_scatter(g_o.astype(jnp.bfloat16), "ctx", scatter_dimension=1, tiled=True).astype(
            jnp.float32
        ),
        lax.psum_scatter(
            g_mlp_gain.astype(jnp.bfloat16), "ctx", scatter_dimension=0, tiled=True
        ).astype(jnp.float32),
        lax.psum_scatter(
            g_gate.astype(jnp.bfloat16), "ctx", scatter_dimension=0, tiled=True
        ).astype(jnp.float32),
        lax.psum_scatter(g_up.astype(jnp.bfloat16), "ctx", scatter_dimension=0, tiled=True).astype(
            jnp.float32
        ),
        lax.psum_scatter(
            g_down.astype(jnp.bfloat16), "ctx", scatter_dimension=1, tiled=True
        ).astype(jnp.float32),
    )
    out_attn_gain, out_q, out_q_bias, out_o, out_mlp_gain, out_gate, out_up, out_down = every_grad
    out_kv, out_kv_bias = kv_sent
    return (
        output,
        d_inputs,
        out_attn_gain,
        out_q,
        out_q_bias,
        out_kv,
        out_kv_bias,
        out_o,
        out_mlp_gain,
        out_gate,
        out_up,
        out_down,
    )


def solution(mesh):
    return jax.shard_map(
        per_device,
        mesh=mesh,
        in_specs=(
            P("ctx", None),
            P("ctx"),
            P("ctx"),
            P(),
            P(None, "tp"),
            P("tp", None),
            P(),
            P(),
            P("tp", None),
            P(),
            P(None, "tp"),
            P(None, "tp"),
            P("tp", None),
            P("ctx", None),
        ),
        out_specs=(
            P("ctx", None),
            P("ctx", None),
            P("ctx"),
            P("ctx", "tp"),
            P("tp", "ctx"),
            P(("ctx", "tp"), None),
            P(("ctx", "tp")),
            P("tp", "ctx"),
            P("ctx"),
            P("ctx", "tp"),
            P("ctx", "tp"),
            P("tp", "ctx"),
        ),
        check_vma=False,
    )
```

profile of v0, /device:TPU:0, one launch (start us, length us, event | category | flops | bytes accessed | tf_op | source)
XLA Modules:
  0.0 1231.4 jit_solution(16032636924949571685)
XLA Ops:
  21.9 27.9 %all-gather.1 = s32[8,1,512]{2,1,0:T(1,128)S(1)} all-gather(s32[1,1,512]{2,1,0:T(1,128)S(1)} %bitcast.135), channel_id=1, replica_groups=mesh['ctx'=8,'tp'=4] {'ctx'}, dimensions={0}, use_global_device_ids=true | all-gather | bytes 18432 | tf_op jit(solution)/shard_map/all_gather | solution.py:187
  59.2 38.8 %all-gather.5.cloned.1.call-done = bf16[4096,128]{0,1:T(8,128)(2,1)} async-done(((bf16[512,128]{0,1:T(8,128)(2,1)}), bf16[4096,128]{0,1:T(8,128)(2,1)}) %all-gather.5.cloned.1.call-update) | async-done | bytes 1048592 | tf_op jit(solution)/shard_map/all_gather | solution.py:186
  100.3 12.3 while.31
  119.7 87.6 %all-reduce.9.cloned.1.call-done = f32[512,1536]{1,0:T(8,128)} async-done(((f32[512,1536]{1,0:T(8,128)}), f32[512,1536]{1,0:T(8,128)}) %all-reduce.9.cloned.1.call-update) | async-done | bytes 3145744 | tf_op jit(solution)/shard_map/psum | solution.py:193
  210.6 9.7 fusion.92
  225.9 11.5 multiply_convert_fusion
  250.0 68.5 %all-reduce.11.cloned.1.call-done = f32[512,1536]{1,0:T(8,128)} async-done(((f32[512,1536]{1,0:T(8,128)}), f32[512,1536]{1,0:T(8,128)}) %all-reduce.11.cloned.1.call-update) | async-done | bytes 3145744 | tf_op jit(solution)/shard_map/psum | solution.py:215
  327.4 21.4 %while.32 = (s32[]{:T(128)}, f32[512,3,128]{2,0,1:T(8,128)S(1)}, bf16[4,1024,256]{1,2,0:T(8,128)(2,1)}, s32[4]{0:T(128)S(1)}, s32[]{:T(128)}, /*index=5*/s32[]{:...) while((s32[]{:T(128)}, f32[512,3,128]{2,0,1:T(8,128)S(1)}, ...), condition=%wide.region_15.16_spmd, body=%wide.region_12.15_spmd.sunk | while | flops 2029127168 | bytes 38046016 | solution.py:247
  328.6 12.8 %conditional.5 = (f32[512,3,128]{2,0,1:T(8,128)S(1)}, bf16[1,1024,256]{1,2,0:T(8,128)(2,1)S(1)}) conditional(s32[]{:T(128)} %convert_element_type.289, (s32[]{:T(128)}, s32[]{:T(128)}, s32[4,1024]{1,0:T(4,128)}, s32[]{:T(128)}, s32[512]{0:T(512)S(1)}, /*index=5*/bf16[4,1024,128]{2,1,0:T(8,128)(2,1)}, bf16[512,3,128]{0,2,1:T(8,128)(2,1)}, ...), branch_computations={%region_13.13_spmd, %region_14.14_spmd} | conditional | flops 2029127168 | bytes 36996664 | solution.py:115
  360.1 8.7 convolution_convert_fusion.3
  371.5 87.2 %reduce-scatter.11.cloned.1.call-done = bf16[512,256]{0,1:T(8,128)(2,1)} async-done(((bf16[4096,256]{0,1:T(8,128)(2,1)}), bf16[512,256]{0,1:T(8,128)(2,1)}) %reduce-scatter.11.cloned.1.call-update) | async-done | bytes 262160 | tf_op jit(solution)/shard_map/reduce_scatter | solution.py:250
  464.1 8.9 convolution_convert_fusion.2
  473.3 9.0 convolution_convert_fusion.1
  482.4 8.8 convolution_convert_fusion
  497.5 17.3 %reduce-scatter.25.cloned.1.call-done = bf16[16,3]{1,0:T(8,128)(2,1)} async-done(((bf16[128,3]{1,0:T(8,128)(2,1)}), bf16[16,3]{1,0:T(8,128)(2,1)}) %reduce-scatter.25.cloned.1.call-update) | async-done | bytes 112
  516.2 65.7 %reduce-scatter.13.cloned.1.call-done = bf16[192,384]{1,0:T(8,128)(2,1)} async-done(((bf16[1536,384]{1,0:T(8,128)(2,1)}), bf16[192,384]{1,0:T(8,128)(2,1)}) %reduce-scatter.13.cloned.1.call-update) | async-done | bytes 147472 | tf_op jit(solution)/shard_map/reduce_scatter | solution.py:289
  583.5 64.8 %reduce-scatter.17.cloned.1.call-done = bf16[384,192]{0,1:T(8,128)(2,1)} async-done(((bf16[384,1536]{0,1:T(8,128)(2,1)}), bf16[384,192]{0,1:T(8,128)(2,1)}) %reduce-scatter.17.cloned.1.call-update) | async-done | bytes 147472 | tf_op jit(solution)/shard_map/reduce_scatter | solution.py:295
  650.3 40.1 %all-reduce.1 = f32[512]{0:T(512)S(1)} all-reduce(f32[512]{0:T(512)S(1)} %slice_dynamic-update-slice_fusion.2), channel_id=8, replica_groups=mesh['ctx'=8,'tp'=4] {'ctx','tp'}, use_global_device_ids=true, to_apply=%region_26.27.clone | all-reduce | flops 512 | bytes 4096
  691.0 29.1 %all-reduce.13.cloned.1.call-done = (bf16[512,1536]{1,0:T(8,128)(2,1)}, bf16[512,1536]{1,0:T(8,128)(2,1)}) async-done(((bf16[512,1536]{1,0:T(8,128)(2,1)}, bf16[512,1536]{1,0:T(8,128)(2,1)}), (bf16[512,1536]{1,0:T(8,128)(2,1)}, bf16[512,1536]{1,0:T(8,128)(2,1)})) %all-reduce.13.cloned.1.call-update) | async-done | bytes 3145744 | tf_op jit(solution)/shard_map/psum | solution.py:201
  722.8 22.3 %all-reduce.3 = (bf16[1536]{0:T(1024)(128)(2,1)S(1)}, bf16[1536]{0:T(1024)(128)(2,1)S(1)}) all-reduce(bf16[1536]{0:T(1024)(128)(2,1)S(1)} %get-tuple-element.553, bf16[1536]{0:T(1024)(128)(2,1)S(1)} %copy-done.34), channel_id=4, replica_groups=mesh['ctx'=8,'tp'=4] {'ctx'}, use_global_device_ids=true, to_apply=%region_20.21.clone | all-reduce | flops 3072 | bytes 12288
  753.0 100.0 %reduce-scatter.19.cloned.1.call-done = bf16[192,2240]{1,0:T(8,128)(2,1)} async-done(((bf16[1536,2240]{1,0:T(8,128)(2,1)}), bf16[192,2240]{1,0:T(8,128)(2,1)}) %reduce-scatter.19.cloned.1.call-update) | async-done | bytes 860176 | tf_op jit(solution)/shard_map/reduce_scatter | solution.py:301
  855.6 129.7 %reduce-scatter.21.cloned.1.call-done = bf16[192,2240]{1,0:T(8,128)(2,1)} async-done(((bf16[1536,2240]{1,0:T(8,128)(2,1)}), bf16[192,2240]{1,0:T(8,128)(2,1)}) %reduce-scatter.21.cloned.1.call-update) | async-done | bytes 860176 | tf_op jit(solution)/shard_map/reduce_scatter | solution.py:304
  987.8 129.2 %reduce-scatter.23.cloned.1.call-done = bf16[2240,192]{0,1:T(8,128)(2,1)} async-done(((bf16[2240,1536]{0,1:T(8,128)(2,1)}), bf16[2240,192]{0,1:T(8,128)(2,1)}) %reduce-scatter.23.cloned.1.call-update) | async-done | bytes 860176 | tf_op jit(solution)/shard_map/reduce_scatter | solution.py:307
  1119.4 105.0 %reduce-scatter.15.cloned.1.call-done = f32[48,512]{1,0:T(8,128)} async-done(((f32[1536,512]{1,0:T(8,128)}), f32[48,512]{1,0:T(8,128)}) %reduce-scatter.15.cloned.1.call-update) | async-done | bytes 98320 | tf_op jit(solution)/shard_map/reduce_scatter | solution.py:282
  (238 shorter events, 147.6 us)
Async XLA Ops:
  7.2 108.5 %copy-start = (bf16[384,1536]{1,0:T(8,128)(2,1)S(1)}, bf16[384,1536]{1,0:T(8,128)(2,1)}, u32[]{:S(2)}) copy-start(bf16[384,1536]{1,0:T(8,128)(2,1)} %param.30) | copy-start | bytes 3538948
  7.2 49.7 %all-gather.7.cloned.1.call-start = ((), (), s32[]{:S(2)}) async-start(), calls=%async_computation.18 | async-start | bytes 1179648 | tf_op jit(solution)/shard_map/all_gather | solution.py:185
  14.3 83.7 %all-gather.5.cloned.1.call-start = ((), (), s32[]{:S(2)}) async-start(), calls=%async_computation.8 | async-start | bytes 1179648 | tf_op jit(solution)/shard_map/all_gather | solution.py:186
  15.0 192.3 %all-reduce.9.cloned.1.call-start = ((), (), s32[]{:S(2)}) async-start(), calls=%async_computation.9 | async-start | bytes 6291456 | tf_op jit(solution)/shard_map/psum | solution.py:193
  118.4 200.1 %all-reduce.11.cloned.1.call-start = ((), (), s32[]{:S(2)}) async-start(), calls=%async_computation.10 | async-start | bytes 6291456 | tf_op jit(solution)/shard_map/psum | solution.py:215
  209.7 10.7 copy-start.2
  220.4 17.1 %slice-start.2 = ((s8[6881280]{0:T(1024)(128)(4,1)}), s8[4194304]{0:T(1024)(128)(4,1)S(1)}, s32[]{:S(2)}) async-start(s8[6881280]{0:T(1024)(128)(4,1)} %bitcast.138), calls=%async_computation.23 | async-start | bytes 8388608
  225.9 11.5 slice-start.3
  249.8 209.0 %reduce-scatter.11.cloned.1.call-start = ((), (), s32[]{:S(2)}) async-start(), calls=%async_computation.11 | async-start | bytes 2359296 | tf_op jit(solution)/shard_map/reduce_scatter | solution.py:250
  352.1 162.8 %reduce-scatter.25.cloned.1.call-start = ((), (), s32[]{:S(2)}) async-start(), calls=%async_computation.19 | async-start | bytes 36864
  353.5 228.4 %reduce-scatter.13.cloned.1.call-start = ((), (), s32[]{:S(2)}) async-start(), calls=%async_computation.12 | async-start | bytes 1327104 | tf_op jit(solution)/shard_map/reduce_scatter | solution.py:289
  355.8 292.6 %reduce-scatter.17.cloned.1.call-start = ((), (), s32[]{:S(2)}) async-start(), calls=%async_computation.14 | async-start | bytes 1327104 | tf_op jit(solution)/shard_map/reduce_scatter | solution.py:295
  360.0 360.1 %all-reduce.13.cloned.1.call-start = ((), (), s32[]{:S(2)}) async-start(), calls=%async_computation.20 | async-start | bytes 6291456 | tf_op jit(solution)/shard_map/psum | solution.py:201
  368.8 90.9 %copy-start.27 = (f32[512]{0:T(512)S(1)}, f32[512]{0:T(512)}, u32[]{:S(2)}) copy-start(f32[512]{0:T(512)} %copy-done.26) | copy-start | bytes 6148
  368.8 90.9 %copy-start.36 = (f32[64]{0:T(128)S(1)}, f32[64]{0:T(128)}, u32[]{:S(2)}) copy-start(f32[64]{0:T(128)} %copy-done.35) | copy-start | bytes 772
  368.8 91.5 %copy-start.12 = (bf16[1536,128]{1,0:T(8,128)(2,1)S(1)}, bf16[1536,128]{1,0:T(8,128)(2,1)}, u32[]{:S(2)}) copy-start(bf16[1536,128]{1,0:T(8,128)(2,1)} %copy-done.11) | copy-start | bytes 1179652
  368.8 91.5 %copy-start.14 = (bf16[1536,128]{1,0:T(8,128)(2,1)S(1)}, bf16[1536,128]{1,0:T(8,128)(2,1)}, u32[]{:S(2)}) copy-start(bf16[1536,128]{1,0:T(8,128)(2,1)} %copy-done.13) | copy-start | bytes 1179652
  464.1 388.9 %reduce-scatter.19.cloned.1.call-start = ((), (), s32[]{:S(2)}) async-start(), calls=%async_computation.15 | async-start | bytes 7962624 | tf_op jit(solution)/shard_map/reduce_scatter | solution.py:301
  473.0 512.2 %reduce-scatter.21.cloned.1.call-start = ((), (), s32[]{:S(2)}) async-start(), calls=%async_computation.16 | async-start | bytes 7962624 | tf_op jit(solution)/shard_map/reduce_scatter | solution.py:304
  482.3 634.6 %reduce-scatter.23.cloned.1.call-start = ((), (), s32[]{:S(2)}) async-start(), calls=%async_computation.17 | async-start | bytes 7962624 | tf_op jit(solution)/shard_map/reduce_scatter | solution.py:307
  491.2 733.2 %reduce-scatter.15.cloned.1.call-start = ((), (), s32[]{:S(2)}) async-start(), calls=%async_computation.13 | async-start | bytes 3244032 | tf_op jit(solution)/shard_map/reduce_scatter | solution.py:282
  496.2 226.5 %copy-start.34 = (bf16[1536]{0:T(1024)(128)(2,1)S(1)}, bf16[1536]{0:T(1024)(128)(2,1)}, u32[]{:S(2)}) copy-start(bf16[1536]{0:T(1024)(128)(2,1)} %get-tuple-element.551) | copy-start | bytes 9220
  496.2 249.5 %copy-start.31 = (f32[512]{0:T(512)S(1)}, f32[512]{0:T(512)}, u32[]{:S(2)}) copy-start(f32[512]{0:T(512)} %copy-done.30) | copy-start | bytes 6148
  853.0 371.4 %copy-start.1 = (bf16[384,1536]{1,0:T(8,128)(2,1)S(1)}, bf16[384,1536]{1,0:T(8,128)(2,1)}, u32[]{:S(2)}) copy-start(bf16[384,1536]{1,0:T(8,128)(2,1)} %param.30) | copy-start | bytes 3538948
  (35 other events, 148.3 us)
Sparse Core Ops, SparseCore 0:
  14.4 42.4 all-gather.6
  59.5 38.3 all-gather.4
  118.5 88.7 all-reduce.8
  249.9 68.5 all-reduce.10
  352.2 106.5 reduce-scatter.10
  462.3 52.4 reduce-scatter.24
  518.8 63.0 reduce-scatter.12
  585.3 63.0 reduce-scatter.16
  651.9 68.1 all-reduce.12
  723.6 129.3 reduce-scatter.18
  857.1 128.0 reduce-scatter.20
  988.8 128.0 reduce-scatter.22
  1123.8 100.5 reduce-scatter.14
where the time goes:
time: 1240 us; the launch traced here: 1230 us
  waiting for transfers between devices  930 us (75%)
  matrix products  111 us (9%)
  blocking collectives  90.3 us (7%)
  other arithmetic  42.8 us (3%)
  local copies, waits for them, and re-layouts  35 us (3%)
  between operations  15.7 us (1%)
    reduce_scatter x1, waiting for transfers between devices, per_device(): lax.psum_scatter(g_up.astype(jnp.bfloat16), 'ctx', scatter_dimension=0, t...  130 us
    reduce_scatter x1, waiting for transfers between devices, per_device(): lax.psum_scatter(g_down.astype(jnp.bfloat16), 'ctx', scatter_dimension=1,...  129 us
    reduce_scatter x1, waiting for transfers between devices, per_device(): lax.psum_scatter(g_kv, ('ctx', 'tp'), scatter_dimension=0, tiled=True)  105 us
    reduce_scatter x1, waiting for transfers between devices, per_device(): lax.psum_scatter(g_gate.astype(jnp.bfloat16), 'ctx', scatter_dimension=0,...  100 us
    psum x1, waiting for transfers between devices, per_device(): hidden_in = inputs + lax.psum(attn_part, 'tp')  87.6 us
    reduce_scatter x1, waiting for transfers between devices, per_device(): lax.psum_scatter(key_grads.reshape(key_count, 2 * head_dim).astype(jnp.bf...  87.2 us
    psum x1, waiting for transfers between devices, per_device(): d_normed_two = lax.psum(d_normed_two, 'tp')  68.5 us
    reduce_scatter x1, waiting for transfers between devices, per_device(): lax.psum_scatter(g_q.astype(jnp.bfloat16), 'ctx', scatter_dimension=0, ti...  65.7 us
  transfers between devices with their start and end apart: 13, of which 13 were waited for; matrix products, arithmetic and copies ran while one was open for 7% of the time, Pallas kernels for 0%

commit v1 on v0

v1 whole, which is shorter than its diff:
```python
import functools

import jax
import jax.numpy as jnp
from jax import lax
from jax.experimental import pallas as pl
from jax.experimental.pallas import tpu as pltpu
from jax.sharding import PartitionSpec as P

RMS_EPS = 1e-06
ROPE_BASE = 1000000.0
LOG2E = 1.4426950408889634
BF16 = jnp.bfloat16
F32 = jnp.float32
EXTRA = 16


def mm(a, b, ca, cb):
    return lax.dot_general(a, b, (((ca,), (cb,)), ((), ())), preferred_element_type=F32)


def rope_tables(positions, head_dim):
    half = head_dim // 2
    freqs = ROPE_BASE ** (-2.0 * jnp.arange(half, dtype=F32) / head_dim)
    angles = positions.astype(F32)[:, None] * freqs[None, :]
    return jnp.cos(angles), jnp.sin(angles)


def rotate(values, cosine, sine):
    half = cosine.shape[-1]
    first, second = values[..., :half], values[..., half:]
    return jnp.concatenate([first * cosine - second * sine, second * cosine + first * sine], axis=-1)


def swap_core(x):
    return lax.ppermute(x, "tp", [(0, 1), (1, 0), (2, 3), (3, 2)])


def swap_y(x):
    return lax.ppermute(x, "tp", [(0, 2), (2, 0), (1, 3), (3, 1)])


def gather_tp(x, core, y):
    mate = swap_core(x)
    far = swap_y(x)
    far_mate = swap_core(far)
    a0, a1 = jnp.where(core == 0, x, mate), jnp.where(core == 0, mate, x)
    b0, b1 = jnp.where(core == 0, far, far_mate), jnp.where(core == 0, far_mate, far)
    return [
        jnp.where(y == 0, a0, b0),
        jnp.where(y == 0, a1, b1),
        jnp.where(y == 0, b0, a0),
        jnp.where(y == 0, b1, a1),
    ]


def sum_tp(part, core):
    rows = part.shape[0] // 2
    keep = lax.dynamic_slice_in_dim(part, core * rows, rows, 0)
    give = lax.dynamic_slice_in_dim(part, (1 - core) * rows, rows, 0).astype(BF16)
    half = (keep + swap_core(give).astype(F32)).astype(BF16)
    half = (half.astype(F32) + swap_y(half).astype(F32)).astype(BF16)
    mate = swap_core(half)
    return jnp.concatenate([jnp.where(core == 0, half, mate), jnp.where(core == 0, mate, half)], axis=0)


def sum_scatter(parts):
    got = lax.all_to_all(parts, "ctx", split_axis=0, concat_axis=0, tiled=True)
    return jnp.sum(got.astype(F32), axis=0)


def block_bounds(scal, rows):
    return lax.div(scal[1], rows), scal[0] + 1


def probs_t(scal, kb, qh, lo_row, b, rows, factor, shift, masked):
    s = mm(kb, qh, 1, 1) * factor
    if shift is not None:
        s = s - shift
    p = jnp.exp2(s)
    if masked:
        key = b * rows + lax.broadcasted_iota(jnp.int32, p.shape, 0)
        query = scal[0] * p.shape[1] + lax.broadcasted_iota(jnp.int32, p.shape, 1)
        p = jnp.where((key <= query) & (key >= lo_row), p, 0.0)
    return p


def for_blocks(scal, rows, run):
    start, stop = block_bounds(scal, rows)

    def body(b, carry):
        plain = (b < scal[0]) & (scal[2] <= b * rows)

        @pl.when(plain)
        def _():
            run(b, False)

        @pl.when(jnp.logical_not(plain))
        def _():
            run(b, True)

        return carry

    lax.fori_loop(start, stop, body, 0)


def attend_kernel(scal, q_ref, mine_ref, other_ref, lo_ref, att_ref, log_ref, acc, tot):
    rows, width = q_ref.shape
    hd = mine_ref.shape[2]
    heads = width // hd
    factor = LOG2E * hd**-0.5
    acc[...] = jnp.zeros_like(acc)
    tot[...] = jnp.zeros_like(tot)

    def run(b, masked):
        a = mine_ref[b, 0:rows, :]
        o = other_ref[b, 0:rows, :]
        kb = jnp.where(scal[3] == 0, a, o)
        vt = jnp.where(scal[3] == 0, o, a).astype(F32).T.astype(BF16)
        for h in range(heads):
            p = probs_t(
                scal, kb, q_ref[:, h * hd : (h + 1) * hd], lo_ref[...], b, rows, factor, None, masked
            )
            tot[h] += jnp.sum(p.reshape(rows // 8, 8, p.shape[1]), axis=0)
            acc[h] += mm(vt, p.astype(BF16), 1, 0)

    for_blocks(scal, rows, run)
    for h in range(heads):
        total = jnp.sum(tot[h], axis=0, keepdims=True)
        att_ref[:, h * hd : (h + 1) * hd] = (acc[h] / total).T.astype(BF16)
        log_ref[h] = jnp.broadcast_to(jnp.log2(total), log_ref.shape[1:])


def attend_back_kernel(
    scal, q_ref, mine_ref, other_ref, lo_ref, att_ref, log_ref, d_ref, dq_ref, dk_ref, dv_ref, acc, delta
):
    rows, width = q_ref.shape
    hd = mine_ref.shape[2]
    heads = width // hd
    scale = hd**-0.5
    factor = LOG2E * scale
    acc[...] = jnp.zeros_like(acc)
    for h in range(heads):
        cols = slice(h * hd, (h + 1) * hd)
        both = d_ref[:, cols].astype(F32) * att_ref[:, cols].astype(F32)
        delta[h] = jnp.broadcast_to(jnp.sum(both.T, axis=0, keepdims=True), delta.shape[1:])
    zero = jnp.zeros((rows, hd), BF16)

    def clear(b, carry):
        dk_ref[b] = zero
        dv_ref[b] = zero
        return carry

    start, stop = block_bounds(scal, rows)
    lax.fori_loop(0, start, clear, 0)
    lax.fori_loop(stop, dk_ref.shape[0], clear, 0)

    def run(b, masked):
        a = mine_ref[b, 0:rows, :]
        o = other_ref[b, 0:rows, :]
        kb = jnp.where(scal[3] == 0, a, o)
        vb = jnp.where(scal[3] == 0, o, a)
        kt = kb.astype(F32).T.astype(BF16)
        dk = jnp.zeros((rows, hd), F32)
        dv = jnp.zeros((rows, hd), F32)
        for h in range(heads):
            cols = slice(h * hd, (h + 1) * hd)
            qh = q_ref[:, cols]
            dh = d_ref[:, cols]
            p = probs_t(scal, kb, qh, lo_ref[...], b, rows, factor, log_ref[h, 0:1, :], masked)
            dp = mm(vb, dh, 1, 1)
            ds = (p * (dp - delta[h, 0:1, :])).astype(BF16)
            dv += mm(p.astype(BF16), dh, 1, 0)
            dk += mm(ds, qh, 1, 0)
            acc[h] += mm(kt, ds, 1, 0)
        dk_ref[b] = (dk * scale).astype(BF16)
        dv_ref[b] = dv.astype(BF16)

    for_blocks(scal, rows, run)
    for h in range(heads):
        dq_ref[:, h * hd : (h + 1) * hd] = (acc[h] * scale).T


VMEM = pl.BlockSpec(memory_space=pltpu.VMEM)
SMEM = pl.BlockSpec(memory_space=pltpu.SMEM)
LIMIT = 56 * 1024 * 1024


def attend(scal, q, mine, other, lo):
    rows, width = q.shape
    hd = mine.shape[2]
    heads = width // hd
    blocks = mine.shape[0]
    work = rows * width * rows * blocks
    return pl.pallas_call(
        attend_kernel,
        in_specs=[SMEM, VMEM, VMEM, VMEM, VMEM],
        out_specs=[VMEM, VMEM],
        out_shape=[
            jax.ShapeDtypeStruct((rows, width), BF16),
            jax.ShapeDtypeStruct((heads, 8, rows), F32),
        ],
        scratch_shapes=[pltpu.VMEM((heads, hd, rows), F32), pltpu.VMEM((heads, 8, rows), F32)],
        compiler_params=pltpu.CompilerParams(vmem_limit_bytes=LIMIT),
        cost_estimate=pl.CostEstimate(
            flops=4 * work, bytes_accessed=4 * mine.size, transcendentals=work // hd
        ),
        name="attend",
    )(scal, q, mine, other, lo)


def attend_back(scal, q, mine, other, lo, att, logs, d_att):
    rows, width = q.shape
    hd = mine.shape[2]
    heads = width // hd
    blocks = mine.shape[0]
    work = rows * width * rows * blocks
    grads = jax.ShapeDtypeStruct((blocks, rows, hd), BF16)
    return pl.pallas_call(
        attend_back_kernel,
        in_specs=[SMEM] + [VMEM] * 7,
        out_specs=[VMEM, VMEM, VMEM],
        out_shape=[jax.ShapeDtypeStruct((rows, width), F32), grads, grads],
        scratch_shapes=[pltpu.VMEM((heads, hd, rows), F32), pltpu.VMEM((heads, 8, rows), F32)],
        compiler_params=pltpu.CompilerParams(vmem_limit_bytes=LIMIT),
        cost_estimate=pl.CostEstimate(
            flops=10 * work, bytes_accessed=8 * mine.size, transcendentals=work // hd
        ),
        name="attend_back",
    )(scal, q, mine, other, lo, att, logs, d_att)


def per_device(
    layer_input,
    segment_ids,
    positions,
    attn_gain,
    q_weight,
    q_bias,
    kv_weight,
    kv_bias,
    o_weight,
    mlp_gain,
    gate_weight,
    up_weight,
    down_weight,
    cotangent,
):
    rows, width = layer_input.shape
    heads, hd = q_bias.shape
    ff = gate_weight.shape[1]
    n = lax.axis_size("ctx")
    ntp = lax.axis_size("tp")
    ctx = lax.axis_index("ctx")
    tp = lax.axis_index("tp")
    core = tp % 2
    y = tp // 2
    quarter = rows // ntp
    unit = ff // n

    o_full = lax.all_gather(o_weight, "tp", axis=0, tiled=True)
    q_full = lax.all_gather(q_weight.T, "tp", axis=0, tiled=True)
    cot_all = lax.all_gather(
        lax.dynamic_slice_in_dim(cotangent, tp * quarter, quarter, 0), ("ctx", "tp"), axis=0, tiled=True
    )
    gate_s = lax.dynamic_slice_in_dim(gate_weight, ctx * unit, unit, 1)
    up_s = lax.dynamic_slice_in_dim(up_weight, ctx * unit, unit, 1)
    down_s = lax.dynamic_slice_in_dim(down_weight, ctx * unit, unit, 0)

    inputs = layer_input.astype(F32)
    gain_one = attn_gain.astype(F32)
    factor_one = lax.rsqrt(jnp.mean(inputs * inputs, axis=-1, keepdims=True) + RMS_EPS)
    normed = (inputs * factor_one * gain_one).astype(BF16)
    cosine, sine = rope_tables(positions, hd)
    query = mm(normed, q_weight, 1, 0) + q_bias.astype(F32).reshape(-1)
    query_rot = rotate(query.reshape(rows, heads, hd), cosine[:, None], sine[:, None])
    query_rot = query_rot.astype(BF16).reshape(rows, heads * hd)
    column = (2 * core + y) * hd
    kv_cols = lax.dynamic_slice_in_dim(kv_weight, column, hd, 1)
    kv_own_bias = lax.dynamic_slice_in_dim(kv_bias, column, hd, 0).astype(F32)
    kv_own = mm(normed, kv_cols, 1, 0) + kv_own_bias
    kv_own = jnp.where(core == 0, rotate(kv_own, cosine, sine), kv_own).astype(BF16)

    ids = segment_ids.astype(BF16).reshape(rows // hd, hd)
    ids = jnp.pad(ids, ((0, EXTRA - rows // hd), (0, 0)))
    packed = jnp.concatenate([kv_own, ids], axis=0)
    mine = lax.all_to_all(
        jnp.broadcast_to(packed[None], (n,) + packed.shape), "ctx", split_axis=0, concat_axis=0, tiled=True
    )
    other = swap_core(mine)
    all_ids = mine[:, rows : rows + rows // hd, :].astype(F32)
    starts = [jnp.sum((all_ids < k).astype(F32)).astype(jnp.int32) for k in (1, 2, 3)]
    lo = jnp.where(
        segment_ids == 0,
        0,
        jnp.where(segment_ids == 1, starts[0], jnp.where(segment_ids == 2, starts[1], starts[2])),
    )
    scal = jnp.stack([ctx, lo[0], lo[-1], core]).astype(jnp.int32)
    lo = lo.reshape(1, rows)

    attended, logs = attend(scal, query_rot, mine, other, lo)
    attended_all = jnp.concatenate(gather_tp(attended, core, y), axis=1)
    hidden_in = inputs + mm(attended_all, o_full, 1, 0)

    gain_two = mlp_gain.astype(F32)
    factor_two = lax.rsqrt(jnp.mean(hidden_in * hidden_in, axis=-1, keepdims=True) + RMS_EPS)
    normed_two = (hidden_in * factor_two * gain_two).astype(BF16)
    normed_all = lax.all_gather(
        lax.dynamic_slice_in_dim(normed_two, tp * quarter, quarter, 0), ("ctx", "tp"), axis=0, tiled=True
    )

    gate = mm(normed_two, gate_weight, 1, 0)
    up = mm(normed_two, up_weight, 1, 0)
    d_hidden = mm(cotangent, down_weight, 1, 1)
    sig = jax.nn.sigmoid(gate)
    hidden = (gate * sig * up).astype(BF16)
    d_gate = (d_hidden * up * sig * (1.0 + gate * (1.0 - sig))).astype(BF16)
    d_up = (d_hidden * gate * sig).astype(BF16)
    d_normed_two = mm(d_gate, gate_weight, 1, 1) + mm(d_up, up_weight, 1, 1)
    d_normed_two = sum_tp(d_normed_two, core).astype(F32)
    mlp_part = mm(hidden, down_weight, 1, 0).astype(BF16)
    output = (hidden_in + lax.psum(mlp_part, "tp").astype(F32)).astype(BF16)

    w_two = hidden_in * factor_two
    part_mlp_gain = jnp.sum(d_normed_two * w_two, axis=0)
    dg_two = d_normed_two * gain_two
    d_hidden_in = cotangent.astype(F32) + factor_two * (
        dg_two - w_two * jnp.mean(dg_two * w_two, axis=-1, keepdims=True)
    )
    d_attn = d_hidden_in.astype(BF16)
    d_attended = mm(d_attn, o_weight, 1, 1).astype(BF16)

    d_query_rot, dk_all, dv_all = attend_back(scal, query_rot, mine, other, lo, attended, logs, d_attended)
    keep = jnp.where(core == 0, dk_all, dv_all)
    give = jnp.where(core == 0, dv_all, dk_all)
    d_kv = (keep.astype(F32) + swap_core(give).astype(F32)).astype(BF16)
    d_kv = sum_scatter(d_kv)
    d_kv = jnp.where(core == 0, rotate(d_kv, cosine, -sine), d_kv).astype(BF16)
    d_query = rotate(d_query_rot.reshape(rows, heads, hd), cosine[:, None], -sine[:, None])
    d_query = d_query.astype(BF16).reshape(rows, heads * hd)
    d_query_all = jnp.concatenate(gather_tp(d_query, core, y), axis=1)
    k0, v0, k1, v1 = gather_tp(d_kv, core, y)
    d_kv_all = jnp.concatenate([k0, k1, v0, v1], axis=1)
    d_normed = mm(d_query_all, q_full, 1, 0) + mm(d_kv_all, kv_weight, 1, 1)
    w_one = inputs * factor_one
    part_attn_gain = jnp.sum(d_normed * w_one, axis=0)
    dg_one = d_normed * gain_one
    dx = d_hidden_in + factor_one * (dg_one - w_one * jnp.mean(dg_one * w_one, axis=-1, keepdims=True))

    gate_t = mm(gate_s, normed_all, 0, 1)
    up_t = mm(up_s, normed_all, 0, 1)
    d_hidden_t = mm(down_s, cot_all, 1, 1)
    sig_t = jax.nn.sigmoid(gate_t)
    hidden_t = (gate_t * sig_t * up_t).astype(BF16)
    d_gate_t = (d_hidden_t * up_t * sig_t * (1.0 + gate_t * (1.0 - sig_t))).astype(BF16)
    d_up_t = (d_hidden_t * gate_t * sig_t).astype(BF16)
    part = width // n
    ff_grads = jnp.concatenate(
        [mm(d_gate_t, normed_all, 1, 0), mm(d_up_t, normed_all, 1, 0), mm(hidden_t, cot_all, 1, 0)], axis=0
    ).astype(BF16)
    ff_grads = ff_grads.reshape(3 * unit, n, part).transpose(1, 0, 2)
    ff_grads = lax.all_to_all(ff_grads, "ctx", split_axis=0, concat_axis=0, tiled=True)
    ff_grads = ff_grads.reshape(n, 3, unit, part).astype(F32)
    g_gate = ff_grads[:, 0].reshape(ff, part).T
    g_up = ff_grads[:, 1].reshape(ff, part).T
    g_down = ff_grads[:, 2].reshape(ff, part)

    g_o = mm(d_attn, attended, 0, 0).astype(BF16)
    g_o = sum_scatter(g_o.reshape(n, part, heads * hd)).T
    g_q = mm(normed, d_query, 0, 0).astype(BF16)
    g_q = sum_scatter(g_q.reshape(n, part, heads * hd))

    small = width // (n * ntp)
    g_kv = mm(normed, d_kv, 0, 0).astype(BF16).reshape(n * ntp, small, hd)
    bias_row = jnp.sum(d_kv.astype(F32), axis=0).astype(BF16)
    bias_rows = jnp.broadcast_to(bias_row[None, None], (n * ntp, EXTRA, hd))
    g_kv = lax.all_to_all(
        jnp.concatenate([g_kv, bias_rows], axis=1), ("ctx", "tp"), split_axis=0, concat_axis=0, tiled=True
    )
    g_kv = jnp.sum(g_kv.reshape(n, ntp, small + EXTRA, hd).astype(F32), axis=0)
    g_kv = jnp.concatenate([g_kv[0], g_kv[2], g_kv[1], g_kv[3]], axis=1)
    bias_size = kv_bias.shape[0] // (n * ntp)
    g_kv_bias = lax.dynamic_slice_in_dim(g_kv[small], (ctx * ntp + tp) * bias_size, bias_size, 0)
    g_kv = g_kv[:small]

    bias_cols = hd // n
    part_q_bias = jnp.sum(d_query.astype(F32), axis=0).reshape(heads, n, bias_cols).transpose(1, 0, 2)
    vectors = jnp.concatenate(
        [part_mlp_gain.reshape(n, part), part_attn_gain.reshape(n, part), part_q_bias.reshape(n, -1)], axis=1
    )
    vectors = sum_scatter(vectors)
    g_mlp_gain = vectors[:part]
    g_attn_gain = vectors[part : 2 * part]
    g_q_bias = vectors[2 * part :].reshape(heads, bias_cols)

    return (
        output,
        dx,
        g_attn_gain,
        g_q,
        g_q_bias,
        g_kv,
        g_kv_bias,
        g_o,
        g_mlp_gain,
        g_gate,
        g_up,
        g_down,
    )


def solution(mesh):
    return jax.shard_map(
        per_device,
        mesh=mesh,
        in_specs=(
            P("ctx", None),
            P("ctx"),
            P("ctx"),
            P(),
            P(None, "tp"),
            P("tp", None),
            P(),
            P(),
            P("tp", None),
            P(),
            P(None, "tp"),
            P(None, "tp"),
            P("tp", None),
            P("ctx", None),
        ),
        out_specs=(
            P("ctx", None),
            P("ctx", None),
            P("ctx"),
            P("ctx", "tp"),
            P("tp", "ctx"),
            P(("ctx", "tp"), None),
            P(("ctx", "tp")),
            P("tp", "ctx"),
            P("ctx"),
            P("ctx", "tp"),
            P("ctx", "tp"),
            P("tp", "ctx"),
        ),
        check_vma=False,
    )
```

time: 1240 us -> 618 us (0.50)
  waiting for transfers between devices: 930 us -> 288 us
  blocking collectives: 90.3 us -> 0 us
  starting transfers between devices: 1.64 us -> 71.8 us
  matrix products: 111 us -> 128 us
    reduce_scatter x7 -> x0, waiting for transfers between devices: 682 us -> none  [the longest x1 130 us: per_device(): lax.psum_scatter(g_up.astype(jnp.bfloat16), 'ctx', scatter_dimension=0, t...]
    psum x3 -> x1, waiting for transfers between devices: 185 us -> 0.01 us  [per_device(): output = (hidden_in + lax.psum(mlp_part, 'tp').astype(F32)).astype(BF16)]
    all_to_all x0 -> x7, waiting for transfers between devices: none -> 101 us  [the longest x1 50.6 us: per_device(): lax.all_to_all(ff_grads, 'ctx', split_axis=0, concat_axis=0, tiled=True)]
    all_gather x2 -> x4, waiting for transfers between devices: 45.2 us -> 135 us  [the longest x1 86.3 us: per_device(): lax.all_gather(lax.dynamic_slice_in_dim(normed_two, tp * quarter, quarter...]
    all_to_all x0 -> x7, starting transfers between devices: none -> 65.8 us  [the longest x4 46.2 us: sum_scatter(): got = lax.all_to_all(parts, 'ctx', split_axis=0, concat_axis=0, tiled=True)]
    unnamed x2 -> x0, blocking collectives: 62.4 us -> none
    ppermute x0 -> x14, waiting for transfers between devices: none -> 50.7 us  [the longest x4 42.5 us: swap_y(): return lax.ppermute(x, 'tp', [(0, 2), (2, 0), (1, 3), (3, 1)])]
    all_gather x1 -> x0, blocking collectives: 27.9 us -> none  [per_device(): lax.all_gather(segment_ids, 'ctx', axis=0, tiled=True)]
  transfers between devices with their start and end apart: 13 -> 26, of which waited for: 13 -> 14; matrix products, arithmetic and copies ran while one was open for 7% -> 29% of each run, Pallas kernels for 0% -> 2%
where the time goes in v1:
time: 618 us; the launch traced here: 612 us
  waiting for transfers between devices  288 us (47%)
  matrix products  128 us (21%)
  starting transfers between devices  71.8 us (12%)
  other arithmetic  48.9 us (8%)
  local copies, waits for them, and re-layouts  47 us (8%)
  between operations  17 us (3%)
  Pallas kernels  11.3 us (2%)
    dot_general x21, matrix products, mm(): lax.dot_general(a, b, (((ca,), (cb,)), ((), ())), preferred_element_type=...  128 us
    all_gather x1, waiting for transfers between devices, per_device(): lax.all_gather(lax.dynamic_slice_in_dim(normed_two, tp * quarter, quarter...  86.3 us
    all_to_all x1, waiting for transfers between devices, per_device(): lax.all_to_all(ff_grads, 'ctx', split_axis=0, concat_axis=0, tiled=True)  50.6 us
    all_gather x1, waiting for transfers between devices, per_device(): lax.all_gather(lax.dynamic_slice_in_dim(cotangent, tp * quarter, quarter,...  48.7 us
    all_to_all x4, starting transfers between devices, sum_scatter(): got = lax.all_to_all(parts, 'ctx', split_axis=0, concat_axis=0, tiled=True)  46.2 us
    ppermute x4, waiting for transfers between devices, swap_y(): return lax.ppermute(x, 'tp', [(0, 2), (2, 0), (1, 3), (3, 1)])  42.5 us
    all_to_all x4, waiting for transfers between devices, sum_scatter(): got = lax.all_to_all(parts, 'ctx', split_axis=0, concat_axis=0, tiled=True)  27 us
    all_to_all x1, waiting for transfers between devices, per_device(): lax.all_to_all(jnp.broadcast_to(packed[None], (n,) + packed.shape), 'ctx'...  23.4 us
  transfers between devices with their start and end apart: 26, of which 14 were waited for; matrix products, arithmetic and copies ran while one was open for 29% of the time, Pallas kernels for 2%

profile of v1, /device:TPU:0, one launch (start us, length us, event | category | flops | bytes accessed | tf_op | source)
XLA Modules:
  0.0 612.0 jit_solution(15306473791185332024)
XLA Ops:
  16.8 7.3 %all-to-all-start = ((bf16[8,528,128]{2,1,0:T(8,128)(2,1)}), bf16[8,528,128]{2,1,0:T(8,128)(2,1)}, u32[]{:S(2)}, u32[]{:S(2)}) async-start(bf16[8,528,128]{2,1,0:T(8,128)(2,1)} %broadcast_in_dim.17), calls=%async_computation | async-start | bytes 2162688 | tf_op jit(solution)/shard_map/all_to_all | solution.py:287
  27.3 23.4 %all-to-all-done.mine_ref = bf16[8,528,128]{2,1,0:T(8,128)(2,1)} async-done(((bf16[8,528,128]{2,1,0:T(8,128)(2,1)}), bf16[8,528,128]{2,1,0:T(8,128)(2,1)}, u32[]{:S(2)}, u32[]{:S(2)}) %all-to-all-start) | async-done | bytes 1081376 | tf_op jit(solution)/shard_map/all_to_all | solution.py:287
  66.1 10.0 %collective-permute-done.2 = bf16[512,384]{1,0:T(8,128)(2,1)S(1)} collective-permute-done((bf16[512,384]{1,0:T(8,128)(2,1)}, bf16[512,384]{1,0:T(8,128)(2,1)S(1)}, u32[]{:S(2)}, u32[]{:S(2)}) %collective-permute-start.2) | collective-permute-done | bytes 393248 | tf_op jit(solution)/shard_map/ppermute | solution.py:40
  80.5 5.7 multiply_reduce_fusion
  105.8 6.2 %fusion.94 = f32[512,2240]{0,1:T(8,128)S(1)} fusion(bf16[512,1536]{1,0:T(8,128)(2,1)S(1)} %copy-done.10, bf16[2240,1536]{1,0:T(8,128)(2,1)} %param.26), kind=kOutput, calls=%fused_computation.195 | convolution fusion | flops 3523215360 | bytes 13041664 | tf_op jit(solution)/shard_map/dot_general | solution.py:19
  112.0 8.9 %fusion.19 = f32[512,1536]{1,0:T(8,128)S(1)} fusion(bf16[1536,2240]{0,1:T(8,128)(2,1)} %param.24, f32[512,2240]{0,1:T(8,128)} %copy-done.29, f32[512,2240]{0,1:T(8,128)S(1)} %fusion.94, f32[512,2240]{0,1:T(8,128)} %copy-done.30), kind=kOutput, calls=%fused_computation.47 | convolution fusion | flops 3534684160 | bytes 23789568 | tf_op jit(solution)/shard_map/dot_general | solution.py:19
  132.3 27.6 %collective-permute-done.5 = bf16[256,1536]{1,0:T(8,128)(2,1)S(1)} collective-permute-done((bf16[256,1536]{1,0:T(8,128)(2,1)S(1)}, bf16[256,1536]{1,0:T(8,128)(2,1)S(1)}, u32[]{:S(2)}, u32[]{:S(2)}) %collective-permute-start.5) | collective-permute-done | bytes 786464 | tf_op jit(solution)/shard_map/ppermute | solution.py:40
  164.1 5.4 fusion.8
  172.8 6.9 %attend_back.1 = (f32[512,384]{1,0:T(8,128)}, bf16[8,512,128]{2,1,0:T(8,128)(2,1)}, bf16[8,512,128]{2,1,0:T(8,128)(2,1)}) custom-call(s32[4]{0:T(128)} %pad_add_fusion.scal, bf16[512,384]{1,0:T(8,128)(2,1)} %copy.63.q_ref, bf16[8,528,128]{2,1,0:T(8,128)(2,1)} %all-to-all-done.mine_ref, bf16[8,528,128]{2,1,0:T(8,128)(2,1)} %collective-permute-done.other_ref, ...), custom_call_target="tpu_custom_call" | custom-call | flops 8053063680 | bytes 4325376 | tf_op jit(solution)/shard_map/attend_back/pallas_call | solution.py:219
  185.3 34.1 %all-to-all-start.1 = ((bf16[8,512,128]{2,1,0:T(8,128)(2,1)}), bf16[8,512,128]{2,1,0:T(8,128)(2,1)}, u32[]{:S(2)}, u32[]{:S(2)}) async-start(bf16[8,512,128]{2,1,0:T(8,128)(2,1)} %add_convert_fusion.1), calls=%async_computation.1 | async-start | bytes 2097152 | tf_op jit(solution)/shard_map/all_to_all | solution.py:68
  235.9 18.9 %all-to-all-done.1 = bf16[8,512,128]{2,1,0:T(8,128)(2,1)} async-done(((bf16[8,512,128]{2,1,0:T(8,128)(2,1)}), bf16[8,512,128]{2,1,0:T(8,128)(2,1)}, u32[]{:S(2)}, u32[]{:S(2)}) %all-to-all-start.1) | async-done | bytes 1048608 | tf_op jit(solution)/shard_map/all_to_all | solution.py:68
  273.4 8.2 %fusion.15 = (f32[1536]{0:T(1024)S(1)}, f32[512]{0:T(512)S(1)}, f32[512,1536]{1,0:T(8,128)}) fusion(bf16[512,1536]{1,0:T(8,128)(2,1)S(1)} %copy-done.6, f32[512]{0:T(512)S(1)} %copy-done.21, f32[1536]{0:T(1024)S(1)} %copy-done.19, f32[512,1536]{1,0:T(8,128)} %fusion.42, bf16[1536,1536]{0,1:T(8,128)(2,1)} %all-gather.7.cloned.1.call-done, ...), kind=kOutput, calls=%fused_computation.30 | convolution fusion | flops 2428499968 | bytes 14172160 | tf_op jit(solution)/shard_map/dot_general | solution.py:19
  282.3 48.7 %all-gather.9.cloned.1.call-done = bf16[4096,1536]{1,0:T(8,128)(2,1)} async-done(((bf16[128,1536]{1,0:T(8,128)(2,1)}), bf16[4096,1536]{1,0:T(8,128)(2,1)}) %all-gather.9.cloned.1.call-update) | async-done | bytes 12582928 | tf_op jit(solution)/shard_map/all_gather | solution.py:263
  331.0 10.8 %fusion.38 = f32[280,4096]{1,0:T(8,128)} fusion(bf16[4096,1536]{1,0:T(8,128)(2,1)} %all-gather.9.cloned.1.call-done, bf16[2240,1536]{1,0:T(8,128)(2,1)} %param.26, s32[]{:T(128)S(6)} %select_n.232), kind=kOutput, calls=%fused_computation.77 | convolution fusion | flops 3523215360 | bytes 18030596 | tf_op jit(solution)/shard_map/dot_general | solution.py:19
  341.9 86.3 %all-gather.11.cloned.1.call-done = bf16[4096,1536]{1,0:T(8,128)(2,1)} async-done(((bf16[128,1536]{1,0:T(8,128)(2,1)}), bf16[4096,1536]{1,0:T(8,128)(2,1)}) %all-gather.11.cloned.1.call-update) | async-done | bytes 12582928 | tf_op jit(solution)/shard_map/all_gather | solution.py:308
  428.1 10.7 %fusion.36 = f32[280,4096]{1,0:T(8,128)} fusion(bf16[4096,1536]{1,0:T(8,128)(2,1)} %all-gather.11.cloned.1.call-done, bf16[1536,2240]{0,1:T(8,128)(2,1)} %param.25, s32[]{:T(128)S(6)} %select_n.232), kind=kOutput, calls=%fused_computation.75 | convolution fusion | flops 3523215360 | bytes 18030596 | tf_op jit(solution)/shard_map/dot_general | solution.py:19
  442.8 7.1 %fusion.34 = f32[280,4096]{1,0:T(8,128)S(1)} fusion(bf16[4096,1536]{1,0:T(8,128)(2,1)} %all-gather.11.cloned.1.call-done, bf16[1536,2240]{0,1:T(8,128)(2,1)} %param.24, s32[]{:T(128)S(6)} %select_n.232), kind=kOutput, calls=%fused_computation.73 | convolution fusion | flops 3523215360 | bytes 18030596 | tf_op jit(solution)/shard_map/dot_general | solution.py:19
  452.0 11.6 %convolution_convert_fusion.5 = bf16[280,1536]{1,0:T(8,128)(2,1)} fusion(bf16[4096,1536]{1,0:T(8,128)(2,1)} %all-gather.11.cloned.1.call-done, f32[280,4096]{1,0:T(8,128)S(1)} %fusion.34, f32[280,4096]{1,0:T(8,128)} %fusion.38, f32[280,4096]{1,0:T(8,128)S(1)} %copy-done.28), kind=kOutput, calls=%fused_computation.41 | convolution fusion | flops 3535114240 | bytes 27205632 | tf_op jit(solution)/shard_map/dot_general | solution.py:19
  463.7 8.1 %all-to-all-done.5 = bf16[8,192,384]{2,1,0:T(8,128)(2,1)S(1)} async-done(((bf16[8,192,384]{2,1,0:T(8,128)(2,1)}), bf16[8,192,384]{2,1,0:T(8,128)(2,1)S(1)}, u32[]{:S(2)}, u32[]{:S(2)}) %all-to-all-start.5) | async-done | bytes 1179680 | tf_op jit(solution)/shard_map/all_to_all | solution.py:68
  475.5 12.1 %convolution_convert_fusion.3 = bf16[280,1536]{1,0:T(8,128)(2,1)} fusion(bf16[4096,1536]{1,0:T(8,128)(2,1)} %all-gather.9.cloned.1.call-done, f32[280,4096]{1,0:T(8,128)} %fusion.36, f32[280,4096]{1,0:T(8,128)} %copy-done.27), kind=kOutput, calls=%fused_computation.39 | convolution fusion | flops 3530526720 | bytes 22618112 | tf_op jit(solution)/shard_map/dot_general | solution.py:19
  487.5 6.4 %all-to-all-start.4 = ((bf16[32,64,128]{2,1,0:T(8,128)(2,1)}), bf16[32,64,128]{2,1,0:T(8,128)(2,1)}, u32[]{:S(2)}, u32[]{:S(2)}) async-start(bf16[32,64,128]{2,1,0:T(8,128)(2,1)} %pad_maximum_fusion.1), calls=%async_computation.4 | async-start | bytes 1048576 | tf_op jit(solution)/shard_map/all_to_all | solution.py:377
  494.0 11.9 %convolution_convert_fusion.4 = bf16[280,1536]{1,0:T(8,128)(2,1)} fusion(bf16[4096,1536]{1,0:T(8,128)(2,1)} %all-gather.11.cloned.1.call-done, f32[280,4096]{1,0:T(8,128)} %fusion.38, f32[280,4096]{1,0:T(8,128)} %copy-done.27), kind=kOutput, calls=%fused_computation.40 | convolution fusion | flops 3530526720 | bytes 22618112 | tf_op jit(solution)/shard_map/dot_general | solution.py:19
  517.7 5.9 all-to-all-start.6
  535.7 50.6 %all-to-all-done.6 = bf16[8,840,192]{1,2,0:T(8,128)(2,1)} async-done(((bf16[8,840,192]{1,2,0:T(8,128)(2,1)}), bf16[8,840,192]{1,2,0:T(8,128)(2,1)}, u32[]{:S(2)}, u32[]{:S(2)}) %all-to-all-start.6) | async-done | bytes 2580512 | tf_op jit(solution)/shard_map/all_to_all | solution.py:362
  (221 shorter events, 162.2 us)
Async XLA Ops:
  7.2 73.3 %all-gather.5.cloned.1.call-start = ((), (), s32[]{:S(2)}) async-start(), calls=%async_computation.7 | async-start | bytes 5898240 | tf_op jit(solution)/shard_map/all_gather | solution.py:261
  16.8 33.8 %all-to-all-start = ((bf16[8,528,128]{2,1,0:T(8,128)(2,1)}), bf16[8,528,128]{2,1,0:T(8,128)(2,1)}, u32[]{:S(2)}, u32[]{:S(2)}) async-start(bf16[8,528,128]{2,1,0:T(8,128)(2,1)} %broadcast_in_dim.17), calls=%async_computation | async-start | bytes 2162688 | tf_op jit(solution)/shard_map/all_to_all | solution.py:287
  24.1 140.0 %all-reduce.3.cloned.1.call-start = ((), (), s32[]{:S(2)}) async-start(), calls=%async_computation.8 | async-start | bytes 3145728 | tf_op jit(solution)/shard_map/psum | solution.py:322
  50.7 9.3 %collective-permute-start = (bf16[8,528,128]{2,1,0:T(8,128)(2,1)}, bf16[8,528,128]{2,1,0:T(8,128)(2,1)}, u32[]{:S(2)}, u32[]{:S(2)}) collective-permute-start(bf16[8,528,128]{2,1,0:T(8,128)(2,1)} %all-to-all-done.mine_ref), channel_id=1, source_target_pairs={{0,1},{1,0},{2,3},{3,2},{4,5},{5,4},{6,7},{7,6},{8,9},{9,8},{10,11... | collective-permute-start | bytes 3244040 | tf_op jit(solution)/shard_map/ppermute | solution.py:36
  64.4 11.7 %collective-permute-start.2 = (bf16[512,384]{1,0:T(8,128)(2,1)}, bf16[512,384]{1,0:T(8,128)(2,1)S(1)}, u32[]{:S(2)}, u32[]{:S(2)}) collective-permute-start(bf16[512,384]{1,0:T(8,128)(2,1)} %get-tuple-element.17.att_ref), channel_id=1, source_target_pairs={{0,2},{2,0},{1,3},{3,1},{4,6},{6,4},{5,7},{7,5},{8,10},{10,8},{9,1... | collective-permute-start | bytes 1179656 | tf_op jit(solution)/shard_map/ppermute | solution.py:40
  65.9 10.9 %collective-permute-start.1 = (bf16[512,384]{1,0:T(8,128)(2,1)}, bf16[512,384]{1,0:T(8,128)(2,1)}, u32[]{:S(2)}, u32[]{:S(2)}) collective-permute-start(bf16[512,384]{1,0:T(8,128)(2,1)} %get-tuple-element.17.att_ref), channel_id=1, source_target_pairs={{0,1},{1,0},{2,3},{3,2},{4,5},{5,4},{6,7},{7,6},{8,9},{9,8},{10,11... | collective-permute-start | bytes 1179656 | tf_op jit(solution)/shard_map/ppermute | solution.py:36
  101.9 171.5 %all-gather.7.cloned.1.call-start = ((), (), s32[]{:S(2)}) async-start(), calls=%async_computation.9 | async-start | bytes 5898240 | tf_op jit(solution)/shard_map/all_gather | solution.py:262
  102.6 228.4 %all-gather.9.cloned.1.call-start = ((), (), s32[]{:S(2)}) async-start(), calls=%async_computation.10 | async-start | bytes 12976128 | tf_op jit(solution)/shard_map/all_gather | solution.py:263
  103.5 324.7 %all-gather.11.cloned.1.call-start = ((), (), s32[]{:S(2)}) async-start(), calls=%async_computation.11 | async-start | bytes 12976128 | tf_op jit(solution)/shard_map/all_gather | solution.py:308
  126.7 2.4 collective-permute-start.4
  130.7 29.2 %collective-permute-start.5 = (bf16[256,1536]{1,0:T(8,128)(2,1)S(1)}, bf16[256,1536]{1,0:T(8,128)(2,1)S(1)}, u32[]{:S(2)}, u32[]{:S(2)}) collective-permute-start(bf16[256,1536]{1,0:T(8,128)(2,1)S(1)} %add_convert_fusion.3), channel_id=1, source_target_pairs={{0,2},{2,0},{1,3},{3,1},{4,6},{6,4},{5,7},{7,5},{8,10},{10,8},{9,1... | collective-permute-start | bytes 2359304 | tf_op jit(solution)/shard_map/ppermute | solution.py:40
  181.2 2.7 collective-permute-start.10
  185.3 69.5 %all-to-all-start.1 = ((bf16[8,512,128]{2,1,0:T(8,128)(2,1)}), bf16[8,512,128]{2,1,0:T(8,128)(2,1)}, u32[]{:S(2)}, u32[]{:S(2)}) async-start(bf16[8,512,128]{2,1,0:T(8,128)(2,1)} %add_convert_fusion.1), calls=%async_computation.1 | async-start | bytes 2097152 | tf_op jit(solution)/shard_map/all_to_all | solution.py:68
  224.1 40.5 %collective-permute-start.7 = (bf16[512,384]{1,0:T(8,128)(2,1)}, bf16[512,384]{1,0:T(8,128)(2,1)}, u32[]{:S(2)}, u32[]{:S(2)}) collective-permute-start(bf16[512,384]{1,0:T(8,128)(2,1)} %copy.67), channel_id=1, source_target_pairs={{0,1},{1,0},{2,3},{3,2},{4,5},{5,4},{6,7},{7,6},{8,9},{9,8},{10,11... | collective-permute-start | bytes 1179656 | tf_op jit(solution)/shard_map/ppermute | solution.py:36
  224.1 11.8 %collective-permute-start.8 = (bf16[512,384]{1,0:T(8,128)(2,1)}, bf16[512,384]{1,0:T(8,128)(2,1)}, u32[]{:S(2)}, u32[]{:S(2)}) collective-permute-start(bf16[512,384]{1,0:T(8,128)(2,1)} %copy.67), channel_id=1, source_target_pairs={{0,2},{2,0},{1,3},{3,1},{4,6},{6,4},{5,7},{7,5},{8,10},{10,8},{9,1... | collective-permute-start | bytes 1179656 | tf_op jit(solution)/shard_map/ppermute | solution.py:40
  235.9 28.6 %collective-permute-start.9 = (bf16[512,384]{1,0:T(8,128)(2,1)}, bf16[512,384]{1,0:T(8,128)(2,1)}, u32[]{:S(2)}, u32[]{:S(2)}) collective-permute-start(bf16[512,384]{1,0:T(8,128)(2,1)} %collective-permute-done.8), channel_id=1, source_target_pairs={{0,1},{1,0},{2,3},{3,2},{4,5},{5,4},{6,7},{7,6},{8,9},{9,8},{10,11... | collective-permute-start | bytes 1179656 | tf_op jit(solution)/shard_map/ppermute | solution.py:36
  254.8 184.0 %all-to-all-start.3 = ((bf16[8,192,384]{2,1,0:T(8,128)(2,1)}), bf16[8,192,384]{2,1,0:T(8,128)(2,1)}, u32[]{:S(2)}, u32[]{:S(2)}) async-start(bf16[8,192,384]{2,1,0:T(8,128)(2,1)} %bitcast.80), calls=%async_computation.3 | async-start | bytes 2359296 | tf_op jit(solution)/shard_map/all_to_all | solution.py:68
  263.2 5.0 collective-permute-start.12
  267.1 3.5 collective-permute-start.11
  268.2 2.4 collective-permute-start.13
  438.8 33.0 %all-to-all-start.5 = ((bf16[8,192,384]{2,1,0:T(8,128)(2,1)}), bf16[8,192,384]{2,1,0:T(8,128)(2,1)S(1)}, u32[]{:S(2)}, u32[]{:S(2)}) async-start(bf16[8,192,384]{2,1,0:T(8,128)(2,1)} %bitcast.69), calls=%async_computation.5 | async-start | bytes 2359296 | tf_op jit(solution)/shard_map/all_to_all | solution.py:68
  471.8 15.7 %all-to-all-start.2 = ((f32[8,1,432]{2,1,0:T(1,128)}), f32[8,1,432]{2,1,0:T(1,128)S(1)}, u32[]{:S(2)}, u32[]{:S(2)}) async-start(f32[8,1,432]{2,1,0:T(1,128)} %all_to_all.26), calls=%async_computation.2 | async-start | bytes 32768 | tf_op jit(solution)/shard_map/all_to_all | solution.py:68
  487.5 30.2 %all-to-all-start.4 = ((bf16[32,64,128]{2,1,0:T(8,128)(2,1)}), bf16[32,64,128]{2,1,0:T(8,128)(2,1)}, u32[]{:S(2)}, u32[]{:S(2)}) async-start(bf16[32,64,128]{2,1,0:T(8,128)(2,1)} %pad_maximum_fusion.1), calls=%async_computation.4 | async-start | bytes 1048576 | tf_op jit(solution)/shard_map/all_to_all | solution.py:377
  517.7 68.6 %all-to-all-start.6 = ((bf16[8,840,192]{1,2,0:T(8,128)(2,1)}), bf16[8,840,192]{1,2,0:T(8,128)(2,1)}, u32[]{:S(2)}, u32[]{:S(2)}) async-start(bf16[8,840,192]{1,2,0:T(8,128)(2,1)} %maximum_bitcast_fusion), calls=%async_computation.6 | async-start | bytes 5505024 | tf_op jit(solution)/shard_map/all_to_all | solution.py:362
  (43 other events, 479.5 us)
Sparse Core Ops, SparseCore 0:
  9.6 40.1 all-gather.4
  102.0 61.3 all-reduce.2
  165.0 40.8 all-gather.6
  208.6 122.3 all-gather.8
  333.8 94.3 all-gather.10

commit v2 on v1

v2 whole, which is shorter than its diff:
```python
import functools

import jax
import jax.numpy as jnp
from jax import lax
from jax.experimental import pallas as pl
from jax.experimental.pallas import tpu as pltpu
from jax.sharding import PartitionSpec as P

RMS_EPS = 1e-06
ROPE_BASE = 1000000.0
LOG2E = 1.4426950408889634
BF16 = jnp.bfloat16
F32 = jnp.float32
EXTRA = 16


def mm(a, b, ca, cb):
    return lax.dot_general(a, b, (((ca,), (cb,)), ((), ())), preferred_element_type=F32)


def rope_tables(positions, head_dim):
    half = head_dim // 2
    freqs = ROPE_BASE ** (-2.0 * jnp.arange(half, dtype=F32) / head_dim)
    angles = positions.astype(F32)[:, None] * freqs[None, :]
    return jnp.cos(angles), jnp.sin(angles)


def rotate(values, cosine, sine):
    half = cosine.shape[-1]
    first, second = values[..., :half], values[..., half:]
    return jnp.concatenate([first * cosine - second * sine, second * cosine + first * sine], axis=-1)


def swap(x, axis):
    return lax.ppermute(x, axis, [(0, 1), (1, 0)])


def gather_tp(x, core, y):
    far = swap(x, "y")
    mate = swap(x, "core")
    far_mate = swap(far, "core")
    a0, a1 = jnp.where(core == 0, x, mate), jnp.where(core == 0, mate, x)
    b0, b1 = jnp.where(core == 0, far, far_mate), jnp.where(core == 0, far_mate, far)
    return [
        jnp.where(y == 0, a0, b0),
        jnp.where(y == 0, a1, b1),
        jnp.where(y == 0, b0, a0),
        jnp.where(y == 0, b1, a1),
    ]


def sum_core(keep, give):
    return (keep + swap(give, "core").astype(F32)).astype(BF16)


def sum_y(half):
    return (half.astype(F32) + swap(half, "y").astype(F32)).astype(BF16)


def join_core(half, core):
    mate = swap(half, "core")
    return jnp.concatenate([jnp.where(core == 0, half, mate), jnp.where(core == 0, mate, half)], axis=0)


def split_core(part, core):
    rows = part.shape[0] // 2
    keep = lax.dynamic_slice_in_dim(part, core * rows, rows, 0)
    return keep, lax.dynamic_slice_in_dim(part, (1 - core) * rows, rows, 0).astype(BF16)


def sum_x(parts, x):
    keep = lax.dynamic_index_in_dim(parts, x, 0, keepdims=False)
    give = lax.dynamic_index_in_dim(parts, 1 - x, 0, keepdims=False)
    return (keep.astype(F32) + swap(give, "x").astype(F32)).astype(BF16)


def along_z(block, distance):
    nz = lax.axis_size("z")
    return lax.ppermute(block, "z", [(i, (i + distance) % nz) for i in range(nz)])


def column_tokens(block, tp):
    quarter = block.shape[0] // 4
    own = lax.dynamic_slice_in_dim(block, tp * quarter, quarter, 0)
    return lax.all_gather(own, ("z", "y", "core"), axis=0, tiled=True)


def column_start(block, tp):
    nz = lax.axis_size("z")
    quarter = block.shape[0] // 4
    own = lax.dynamic_slice_in_dim(block, tp * quarter, quarter, 0)
    return tuple(lax.ppermute(own, "z", [(i, (i + s) % nz) for i in range(nz)]) for s in range(1, nz))


def after(values, *done):
    return lax.optimization_barrier((values, done))[0]


def block_bounds(scal, rows):
    return lax.div(scal[1], rows), scal[0] + 1


def probs_t(scal, kb, qh, lo_row, b, rows, factor, shift, masked):
    s = mm(kb, qh, 1, 1) * factor
    if shift is not None:
        s = s - shift
    p = jnp.exp2(s)
    if masked:
        key = b * rows + lax.broadcasted_iota(jnp.int32, p.shape, 0)
        query = scal[0] * p.shape[1] + lax.broadcasted_iota(jnp.int32, p.shape, 1)
        p = jnp.where((key <= query) & (key >= lo_row), p, 0.0)
    return p


def for_blocks(scal, rows, run):
    start, stop = block_bounds(scal, rows)

    def body(b, carry):
        plain = (b < scal[0]) & (scal[2] <= b * rows)

        @pl.when(plain)
        def _():
            run(b, False)

        @pl.when(jnp.logical_not(plain))
        def _():
            run(b, True)

        return carry

    lax.fori_loop(start, stop, body, 0)


def key_value(scal, refs, b, rows):
    z = lax.div(b, 2)
    near = lax.rem(b, 2) == lax.rem(scal[0], 2)
    mine = jnp.where(near, refs[0][z, 0:rows, :], refs[1][z, 0:rows, :])
    other = jnp.where(near, refs[2][z, 0:rows, :], refs[3][z, 0:rows, :])
    return jnp.where(scal[3] == 0, mine, other), jnp.where(scal[3] == 0, other, mine)


def attend_kernel(scal, q_ref, r0, r1, r2, r3, lo_ref, att_ref, log_ref, acc, tot):
    refs = (r0, r1, r2, r3)
    rows, width = q_ref.shape
    hd = r0.shape[2]
    heads = width // hd
    factor = LOG2E * hd**-0.5
    acc[...] = jnp.zeros_like(acc)
    tot[...] = jnp.zeros_like(tot)

    def run(b, masked):
        kb, vb = key_value(scal, refs, b, rows)
        vt = vb.astype(F32).T.astype(BF16)
        for h in range(heads):
            p = probs_t(
                scal, kb, q_ref[:, h * hd : (h + 1) * hd], lo_ref[...], b, rows, factor, None, masked
            )
            tot[h] += jnp.sum(p.reshape(rows // 8, 8, p.shape[1]), axis=0)
            acc[h] += mm(vt, p.astype(BF16), 1, 0)

    for_blocks(scal, rows, run)
    for h in range(heads):
        total = jnp.sum(tot[h], axis=0, keepdims=True)
        att_ref[:, h * hd : (h + 1) * hd] = (acc[h] / total).T.astype(BF16)
        log_ref[h] = jnp.broadcast_to(jnp.log2(total), log_ref.shape[1:])


def attend_back_kernel(
    scal, q_ref, r0, r1, r2, r3, lo_ref, att_ref, log_ref, d_ref, dq_ref, keep_near, keep_far, give_near, give_far, acc, delta
):
    refs = (r0, r1, r2, r3)
    rows, width = q_ref.shape
    hd = r0.shape[2]
    heads = width // hd
    scale = hd**-0.5
    factor = LOG2E * scale
    acc[...] = jnp.zeros_like(acc)
    for h in range(heads):
        cols = slice(h * hd, (h + 1) * hd)
        both = d_ref[:, cols].astype(F32) * att_ref[:, cols].astype(F32)
        delta[h] = jnp.broadcast_to(jnp.sum(both.T, axis=0, keepdims=True), delta.shape[1:])
    zero = jnp.zeros((rows, hd), BF16)

    def put(b, keep, give):
        nz = keep_near.shape[0]
        z = lax.rem(lax.div(b, 2) - lax.div(scal[0], 2) + nz, nz)
        near = lax.rem(b, 2) == lax.rem(scal[0], 2)

        @pl.when(near)
        def _():
            keep_near[z] = keep
            give_near[z] = give

        @pl.when(jnp.logical_not(near))
        def _():
            keep_far[z] = keep
            give_far[z] = give

    def clear(b, carry):
        put(b, zero, zero)
        return carry

    start, stop = block_bounds(scal, rows)
    lax.fori_loop(0, start, clear, 0)
    lax.fori_loop(stop, 2 * keep_near.shape[0], clear, 0)

    def run(b, masked):
        kb, vb = key_value(scal, refs, b, rows)
        kt = kb.astype(F32).T.astype(BF16)
        dk = jnp.zeros((rows, hd), F32)
        dv = jnp.zeros((rows, hd), F32)
        for h in range(heads):
            cols = slice(h * hd, (h + 1) * hd)
            qh = q_ref[:, cols]
            dh = d_ref[:, cols]
            p = probs_t(scal, kb, qh, lo_ref[...], b, rows, factor, log_ref[h, 0:1, :], masked)
            dp = mm(vb, dh, 1, 1)
            ds = (p * (dp - delta[h, 0:1, :])).astype(BF16)
            dv += mm(p.astype(BF16), dh, 1, 0)
            dk += mm(ds, qh, 1, 0)
            acc[h] += mm(kt, ds, 1, 0)
        dk = (dk * scale).astype(BF16)
        dv = dv.astype(BF16)
        put(b, jnp.where(scal[3] == 0, dk, dv), jnp.where(scal[3] == 0, dv, dk))

    for_blocks(scal, rows, run)
    for h in range(heads):
        dq_ref[:, h * hd : (h + 1) * hd] = (acc[h] * scale).T


VMEM = pl.BlockSpec(memory_space=pltpu.VMEM)
SMEM = pl.BlockSpec(memory_space=pltpu.SMEM)
LIMIT = 56 * 1024 * 1024


def attend(scal, q, kv, lo):
    rows, width = q.shape
    hd = kv[0].shape[2]
    heads = width // hd
    blocks = 2 * kv[0].shape[0]
    work = rows * width * rows * blocks
    return pl.pallas_call(
        attend_kernel,
        in_specs=[SMEM] + [VMEM] * 6,
        out_specs=[VMEM, VMEM],
        out_shape=[
            jax.ShapeDtypeStruct((rows, width), BF16),
            jax.ShapeDtypeStruct((heads, 8, rows), F32),
        ],
        scratch_shapes=[pltpu.VMEM((heads, hd, rows), F32), pltpu.VMEM((heads, 8, rows), F32)],
        compiler_params=pltpu.CompilerParams(vmem_limit_bytes=LIMIT),
        cost_estimate=pl.CostEstimate(
            flops=4 * work, bytes_accessed=16 * kv[0].size, transcendentals=work // hd
        ),
        name="attend",
    )(scal, q, *kv, lo)


def attend_back(scal, q, kv, lo, att, logs, d_att):
    rows, width = q.shape
    hd = kv[0].shape[2]
    heads = width // hd
    blocks = 2 * kv[0].shape[0]
    work = rows * width * rows * blocks
    grads = jax.ShapeDtypeStruct(kv[0].shape[:1] + (rows, hd), BF16)
    return pl.pallas_call(
        attend_back_kernel,
        in_specs=[SMEM] + [VMEM] * 9,
        out_specs=[VMEM] * 5,
        out_shape=[jax.ShapeDtypeStruct((rows, width), F32)] + [grads] * 4,
        scratch_shapes=[pltpu.VMEM((heads, hd, rows), F32), pltpu.VMEM((heads, 8, rows), F32)],
        compiler_params=pltpu.CompilerParams(vmem_limit_bytes=LIMIT),
        cost_estimate=pl.CostEstimate(
            flops=10 * work, bytes_accessed=32 * kv[0].size, transcendentals=work // hd
        ),
        name="attend_back",
    )(scal, q, *kv, lo, att, logs, d_att)


CHUNK = 512


def column_fetch(scal, quarters, nz, quarter, rows, normed, nbuf, nsem, cots=None, cbuf=None, csem=None):
    z, core, y = scal[1], lax.rem(scal[2], 2), lax.div(scal[2], 2)
    per_chunk = CHUNK // quarter
    chunks = [(k, first) for k in range(quarters) for first in range(0, nz, per_chunk)]

    def fetch(c):
        k, first = chunks[c]
        slot = c % nbuf.shape[0]
        q = 2 * ((1 - y) if k % 2 else y) + ((1 - core) if k // 2 else core)
        for i in range(per_chunk):
            dist = first + i
            row = pl.multiple_of(lax.rem(z - dist + nz, nz) * rows + q * quarter, quarter)
            place = pl.ds(i * quarter, quarter)
            pltpu.make_async_copy(normed.at[pl.ds(row, quarter), :], nbuf.at[slot, place, :], nsem.at[slot]).start()
            if cots is None:
                continue
            if dist == 0:
                source = cots[0].at[pl.ds(pl.multiple_of(q * quarter, quarter), quarter), :]
            else:
                source = cots[k + 1].at[pl.ds((dist - 1) * quarter, quarter), :]
            pltpu.make_async_copy(source, cbuf.at[slot, place, :], csem.at[slot]).start()

    for c in range(min(nbuf.shape[0], len(chunks))):
        fetch(c)
    return fetch, len(chunks)


def column_put(scal, acc, keep, give):
    nz, part, _ = keep.shape
    flat = acc[...].T.astype(BF16)
    for i in range(2 * nz):
        value = flat[i * part : (i + 1) * part, :]
        dist = lax.rem(i // 2 - scal[1] + nz, nz)

        @pl.when(scal[0] == i % 2)
        def _(value=value, dist=dist):
            keep[dist] = value

        @pl.when(scal[0] != i % 2)
        def _(value=value, dist=dist):
            give[dist] = value


def column_first_kernel(quarters, scal, normed, *refs):
    cots = refs[: quarters + 1]
    gate_ref, up_ref, down_ref, kd, gd, d_gate_ref, d_up_ref = refs[quarters + 1 : quarters + 8]
    nbuf, cbuf, ad, nsem, csem = refs[quarters + 8 :]
    rows = cots[0].shape[0]
    fetch, count = column_fetch(
        scal, quarters, kd.shape[0], rows // quarters, rows, normed, nbuf, nsem, cots, cbuf, csem
    )
    slots = nbuf.shape[0]
    for c in range(count):
        slot = c % slots
        place = slice(c * CHUNK, (c + 1) * CHUNK)
        pltpu.make_async_copy(nbuf.at[slot], nbuf.at[slot], nsem.at[slot]).wait()
        pltpu.make_async_copy(cbuf.at[slot], cbuf.at[slot], csem.at[slot]).wait()
        gate = mm(gate_ref[...], nbuf[slot], 1, 1)
        up = mm(up_ref[...], nbuf[slot], 1, 1)
        d_hidden = mm(down_ref[...], cbuf[slot], 1, 1)
        sig = 1.0 / (1.0 + jnp.exp(-gate))
        silu = gate * sig
        hidden = (silu * up).astype(BF16)
        d_gate_ref[:, place] = (d_hidden * up * sig * (1.0 + gate * (1.0 - sig))).astype(BF16)
        d_up_ref[:, place] = (d_hidden * silu).astype(BF16)
        grad = mm(hidden, cbuf[slot], 1, 0)
        ad[...] = grad if c == 0 else ad[...] + grad
        if c + slots < count:
            fetch(c + slots)
    column_put(scal, ad, kd, gd)


def column_second_kernel(quarters, rows, scal, normed, d_gate_ref, d_up_ref, kg, gg, ku, gu, nbuf, ag, au, nsem):
    fetch, count = column_fetch(scal, quarters, kg.shape[0], rows // quarters, rows, normed, nbuf, nsem)
    slots = nbuf.shape[0]
    for c in range(count):
        slot = c % slots
        place = slice(c * CHUNK, (c + 1) * CHUNK)
        pltpu.make_async_copy(nbuf.at[slot], nbuf.at[slot], nsem.at[slot]).wait()
        for acc, left in ((ag, d_gate_ref), (au, d_up_ref)):
            grad = mm(left[:, place], nbuf[slot], 1, 0)
            acc[...] = grad if c == 0 else acc[...] + grad
        if c + slots < count:
            fetch(c + slots)
    column_put(scal, ag, kg, gg)
    column_put(scal, au, ku, gu)


ANYWHERE = pl.BlockSpec(memory_space=pl.ANY)


def column_first(scal, normed, cots, gate_s, up_s, down_s, n):
    unit, width = gate_s.shape
    quarters = len(cots) - 1
    tokens = normed.shape[0]
    slots = min(tokens // CHUNK, 4)
    out = jax.ShapeDtypeStruct((n // 2, width // n, unit), BF16)
    units = jax.ShapeDtypeStruct((unit, tokens), BF16)
    return pl.pallas_call(
        functools.partial(column_first_kernel, quarters),
        in_specs=[SMEM] + [ANYWHERE] * (quarters + 2) + [VMEM] * 3,
        out_specs=[VMEM] * 4,
        out_shape=[out] * 2 + [units] * 2,
        scratch_shapes=[pltpu.VMEM((slots, CHUNK, width), BF16)] * 2
        + [pltpu.VMEM((unit, width), F32)]
        + [pltpu.SemaphoreType.DMA((slots,))] * 2,
        compiler_params=pltpu.CompilerParams(vmem_limit_bytes=LIMIT),
        cost_estimate=pl.CostEstimate(
            flops=8 * tokens * width * unit,
            bytes_accessed=4 * tokens * width + 12 * width * unit,
            transcendentals=tokens * unit,
        ),
        name="column_first",
    )(scal, normed, *cots, gate_s, up_s, down_s)


def column_second(scal, normed, d_gate, d_up, rows, n):
    unit, tokens = d_gate.shape
    width = normed.shape[1]
    slots = min(tokens // CHUNK, 4)
    out = jax.ShapeDtypeStruct((n // 2, width // n, unit), BF16)
    return pl.pallas_call(
        functools.partial(column_second_kernel, 4, rows),
        in_specs=[SMEM, ANYWHERE, VMEM, VMEM],
        out_specs=[VMEM] * 4,
        out_shape=[out] * 4,
        scratch_shapes=[pltpu.VMEM((slots, CHUNK, width), BF16)]
        + [pltpu.VMEM((unit, width), F32)] * 2
        + [pltpu.SemaphoreType.DMA((slots,))],
        compiler_params=pltpu.CompilerParams(vmem_limit_bytes=LIMIT),
        cost_estimate=pl.CostEstimate(
            flops=4 * tokens * width * unit,
            bytes_accessed=2 * tokens * width + 4 * width * unit,
            transcendentals=0,
        ),
        name="column_second",
    )(scal, normed, d_gate, d_up)


def assemble_kernel(nz, scal, *refs):
    unit = refs[0].shape[1]
    groups, targets = (refs[:nz], refs[nz : 2 * nz], refs[2 * nz : 3 * nz]), refs[3 * nz :]

    def block(group, j):
        dist = lax.rem(scal[1] - j + nz, nz)
        value = group[0][...]
        for d in range(1, nz):
            value = jnp.where(dist == d, group[d][...], value)
        return value.astype(F32)

    for group, target in zip(groups[:2], targets[:2]):
        target[...] = jnp.concatenate([block(group, j) for j in range(nz)], axis=1)
    for j in range(nz):
        targets[2][j * unit : (j + 1) * unit, :] = block(groups[2], j).T


def assemble(scal, gate, up, down):
    nz = len(gate)
    part, unit = gate[0].shape
    ff = nz * unit
    return pl.pallas_call(
        functools.partial(assemble_kernel, nz),
        in_specs=[SMEM] + [VMEM] * (3 * nz),
        out_specs=[VMEM] * 3,
        out_shape=[jax.ShapeDtypeStruct(shape, F32) for shape in ((part, ff), (part, ff), (ff, part))],
        compiler_params=pltpu.CompilerParams(vmem_limit_bytes=LIMIT),
        cost_estimate=pl.CostEstimate(flops=0, bytes_accessed=18 * ff * part, transcendentals=0),
        name="assemble",
    )(scal, *gate, *up, *down)


def per_device(
    layer_input,
    segment_ids,
    positions,
    attn_gain,
    q_weight,
    q_bias,
    kv_weight,
    kv_bias,
    o_weight,
    mlp_gain,
    gate_weight,
    up_weight,
    down_weight,
    cotangent,
):
    rows, width = layer_input.shape
    heads, hd = q_bias.shape
    ff = gate_weight.shape[1]
    nz, x, y, core = lax.axis_size("z"), lax.axis_index("x"), lax.axis_index("y"), lax.axis_index("core")
    z = lax.axis_index("z")
    n, ntp = 2 * nz, 4
    ctx = 2 * z + x
    tp = 2 * y + core
    unit = ff // nz

    o_full = jnp.concatenate(gather_tp(o_weight, core, y), axis=0)
    gate_s = lax.dynamic_slice_in_dim(gate_weight.T, z * unit, unit, 0)
    up_s = lax.dynamic_slice_in_dim(up_weight.T, z * unit, unit, 0)
    down_s = lax.dynamic_slice_in_dim(down_weight, z * unit, unit, 0)

    inputs = layer_input.astype(F32)
    gain_one = attn_gain.astype(F32)
    factor_one = lax.rsqrt(jnp.mean(inputs * inputs, axis=-1, keepdims=True) + RMS_EPS)
    normed = (inputs * factor_one * gain_one).astype(BF16)
    cosine, sine = rope_tables(positions, hd)
    query = mm(normed, q_weight, 1, 0) + q_bias.astype(F32).reshape(-1)
    query_rot = rotate(query.reshape(rows, heads, hd), cosine[:, None], sine[:, None])
    query_rot = query_rot.astype(BF16).reshape(rows, heads * hd)
    column = (2 * core + y) * hd
    kv_cols = lax.dynamic_slice_in_dim(kv_weight, column, hd, 1)
    kv_own_bias = lax.dynamic_slice_in_dim(kv_bias, column, hd, 0).astype(F32)
    kv_own = mm(normed, kv_cols, 1, 0) + kv_own_bias
    kv_own = jnp.where(core == 0, rotate(kv_own, cosine, sine), kv_own).astype(BF16)

    ids = segment_ids.astype(BF16).reshape(rows // hd, hd)
    ids = jnp.pad(ids, ((0, EXTRA - rows // hd), (0, 0)))
    packed = jnp.concatenate([kv_own, ids], axis=0)
    near = lax.all_to_all(
        jnp.broadcast_to(packed[None], (nz,) + packed.shape), "z", split_axis=0, concat_axis=0, tiled=True
    )
    cot_ahead = column_start(after(cotangent, near), tp)
    far = swap(near, "x")
    kv = (near, far, swap(near, "core"), swap(far, "core"))
    kv, gate_s, up_s, down_s = lax.optimization_barrier((kv, gate_s, up_s, down_s))
    all_ids = jnp.stack([near[:, rows : rows + rows // hd], far[:, rows : rows + rows // hd]]).astype(F32)
    starts = [jnp.sum((all_ids < k).astype(F32)).astype(jnp.int32) for k in (1, 2, 3)]
    lo = jnp.where(
        segment_ids == 0,
        0,
        jnp.where(segment_ids == 1, starts[0], jnp.where(segment_ids == 2, starts[1], starts[2])),
    )
    scal = jnp.stack([ctx, lo[0], lo[-1], core]).astype(jnp.int32)
    lo = lo.reshape(1, rows)

    attended, logs = attend(scal, query_rot, kv, lo)
    attended_all = jnp.concatenate(gather_tp(attended, core, y), axis=1)
    d_hidden = mm(after(cotangent, attended), down_weight, 1, 1).astype(BF16)
    hidden_in = inputs + mm(attended_all, o_full, 1, 0)

    gain_two = mlp_gain.astype(F32)
    factor_two = lax.rsqrt(jnp.mean(hidden_in * hidden_in, axis=-1, keepdims=True) + RMS_EPS)
    normed_two = (hidden_in * factor_two * gain_two).astype(BF16)
    normed_all = column_tokens(normed_two, tp)
    normed_two, cot_ahead = lax.optimization_barrier((normed_two, cot_ahead))

    gate = mm(normed_two, gate_weight, 1, 0)
    up = mm(normed_two, up_weight, 1, 0)
    sig = jax.nn.sigmoid(gate)
    hidden = (gate * sig * up).astype(BF16)
    d_gate = (d_hidden * up * sig * (1.0 + gate * (1.0 - sig))).astype(BF16)
    d_up = (d_hidden * gate * sig).astype(BF16)
    d_normed_two = mm(d_gate, gate_weight, 1, 1) + mm(d_up, up_weight, 1, 1)
    d_half = sum_core(*split_core(d_normed_two, core))
    d_half, hidden = lax.optimization_barrier((d_half, hidden))
    d_half = sum_y(d_half)
    cot_here = jnp.concatenate(after(cot_ahead, d_half), axis=0)
    cot_there = swap(cot_here, "y")
    d_normed_two = join_core(d_half, core).astype(F32)

    w_two = hidden_in * factor_two
    part_mlp_gain = jnp.sum(d_normed_two * w_two, axis=0)
    dg_two = d_normed_two * gain_two
    d_hidden_in = cotangent.astype(F32) + factor_two * (
        dg_two - w_two * jnp.mean(dg_two * w_two, axis=-1, keepdims=True)
    )
    d_attn = d_hidden_in.astype(BF16)
    d_attended = mm(d_attn, o_weight, 1, 1).astype(BF16)
    part = width // n
    g_o = mm(d_attn, attended, 0, 0).astype(BF16).reshape(nz, 2, part, heads * hd).swapaxes(0, 1)
    d_attended, g_o = lax.optimization_barrier((d_attended, g_o))
    g_o = sum_x(g_o, x)

    d_query_rot, keep_near, keep_far, give_near, give_far = attend_back(
        scal, query_rot, kv, lo, attended, logs, d_attended
    )
    d_query_rot, g_o, cot_there = lax.optimization_barrier((d_query_rot, g_o, cot_there))
    cots = (cotangent, cot_here, cot_there, swap(cot_here, "core"), swap(cot_there, "core"))
    d_far = (keep_far.astype(F32) + swap(give_far, "core").astype(F32)).astype(BF16)
    came_near = swap(give_near, "core")
    came_far = swap(d_far, "x")
    g_o = lax.all_to_all(g_o, "z", split_axis=0, concat_axis=0, tiled=True)
    d_query_rot, hidden = after((d_query_rot, hidden), d_far)
    mlp_part = mm(hidden, down_weight, 1, 0)
    o_half = sum_core(*split_core(mlp_part, core))
    d_query = rotate(d_query_rot.reshape(rows, heads, hd), cosine[:, None], -sine[:, None])
    d_query = d_query.astype(BF16).reshape(rows, heads * hd)
    g_q = mm(normed, d_query, 0, 0).astype(BF16).reshape(nz, 2, part, heads * hd).swapaxes(0, 1)
    came_near, g_q, o_half, normed_all, cots = lax.optimization_barrier((came_near, g_q, o_half, normed_all, cots))
    g_q = sum_x(g_q, x)
    o_half = sum_y(o_half)

    place = jnp.stack([x, z, tp]).astype(jnp.int32)
    keep_down, give_down, d_gate_c, d_up_c = column_first(place, normed_all, cots, gate_s, up_s, down_s, n)
    came_far, g_o, g_q, o_half, d_gate_c, d_up_c, give_down = lax.optimization_barrier(
        (came_far, g_o, g_q, o_half, d_gate_c, d_up_c, give_down)
    )
    ring = [
        (keep_near[s].astype(F32) + came_near[s].astype(F32) + came_far[s].astype(F32)).astype(BF16)
        for s in range(nz)
    ]
    ring, give_down, d_gate_c = lax.optimization_barrier((ring, give_down, d_gate_c))
    ring = ring[:1] + [along_z(ring[s], s) for s in range(1, nz)]
    came_down = swap(give_down, "x")
    g_q = lax.all_to_all(g_q, "z", split_axis=0, concat_axis=0, tiled=True)
    keep_gate, give_gate, keep_up, give_up = column_second(place, normed_all, d_gate_c, d_up_c, rows, n)
    came_down, ring, g_q, give_gate, give_up = lax.optimization_barrier((came_down, ring, g_q, give_gate, give_up))
    d_kv = sum(r.astype(F32) for r in ring)
    d_kv = jnp.where(core == 0, rotate(d_kv, cosine, -sine), d_kv).astype(BF16)

    def sum_parts(keep, came):
        return [(keep[s].astype(F32) + came[s].astype(F32)).astype(BF16) for s in range(nz)]

    def spread(sums):
        return sums[:1] + [along_z(sums[s], s) for s in range(1, nz)]

    sums, give_gate = lax.optimization_barrier((sum_parts(keep_down, came_down), give_gate))
    came_gate, g_down = swap(give_gate, "x"), spread(sums)
    d_normed = mm(d_query, q_weight, 1, 1) + mm(d_kv, kv_cols, 1, 1)
    d_normed = sum_core(*split_core(d_normed, core))
    d_normed, came_gate, g_down = lax.optimization_barrier((d_normed, came_gate, g_down))
    sums, give_up = lax.optimization_barrier((sum_parts(keep_gate, came_gate), after(give_up, d_normed)))
    came_up, g_gate = swap(give_up, "x"), spread(sums)
    d_normed = sum_y(d_normed)
    d_normed, came_up, g_gate, o_half = lax.optimization_barrier((d_normed, came_up, g_gate, o_half))
    sums, d_normed = lax.optimization_barrier((sum_parts(keep_up, came_up), d_normed))
    g_up = spread(sums)
    d_normed = join_core(d_normed, core).astype(F32)
    w_one = inputs * factor_one
    part_attn_gain = jnp.sum(d_normed * w_one, axis=0)
    dg_one = d_normed * gain_one
    dx = d_hidden_in + factor_one * (dg_one - w_one * jnp.mean(dg_one * w_one, axis=-1, keepdims=True))
    output = (hidden_in + join_core(o_half, core).astype(F32)).astype(BF16)

    small, bias_cols = width // (n * ntp), hd // n
    g_kv = mm(normed, d_kv, 0, 0).astype(BF16).reshape(nz, 2, ntp, small, hd)
    q_bias_sum = jnp.sum(d_query.astype(F32), axis=0).reshape(heads, n, bias_cols).transpose(1, 0, 2)
    tail_rows = jnp.concatenate(
        [
            jnp.broadcast_to(jnp.sum(d_kv.astype(F32), axis=0), (n, hd)),
            part_mlp_gain.reshape(n, part),
            part_attn_gain.reshape(n, part),
            q_bias_sum.reshape(n, heads * bias_cols),
        ],
        axis=1,
    )
    extra = -(-tail_rows.shape[1] // (EXTRA * hd)) * EXTRA
    tail_rows = jnp.pad(tail_rows, ((0, 0), (0, extra * hd - tail_rows.shape[1]))).astype(BF16)
    tail_rows = jnp.broadcast_to(tail_rows.reshape(nz, 2, 1, extra, hd), (nz, 2, ntp, extra, hd))
    g_kv = sum_x(jnp.concatenate([g_kv, tail_rows], axis=3).swapaxes(0, 1), x)
    g_kv = lax.all_to_all(
        g_kv.reshape(nz * ntp, small + extra, hd), ("z", "y", "core"), split_axis=0, concat_axis=0, tiled=True
    )
    g_kv, dx, output, g_up = lax.optimization_barrier((g_kv, dx, output, g_up))
    g_kv = jnp.sum(g_kv.reshape(nz, ntp, small + extra, hd).astype(F32), axis=0)
    sums = lax.dynamic_index_in_dim(g_kv[:, small:], tp, 0, keepdims=False).reshape(-1)[hd:]
    g_mlp_gain = sums[:part]
    g_attn_gain = sums[part : 2 * part]
    g_q_bias = sums[2 * part : 2 * part + heads * bias_cols].reshape(heads, bias_cols)
    g_kv = jnp.concatenate([g_kv[0], g_kv[2], g_kv[1], g_kv[3]], axis=1)
    bias_size = kv_bias.shape[0] // (n * ntp)
    g_kv_bias = lax.dynamic_slice_in_dim(g_kv[small], (ctx * ntp + tp) * bias_size, bias_size, 0)
    g_kv = g_kv[:small]

    g_gate, g_up, g_down = assemble(place, g_gate, g_up, g_down)
    g_o = jnp.sum(g_o.astype(F32), axis=0).T
    g_q = jnp.sum(g_q.astype(F32), axis=0)

    return (
        output,
        dx,
        g_attn_gain,
        g_q,
        g_q_bias,
        g_kv,
        g_kv_bias,
        g_o,
        g_mlp_gain,
        g_gate,
        g_up,
        g_down,
    )


def solution(mesh):
    n, ntp = mesh.shape["ctx"], mesh.shape["tp"]
    fine = jax.sharding.Mesh(mesh.devices.reshape(n // 2, 2, ntp // 2, 2), ("z", "x", "y", "core"))
    ctx, tp = ("z", "x"), ("y", "core")
    both = ctx + tp
    return jax.shard_map(
        per_device,
        mesh=fine,
        in_specs=(
            P(ctx, None),
            P(ctx),
            P(ctx),
            P(),
            P(None, tp),
            P(tp, None),
            P(),
            P(),
            P(tp, None),
            P(),
            P(None, tp),
            P(None, tp),
            P(tp, None),
            P(ctx, None),
        ),
        out_specs=(
            P(ctx, None),
            P(ctx, None),
            P(ctx),
            P(ctx, tp),
            P(tp, ctx),
            P(both, None),
            P(both),
            P(tp, ctx),
            P(ctx),
            P(ctx, tp),
            P(ctx, tp),
            P(tp, ctx),
        ),
        check_vma=False,
    )
```

time: 618 us -> 454 us (0.73)
  waiting for transfers between devices: 288 us -> 87.3 us
  matrix products: 128 us -> 68.7 us
  Pallas kernels: 11.3 us -> 54.4 us
  starting transfers between devices: 71.8 us -> 107 us
  other arithmetic: 48.9 us -> 64.4 us
    all_gather x4 -> x1, waiting for transfers between devices: 135 us -> 0.02 us  [column_tokens(): return lax.all_gather(own, ('z', 'y', 'core'), axis=0, tiled=True)]
    all_to_all x7 -> x4, waiting for transfers between devices: 101 us -> 6.56 us  [the longest x1 6.55 us: per_device(): lax.all_to_all(g_kv.reshape(nz * ntp, small + extra, hd), ('z', 'y', 'cor...]
    ppermute x14 -> x45, starting transfers between devices: 5.46 us -> 65.8 us  [the longest x30 29.4 us: swap(): return lax.ppermute(x, axis, [(0, 1), (1, 0)])]
    dot_general x21 -> x15, matrix products: 128 us -> 68.7 us  [mm(): lax.dot_general(a, b, (((ca,), (cb,)), ((), ())), preferred_element_type=...]
    pallas_call x2 -> x5, Pallas kernels: 11.3 us -> 54.4 us  [the longest x1 23.6 us: column_first(): pl.pallas_call(functools.partial(column_first_kernel, quarters), in_specs...]
    ppermute x14 -> x45, waiting for transfers between devices: 50.7 us -> 80.7 us  [the longest x30 62.8 us: swap(): return lax.ppermute(x, axis, [(0, 1), (1, 0)])]
    all_to_all x7 -> x4, starting transfers between devices: 65.8 us -> 40.8 us  [the longest x1 26.9 us: per_device(): g_o = lax.all_to_all(g_o, 'z', split_axis=0, concat_axis=0, tiled=True)]
    convert_element_type x3 -> x15, other arithmetic: 3.19 us -> 23.2 us  [the longest x3 4.42 us: sum_parts(): (keep[s].astype(F32) + came[s].astype(F32)).astype(BF16)]
  transfers between devices with their start and end apart: 26 -> 50, of which waited for: 14 -> 11; matrix products, arithmetic and copies ran while one was open for 29% -> 31% of each run, Pallas kernels for 2% -> 11%
where the time goes in v2:
time: 454 us; the launch traced here: 445 us
  starting transfers between devices  107 us (24%)
  waiting for transfers between devices  87.3 us (19%)
  matrix products  68.7 us (15%)
  other arithmetic  64.4 us (14%)
  Pallas kernels  54.4 us (12%)
  local copies, waits for them, and re-layouts  46.4 us (10%)
  between operations  17.3 us (4%)
    dot_general x15, matrix products, mm(): lax.dot_general(a, b, (((ca,), (cb,)), ((), ())), preferred_element_type=...  68.7 us
    ppermute x30, waiting for transfers between devices, swap(): return lax.ppermute(x, axis, [(0, 1), (1, 0)])  62.8 us
    ppermute x30, starting transfers between devices, swap(): return lax.ppermute(x, axis, [(0, 1), (1, 0)])  29.4 us
    all_to_all x1, starting transfers between devices, per_device(): g_o = lax.all_to_all(g_o, 'z', split_axis=0, concat_axis=0, tiled=True)  26.9 us
    pallas_call x1, Pallas kernels, column_first(): pl.pallas_call(functools.partial(column_first_kernel, quarters), in_specs...  23.6 us
    ppermute x12, starting transfers between devices, along_z(): lax.ppermute(block, 'z', [(i, (i + distance) % nz) for i in range(nz)])  22.8 us
    ppermute x12, waiting for transfers between devices, along_z(): lax.ppermute(block, 'z', [(i, (i + distance) % nz) for i in range(nz)])  17.9 us
    unnamed x115, local copies, waits for them, and re-layouts  16.9 us
  transfers between devices with their start and end apart: 50, of which 11 were waited for; matrix products, arithmetic and copies ran while one was open for 31% of the time, Pallas kernels for 11%

profile of v2, /device:TPU:0, one launch (start us, length us, event | category | flops | bytes accessed | tf_op | source)
XLA Modules:
  0.0 445.0 jit_solution(11434632035188052889)
XLA Ops:
  19.3 4.9 %all-to-all-start = ((bf16[4,528,128]{2,1,0:T(8,128)(2,1)}), bf16[4,528,128]{2,1,0:T(8,128)(2,1)}, u32[]{:S(2)}, u32[]{:S(2)}) async-start(bf16[4,528,128]{2,1,0:T(8,128)(2,1)} %broadcast_in_dim.22), calls=%async_computation | async-start | bytes 1081344 | tf_op jit(solution)/shard_map/all_to_all | solution.py:503
  48.4 5.7 %collective-permute-done.r1 = bf16[4,528,128]{2,1,0:T(8,128)(2,1)} collective-permute-done((bf16[4,528,128]{2,1,0:T(8,128)(2,1)}, bf16[4,528,128]{2,1,0:T(8,128)(2,1)}, u32[]{:S(2)}, u32[]{:S(2)}) %collective-permute-start) | collective-permute-done | bytes 540704 | tf_op jit(solution)/shard_map/ppermute | solution.py:36
  63.5 4.3 attend.1
  68.4 7.9 %convolution_convert_fusion = bf16[512,2240]{0,1:T(8,128)(2,1)} fusion(bf16[512,1536]{1,0:T(8,128)(2,1)S(1)} %copy-done.10, bf16[2240,1536]{1,0:T(8,128)(2,1)} %param.26), kind=kOutput, calls=%fused_computation.24 | convolution fusion | flops 3524362240 | bytes 10747904 | tf_op jit(solution)/shard_map/dot_general | solution.py:19
  76.3 9.0 %collective-permute-start.11 = (bf16[128,1536]{1,0:T(8,128)(2,1)}, bf16[128,1536]{1,0:T(8,128)(2,1)}, u32[]{:S(2)}, u32[]{:S(2)}) collective-permute-start(bf16[128,1536]{1,0:T(8,128)(2,1)} %constant_dynamic-slice_fusion.6), channel_id=1, source_target_pairs={{0,24},{8,0},{16,8},{24,16},{1,25},{9,1},{17,9},{25,17},{2,26},{10... | collective-permute-start | bytes 1179656 | tf_op jit(solution)/shard_map/ppermute | solution.py:93
  94.8 7.2 %fusion.102 = f32[512,2240]{0,1:T(8,128)S(1)} fusion(bf16[512,1536]{1,0:T(8,128)(2,1)} %copy-done.12, bf16[1536,2240]{0,1:T(8,128)(2,1)} %param.24), kind=kOutput, calls=%fused_computation.229 | convolution fusion | flops 3523215360 | bytes 13041664 | tf_op jit(solution)/shard_map/dot_general | solution.py:19
  104.1 9.1 %multiply_convert_fusion = (bf16[512,2240]{0,1:T(8,128)(2,1)}, f32[512,2240]{0,1:T(8,128)}) fusion(f32[512,2240]{0,1:T(8,128)S(1)} %fusion.102, bf16[512,1536]{1,0:T(8,128)(2,1)S(1)} %copy-done.13, bf16[1536,2240]{0,1:T(8,128)(2,1)} %param.25), kind=kOutput, calls=%fused_computation.22 | convolution fusion | flops 3530096640 | bytes 19922944 | tf_op jit(solution)/shard_map/dot_general | solution.py:19
  113.2 9.3 %fusion.33 = f32[512,1536]{1,0:T(8,128)S(1)} fusion(bf16[1536,2240]{0,1:T(8,128)(2,1)} %param.24, f32[512,2240]{0,1:T(8,128)} %get-tuple-element.329, bf16[512,2240]{0,1:T(8,128)(2,1)} %convolution_convert_fusion, f32[512,2240]{0,1:T(8,128)} %copy-done.52), kind=kOutput, calls=%fused_computation.49 | convolution fusion | flops 3535831040 | bytes 21495808 | tf_op jit(solution)/shard_map/dot_general | solution.py:19
  122.6 6.7 %convolution_add_fusion.1 = f32[512,1536]{1,0:T(8,128)S(1)} fusion(f32[512,1536]{1,0:T(8,128)S(1)} %fusion.33, bf16[1536,2240]{0,1:T(8,128)(2,1)} %param.25, f32[512,2240]{0,1:T(8,128)S(1)} %copy-done.53, bf16[512,2240]{0,1:T(8,128)(2,1)S(1)} %copy-done.54), kind=kOutput, calls=%fused_computation.32 | convolution fusion | flops 3532029952 | bytes 20054016 | tf_op jit(solution)/shard_map/dot_general | solution.py:19
  138.0 26.1 %collective-permute-done.13 = bf16[256,1536]{1,0:T(8,128)(2,1)S(1)} collective-permute-done((bf16[256,1536]{1,0:T(8,128)(2,1)S(1)}, bf16[256,1536]{1,0:T(8,128)(2,1)S(1)}, u32[]{:S(2)}, u32[]{:S(2)}) %collective-permute-start.13) | collective-permute-done | bytes 786464 | tf_op jit(solution)/shard_map/ppermute | solution.py:36
  179.1 6.8 %attend_back.1 = (f32[512,384]{1,0:T(8,128)}, bf16[4,512,128]{2,1,0:T(8,128)(2,1)}, bf16[4,512,128]{2,1,0:T(8,128)(2,1)}, bf16[4,512,128]{2,1,0:T(8,128)(2,1)}, bf16[4,512,128]{2,1,0:T(8,128)(2,1)}) custom-call(s32[4]{0:T(128)} %pad_add_fusion.scal, bf16[512,384]{1,0:T(8,128)(2,1)} %copy.44.q_ref, bf16[4,528,128]{2,1,0:T(8,128)(2,1)} %all-to-all-done.r0, ...), custom_call_target="tpu_custom_call" | custom-call | flops 8053063680 | bytes 8650752 | tf_op jit(solution)/shard_map/attend_back/pallas_call | solution.py:267
  187.8 10.6 %collective-permute-start.16 = (bf16[4,192,384]{2,1,0:T(8,128)(2,1)}, bf16[4,192,384]{2,1,0:T(8,128)(2,1)}, u32[]{:S(2)}, u32[]{:S(2)}) collective-permute-start(bf16[4,192,384]{2,1,0:T(8,128)(2,1)} %dynamic-slice_bitcast_fusion.3), channel_id=1, source_target_pairs={{0,4},{4,0},{1,5},{5,1},{2,6},{6,2},{3,7},{7,3},{8,12},{12,8},{9,1... | collective-permute-start | bytes 1769480 | tf_op jit(solution)/shard_map/ppermute | solution.py:36
  200.8 11.8 %collective-permute-done.16 = bf16[4,192,384]{2,1,0:T(8,128)(2,1)} collective-permute-done((bf16[4,192,384]{2,1,0:T(8,128)(2,1)}, bf16[4,192,384]{2,1,0:T(8,128)(2,1)}, u32[]{:S(2)}, u32[]{:S(2)}) %collective-permute-start.16) | collective-permute-done | bytes 589856 | tf_op jit(solution)/shard_map/ppermute | solution.py:36
  214.8 6.2 %fusion.103 = f32[512,1536]{1,0:T(8,128)S(1)} fusion(bf16[512,2240]{0,1:T(8,128)(2,1)S(1)} %copy-done.51, bf16[2240,1536]{1,0:T(8,128)(2,1)} %param.26), kind=kOutput, calls=%fused_computation.230 | convolution fusion | flops 3523215360 | bytes 12320768 | tf_op jit(solution)/shard_map/dot_general | solution.py:19
  227.3 26.9 %all-to-all-start.1 = ((bf16[4,192,384]{2,1,0:T(8,128)(2,1)}), bf16[4,192,384]{2,1,0:T(8,128)(2,1)}, u32[]{:S(2)}, u32[]{:S(2)}) async-start(bf16[4,192,384]{2,1,0:T(8,128)(2,1)} %fusion.43), calls=%async_computation.1 | async-start | bytes 1179648 | tf_op jit(solution)/shard_map/all_to_all | solution.py:566
  265.7 23.6 %column_first.1 = (bf16[4,192,560]{2,1,0:T(8,128)(2,1)}, bf16[4,192,560]{2,1,0:T(8,128)(2,1)}, bf16[560,2048]{1,0:T(8,128)(2,1)}, bf16[560,2048]{1,0:T(8,128)(2,1)}) custom-call(s32[3]{0:T(128)} %pad_add_fusion.1.scal, bf16[2048,1536]{1,0:T(8,128)(2,1)} %all-gather.2.cloned.1.call-done.normed, bf16[512,1536]{1,0:T(8,128)(2,1)} %refs_0_, ...), custom_call_target="tpu_custom_call" | custom-call | flops 14092861440 | bytes 22904832 | tf_op jit(solution)/shard_map/column_first/pallas_call | solution.py:382
  295.6 5.1 %all-to-all-start.2 = ((bf16[4,192,384]{2,1,0:T(8,128)(2,1)}), bf16[4,192,384]{2,1,0:T(8,128)(2,1)}, u32[]{:S(2)}, u32[]{:S(2)}) async-start(bf16[4,192,384]{2,1,0:T(8,128)(2,1)} %fusion.42), calls=%async_computation.2 | async-start | bytes 1179648 | tf_op jit(solution)/shard_map/all_to_all | solution.py:589
  310.6 14.8 %column_second.1 = (bf16[4,192,560]{2,1,0:T(8,128)(2,1)}, bf16[4,192,560]{2,1,0:T(8,128)(2,1)}, bf16[4,192,560]{2,1,0:T(8,128)(2,1)}, bf16[4,192,560]{2,1,0:T(8,128)(2,1)}) custom-call(s32[3]{0:T(128)} %pad_add_fusion.1.scal, bf16[2048,1536]{1,0:T(8,128)(2,1)} %all-gather.2.cloned.1.call-done.normed, bf16[560,2048]{1,0:T(8,128)(2,1)} %get-tuple-element.174.d_gate_ref, ...), custom_call_target="tpu_custom_call" | custom-call | flops 7046430720 | bytes 9732096 | tf_op jit(solution)/shard_map/column_second/pallas_call | solution.py:405
  339.5 6.1 %collective-permute-done.31.refs_9_ = bf16[192,560]{1,0:T(8,128)(2,1)S(1)} collective-permute-done((bf16[192,560]{1,0:T(8,128)(2,1)S(1)}, bf16[192,560]{1,0:T(8,128)(2,1)S(1)}, u32[]{:S(2)}, u32[]{:S(2)}) %collective-permute-start.31) | collective-permute-done | bytes 215072 | tf_op jit(solution)/shard_map/ppermute | solution.py:80
  345.6 9.7 %collective-permute-done.32.refs_10_ = bf16[192,560]{1,0:T(8,128)(2,1)S(1)} collective-permute-done((bf16[192,560]{1,0:T(8,128)(2,1)S(1)}, bf16[192,560]{1,0:T(8,128)(2,1)S(1)}, u32[]{:S(2)}, u32[]{:S(2)}) %collective-permute-start.32) | collective-permute-done | bytes 215072 | tf_op jit(solution)/shard_map/ppermute | solution.py:80
  367.0 10.6 %collective-permute-done.34 = bf16[256,1536]{1,0:T(8,128)(2,1)S(1)} collective-permute-done((bf16[256,1536]{1,0:T(8,128)(2,1)S(1)}, bf16[256,1536]{1,0:T(8,128)(2,1)S(1)}, u32[]{:S(2)}, u32[]{:S(2)}) %collective-permute-start.34) | collective-permute-done | bytes 786464 | tf_op jit(solution)/shard_map/ppermute | solution.py:36
  406.1 4.9 %fusion.21 = f32[512,1536]{1,0:T(8,128)} fusion(f32[512,1536]{1,0:T(8,128)} %copy-done.1, bf16[512,1536]{1,0:T(8,128)(2,1)S(1)} %copy-done.4, f32[512]{0:T(512)S(1)} %broadcast_multiply_fusion, f32[1536]{0:T(1024)S(1)} %convert_element_type.487, f32[512]{0:T(512)S(1)} %copy-done.43, bf16[256,1536]{1,0:T(8,128)(2,1)} %copy-done.6, bf16[256,1536]{1,0:T(8,128)(2,1)} %copy-done.5), kind=kLoop, calls=%fused_computation.34 | loop fusion | flops 8650752 | bytes 9447424 | tf_op jit(solution)/shard_map/add | solution.py:616
  420.7 6.5 %all-to-all-done.3 = bf16[16,64,128]{2,1,0:T(8,128)(2,1)S(1)} async-done(((bf16[16,64,128]{2,1,0:T(8,128)(2,1)}), bf16[16,64,128]{2,1,0:T(8,128)(2,1)S(1)}, u32[]{:S(2)}, u32[]{:S(2)}) %all-to-all-start.3) | async-done | bytes 262176 | tf_op jit(solution)/shard_map/all_to_all | solution.py:635
  429.9 4.9 %assemble.1 = (f32[192,2240]{1,0:T(8,128)}, f32[192,2240]{1,0:T(8,128)}, f32[2240,192]{1,0:T(8,128)}) custom-call(s32[3]{0:T(128)} %pad_add_fusion.1.scal, bf16[192,560]{1,0:T(8,128)(2,1)} %get-tuple-element.215.refs_0_, bf16[192,560]{1,0:T(8,128)(2,1)} %copy-done.31, bf16[192,560]{1,0:T(8,128)(2,1)} %copy-done.32, bf16[192,560]{1,0:T(8,128)(2,1)} %copy-done.33, ...), custom_call_target="tpu_custom_call" | custom-call | bytes 7741440 | tf_op jit(solution)/shard_map/assemble/pallas_call | solution.py:444
  (305 shorter events, 189.0 us)
Async XLA Ops:
  7.2 69.1 %collective-permute-start.6 = (bf16[384,1536]{1,0:T(8,128)(2,1)}, bf16[384,1536]{1,0:T(8,128)(2,1)}, u32[]{:S(2)}, u32[]{:S(2)}) collective-permute-start(bf16[384,1536]{1,0:T(8,128)(2,1)} %param.22), channel_id=1, source_target_pairs={{0,1},{1,0},{2,3},{3,2},{4,5},{5,4},{6,7},{7,6},{8,9},{9,8},{10,11... | collective-permute-start | bytes 3538952 | tf_op jit(solution)/shard_map/ppermute | solution.py:36
  7.7 52.9 %collective-permute-start.7 = (bf16[384,1536]{1,0:T(8,128)(2,1)}, bf16[384,1536]{1,0:T(8,128)(2,1)}, u32[]{:S(2)}, u32[]{:S(2)}) collective-permute-start(bf16[384,1536]{1,0:T(8,128)(2,1)} %param.22), channel_id=1, source_target_pairs={{0,2},{2,0},{1,3},{3,1},{4,6},{6,4},{5,7},{7,5},{8,10},{10,8},{9,1... | collective-permute-start | bytes 3538952 | tf_op jit(solution)/shard_map/ppermute | solution.py:36
  24.1 239.0 %all-gather.2.cloned.1.call-start = ((), (), s32[]{:S(2)}) async-start(), calls=%async_computation.4 | async-start | bytes 6684672 | tf_op jit(solution)/shard_map/all_gather | solution.py:86
  45.7 49.1 %collective-permute-start.9 = (bf16[128,1536]{1,0:T(8,128)(2,1)}, bf16[128,1536]{1,0:T(8,128)(2,1)}, u32[]{:S(2)}, u32[]{:S(2)}) collective-permute-start(bf16[128,1536]{1,0:T(8,128)(2,1)} %constant_dynamic-slice_fusion.6), channel_id=1, source_target_pairs={{0,8},{8,16},{16,24},{24,0},{1,9},{9,17},{17,25},{25,1},{2,10},{10... | collective-permute-start | bytes 1179656 | tf_op jit(solution)/shard_map/ppermute | solution.py:93
  60.6 34.2 %collective-permute-start.10 = (bf16[128,1536]{1,0:T(8,128)(2,1)}, bf16[128,1536]{1,0:T(8,128)(2,1)}, u32[]{:S(2)}, u32[]{:S(2)}) collective-permute-start(bf16[128,1536]{1,0:T(8,128)(2,1)} %constant_dynamic-slice_fusion.6), channel_id=1, source_target_pairs={{0,16},{8,24},{16,0},{24,8},{1,17},{9,25},{17,1},{25,9},{2,18},{10... | collective-permute-start | bytes 1179656 | tf_op jit(solution)/shard_map/ppermute | solution.py:93
  63.2 22.1 %collective-permute-start.8 = (bf16[384,1536]{1,0:T(8,128)(2,1)}, bf16[384,1536]{1,0:T(8,128)(2,1)S(1)}, u32[]{:S(2)}, u32[]{:S(2)}) collective-permute-start(bf16[384,1536]{1,0:T(8,128)(2,1)} %collective-permute-done.7), channel_id=1, source_target_pairs={{0,1},{1,0},{2,3},{3,2},{4,5},{5,4},{6,7},{7,6},{8,9},{9,8},{10,11... | collective-permute-start | bytes 3538952 | tf_op jit(solution)/shard_map/ppermute | solution.py:36
  136.4 27.7 %collective-permute-start.13 = (bf16[256,1536]{1,0:T(8,128)(2,1)S(1)}, bf16[256,1536]{1,0:T(8,128)(2,1)S(1)}, u32[]{:S(2)}, u32[]{:S(2)}) collective-permute-start(bf16[256,1536]{1,0:T(8,128)(2,1)S(1)} %add_convert_fusion.6), channel_id=1, source_target_pairs={{0,2},{2,0},{1,3},{3,1},{4,6},{6,4},{5,7},{7,5},{8,10},{10,8},{9,1... | collective-permute-start | bytes 2359304 | tf_op jit(solution)/shard_map/ppermute | solution.py:36
  169.8 44.9 %collective-permute-start.17 = (bf16[384,1536]{1,0:T(8,128)(2,1)}, bf16[384,1536]{1,0:T(8,128)(2,1)}, u32[]{:S(2)}, u32[]{:S(2)}) collective-permute-start(bf16[384,1536]{1,0:T(8,128)(2,1)} %constant_dynamic-update-slice_fusion.refs_1_), channel_id=1, source_target_pairs={{0,2},{2,0},{1,3},{3,1},{4,6},{6,4},{5,7},{7,5},{8,10},{10,8},{9,1... | collective-permute-start | bytes 3538952 | tf_op jit(solution)/shard_map/ppermute | solution.py:36
  187.8 24.7 %collective-permute-start.16 = (bf16[4,192,384]{2,1,0:T(8,128)(2,1)}, bf16[4,192,384]{2,1,0:T(8,128)(2,1)}, u32[]{:S(2)}, u32[]{:S(2)}) collective-permute-start(bf16[4,192,384]{2,1,0:T(8,128)(2,1)} %dynamic-slice_bitcast_fusion.3), channel_id=1, source_target_pairs={{0,4},{4,0},{1,5},{5,1},{2,6},{6,2},{3,7},{7,3},{8,12},{12,8},{9,1... | collective-permute-start | bytes 1769480 | tf_op jit(solution)/shard_map/ppermute | solution.py:36
  198.4 64.7 %collective-permute-start.20 = (bf16[384,1536]{1,0:T(8,128)(2,1)}, bf16[384,1536]{1,0:T(8,128)(2,1)}, u32[]{:S(2)}, u32[]{:S(2)}) collective-permute-start(bf16[384,1536]{1,0:T(8,128)(2,1)} %constant_dynamic-update-slice_fusion.refs_1_), channel_id=1, source_target_pairs={{0,1},{1,0},{2,3},{3,2},{4,5},{5,4},{6,7},{7,6},{8,9},{9,8},{10,11... | collective-permute-start | bytes 3538952 | tf_op jit(solution)/shard_map/ppermute | solution.py:36
  223.6 37.2 %collective-permute-start.19 = (bf16[256,1536]{1,0:T(8,128)(2,1)}, bf16[256,1536]{1,0:T(8,128)(2,1)}, u32[]{:S(2)}, u32[]{:S(2)}) collective-permute-start(bf16[256,1536]{1,0:T(8,128)(2,1)} %dynamic-slice_convert_fusion.1), channel_id=1, source_target_pairs={{0,1},{1,0},{2,3},{3,2},{4,5},{5,4},{6,7},{7,6},{8,9},{9,8},{10,11... | collective-permute-start | bytes 2359304 | tf_op jit(solution)/shard_map/ppermute | solution.py:36
  223.6 39.5 %collective-permute-start.21 = (bf16[384,1536]{1,0:T(8,128)(2,1)}, bf16[384,1536]{1,0:T(8,128)(2,1)}, u32[]{:S(2)}, u32[]{:S(2)}) collective-permute-start(bf16[384,1536]{1,0:T(8,128)(2,1)} %collective-permute-done.17.refs_2_), channel_id=1, source_target_pairs={{0,1},{1,0},{2,3},{3,2},{4,5},{5,4},{6,7},{7,6},{8,9},{9,8},{10,11... | collective-permute-start | bytes 3538952 | tf_op jit(solution)/shard_map/ppermute | solution.py:36
  225.6 37.5 %collective-permute-start.15 = (bf16[4,512,128]{2,1,0:T(8,128)(2,1)}, bf16[4,512,128]{2,1,0:T(8,128)(2,1)}, u32[]{:S(2)}, u32[]{:S(2)}) collective-permute-start(bf16[4,512,128]{2,1,0:T(8,128)(2,1)} %get-tuple-element.133), channel_id=1, source_target_pairs={{0,1},{1,0},{2,3},{3,2},{4,5},{5,4},{6,7},{7,6},{8,9},{9,8},{10,11... | collective-permute-start | bytes 1572872 | tf_op jit(solution)/shard_map/ppermute | solution.py:36
  225.6 65.9 %collective-permute-start.22 = (bf16[4,512,128]{2,1,0:T(8,128)(2,1)}, bf16[4,512,128]{2,1,0:T(8,128)(2,1)}, u32[]{:S(2)}, u32[]{:S(2)}) collective-permute-start(bf16[4,512,128]{2,1,0:T(8,128)(2,1)} %add_convert_fusion.7), channel_id=1, source_target_pairs={{0,4},{4,0},{1,5},{5,1},{2,6},{6,2},{3,7},{7,3},{8,12},{12,8},{9,1... | collective-permute-start | bytes 1572872 | tf_op jit(solution)/shard_map/ppermute | solution.py:36
  227.3 64.1 %all-to-all-start.1 = ((bf16[4,192,384]{2,1,0:T(8,128)(2,1)}), bf16[4,192,384]{2,1,0:T(8,128)(2,1)}, u32[]{:S(2)}, u32[]{:S(2)}) async-start(bf16[4,192,384]{2,1,0:T(8,128)(2,1)} %fusion.43), calls=%async_computation.1 | async-start | bytes 1179648 | tf_op jit(solution)/shard_map/all_to_all | solution.py:566
  264.3 25.1 %collective-permute-start.23 = (bf16[4,192,384]{2,1,0:T(8,128)(2,1)S(1)}, bf16[4,192,384]{2,1,0:T(8,128)(2,1)S(1)}, u32[]{:S(2)}, u32[]{:S(2)}) collective-permute-start(bf16[4,192,384]{2,1,0:T(8,128)(2,1)S(1)} %dynamic-slice_bitcast_fusion.2), channel_id=1, source_target_pairs={{0,4},{4,0},{1,5},{5,1},{2,6},{6,2},{3,7},{7,3},{8,12},{12,8},{9,1... | collective-permute-start | bytes 1769480 | tf_op jit(solution)/shard_map/ppermute | solution.py:36
  264.6 25.7 %collective-permute-start.24 = (bf16[256,1536]{1,0:T(8,128)(2,1)}, bf16[256,1536]{1,0:T(8,128)(2,1)S(1)}, u32[]{:S(2)}, u32[]{:S(2)}) collective-permute-start(bf16[256,1536]{1,0:T(8,128)(2,1)} %add_convert_fusion.4), channel_id=1, source_target_pairs={{0,2},{2,0},{1,3},{3,1},{4,6},{6,4},{5,7},{7,5},{8,10},{10,8},{9,1... | collective-permute-start | bytes 2359304 | tf_op jit(solution)/shard_map/ppermute | solution.py:36
  293.8 32.2 %collective-permute-start.25 = (bf16[4,192,560]{2,1,0:T(8,128)(2,1)}, bf16[4,192,560]{2,1,0:T(8,128)(2,1)}, u32[]{:S(2)}, u32[]{:S(2)}) collective-permute-start(bf16[4,192,560]{2,1,0:T(8,128)(2,1)} %get-tuple-element.168), channel_id=1, source_target_pairs={{0,4},{4,0},{1,5},{5,1},{2,6},{6,2},{3,7},{7,3},{8,12},{12,8},{9,1... | collective-permute-start | bytes 2580488 | tf_op jit(solution)/shard_map/ppermute | solution.py:36
  295.6 30.5 %all-to-all-start.2 = ((bf16[4,192,384]{2,1,0:T(8,128)(2,1)}), bf16[4,192,384]{2,1,0:T(8,128)(2,1)}, u32[]{:S(2)}, u32[]{:S(2)}) async-start(bf16[4,192,384]{2,1,0:T(8,128)(2,1)} %fusion.42), calls=%async_computation.2 | async-start | bytes 1179648 | tf_op jit(solution)/shard_map/all_to_all | solution.py:589
  334.5 24.1 %collective-permute-start.30 = (bf16[4,192,560]{2,1,0:T(8,128)(2,1)S(1)}, bf16[4,192,560]{2,1,0:T(8,128)(2,1)S(1)}, u32[]{:S(2)}, u32[]{:S(2)}) collective-permute-start(bf16[4,192,560]{2,1,0:T(8,128)(2,1)S(1)} %copy-done.50), channel_id=1, source_target_pairs={{0,4},{4,0},{1,5},{5,1},{2,6},{6,2},{3,7},{7,3},{8,12},{12,8},{9,1... | collective-permute-start | bytes 2580488 | tf_op jit(solution)/shard_map/ppermute | solution.py:36
  360.5 22.9 %collective-permute-start.35 = (bf16[4,192,560]{2,1,0:T(8,128)(2,1)S(1)}, bf16[4,192,560]{2,1,0:T(8,128)(2,1)S(1)}, u32[]{:S(2)}, u32[]{:S(2)}) collective-permute-start(bf16[4,192,560]{2,1,0:T(8,128)(2,1)S(1)} %copy-done.49), channel_id=1, source_target_pairs={{0,4},{4,0},{1,5},{5,1},{2,6},{6,2},{3,7},{7,3},{8,12},{12,8},{9,1... | collective-permute-start | bytes 2580488 | tf_op jit(solution)/shard_map/ppermute | solution.py:36
  392.7 28.1 %collective-permute-start.42 = (bf16[192,560]{1,0:T(8,128)(2,1)}, bf16[192,560]{1,0:T(8,128)(2,1)}, u32[]{:S(2)}, u32[]{:S(2)}) collective-permute-start(bf16[192,560]{1,0:T(8,128)(2,1)} %get-tuple-element.207), channel_id=1, source_target_pairs={{0,8},{8,16},{16,24},{24,0},{1,9},{9,17},{17,25},{25,1},{2,10},{10... | collective-permute-start | bytes 645128 | tf_op jit(solution)/shard_map/ppermute | solution.py:80
  396.4 24.4 %collective-permute-start.43 = (bf16[192,560]{1,0:T(8,128)(2,1)}, bf16[192,560]{1,0:T(8,128)(2,1)}, u32[]{:S(2)}, u32[]{:S(2)}) collective-permute-start(bf16[192,560]{1,0:T(8,128)(2,1)} %get-tuple-element.208), channel_id=1, source_target_pairs={{0,16},{8,24},{16,0},{24,8},{1,17},{9,25},{17,1},{25,9},{2,18},{10... | collective-permute-start | bytes 645128 | tf_op jit(solution)/shard_map/ppermute | solution.py:80
  399.0 21.7 %collective-permute-start.44 = (bf16[192,560]{1,0:T(8,128)(2,1)}, bf16[192,560]{1,0:T(8,128)(2,1)}, u32[]{:S(2)}, u32[]{:S(2)}) collective-permute-start(bf16[192,560]{1,0:T(8,128)(2,1)} %get-tuple-element.209), channel_id=1, source_target_pairs={{0,24},{8,0},{16,8},{24,16},{1,25},{9,1},{17,9},{25,17},{2,26},{10... | collective-permute-start | bytes 645128 | tf_op jit(solution)/shard_map/ppermute | solution.py:80
  (81 other events, 1020.9 us)
Sparse Core Ops, SparseCore 0:
  113.3 72.8 all-gather.1

commit v3 on v2

--- a/solution.py
+++ b/solution.py
@@ -86,13 +86,6 @@
     return lax.all_gather(own, ("z", "y", "core"), axis=0, tiled=True)
 
 
-def column_start(block, tp):
-    nz = lax.axis_size("z")
-    quarter = block.shape[0] // 4
-    own = lax.dynamic_slice_in_dim(block, tp * quarter, quarter, 0)
-    return tuple(lax.ppermute(own, "z", [(i, (i + s) % nz) for i in range(nz)]) for s in range(1, nz))
-
-
 def after(values, *done):
     return lax.optimization_barrier((values, done))[0]
 
@@ -167,7 +160,7 @@
 
 
 def attend_back_kernel(
-    scal, q_ref, r0, r1, r2, r3, lo_ref, att_ref, log_ref, d_ref, dq_ref, keep_near, keep_far, give_near, give_far, acc, delta
+    scal, q_ref, r0, r1, r2, r3, lo_ref, att_ref, log_ref, d_ref, cos_ref, sin_ref, dq_ref, keep_near, keep_far, give_near, give_far, acc, delta
 ):
     refs = (r0, r1, r2, r3)
     rows, width = q_ref.shape
@@ -226,20 +219,25 @@
 
     for_blocks(scal, rows, run)
     for h in range(heads):
-        dq_ref[:, h * hd : (h + 1) * hd] = (acc[h] * scale).T
+        dq = (acc[h] * scale).T
+        dq = dq * cos_ref[...] + pltpu.roll(dq, hd // 2, 1) * sin_ref[...]
+        dq_ref[:, h * hd : (h + 1) * hd] = dq.astype(BF16)
 
 
 VMEM = pl.BlockSpec(memory_space=pltpu.VMEM)
 SMEM = pl.BlockSpec(memory_space=pltpu.SMEM)
-LIMIT = 56 * 1024 * 1024
+ANYWHERE = pl.BlockSpec(memory_space=pl.ANY)
+MIB = 1024 * 1024
+
+
+def cost(us):
+    return pl.CostEstimate(flops=int(us * 1.15e9), bytes_accessed=0, transcendentals=0)
 
 
 def attend(scal, q, kv, lo):
     rows, width = q.shape
     hd = kv[0].shape[2]
     heads = width // hd
-    blocks = 2 * kv[0].shape[0]
-    work = rows * width * rows * blocks
     return pl.pallas_call(
         attend_kernel,
         in_specs=[SMEM] + [VMEM] * 6,
@@ -249,33 +247,27 @@
             jax.ShapeDtypeStruct((heads, 8, rows), F32),
         ],
         scratch_shapes=[pltpu.VMEM((heads, hd, rows), F32), pltpu.VMEM((heads, 8, rows), F32)],
-        compiler_params=pltpu.CompilerParams(vmem_limit_bytes=LIMIT),
-        cost_estimate=pl.CostEstimate(
-            flops=4 * work, bytes_accessed=16 * kv[0].size, transcendentals=work // hd
-        ),
+        compiler_params=pltpu.CompilerParams(vmem_limit_bytes=20 * MIB),
+        cost_estimate=cost(50),
         name="attend",
     )(scal, q, *kv, lo)
 
 
-def attend_back(scal, q, kv, lo, att, logs, d_att):
+def attend_back(scal, q, kv, lo, att, logs, d_att, cos, sin):
     rows, width = q.shape
     hd = kv[0].shape[2]
     heads = width // hd
-    blocks = 2 * kv[0].shape[0]
-    work = rows * width * rows * blocks
     grads = jax.ShapeDtypeStruct(kv[0].shape[:1] + (rows, hd), BF16)
     return pl.pallas_call(
         attend_back_kernel,
-        in_specs=[SMEM] + [VMEM] * 9,
+        in_specs=[SMEM] + [VMEM] * 11,
         out_specs=[VMEM] * 5,
-        out_shape=[jax.ShapeDtypeStruct((rows, width), F32)] + [grads] * 4,
+        out_shape=[jax.ShapeDtypeStruct((rows, width), BF16)] + [grads] * 4,
         scratch_shapes=[pltpu.VMEM((heads, hd, rows), F32), pltpu.VMEM((heads, 8, rows), F32)],
-        compiler_params=pltpu.CompilerParams(vmem_limit_bytes=LIMIT),
-        cost_estimate=pl.CostEstimate(
-            flops=10 * work, bytes_accessed=32 * kv[0].size, transcendentals=work // hd
-        ),
+        compiler_params=pltpu.CompilerParams(vmem_limit_bytes=26 * MIB),
+        cost_estimate=cost(8),
         name="attend_back",
-    )(scal, q, *kv, lo, att, logs, d_att)
+    )(scal, q, *kv, lo, att, logs, d_att, cos, sin)
 
 
 CHUNK = 512
@@ -369,9 +361,6 @@
     column_put(scal, au, ku, gu)
 
 
-ANYWHERE = pl.BlockSpec(memory_space=pl.ANY)
-
-
 def column_first(scal, normed, cots, gate_s, up_s, down_s, n):
     unit, width = gate_s.shape
     quarters = len(cots) - 1
@@ -387,12 +376,8 @@
         scratch_shapes=[pltpu.VMEM((slots, CHUNK, width), BF16)] * 2
         + [pltpu.VMEM((unit, width), F32)]
         + [pltpu.SemaphoreType.DMA((slots,))] * 2,
-        compiler_params=pltpu.CompilerParams(vmem_limit_bytes=LIMIT),
-        cost_estimate=pl.CostEstimate(
-            flops=8 * tokens * width * unit,
-            bytes_accessed=4 * tokens * width + 12 * width * unit,
-            transcendentals=tokens * unit,
-        ),
+        compiler_params=pltpu.CompilerParams(vmem_limit_bytes=50 * MIB),
+        cost_estimate=cost(14),
         name="column_first",
     )(scal, normed, *cots, gate_s, up_s, down_s)
 
@@ -410,14 +395,120 @@
         scratch_shapes=[pltpu.VMEM((slots, CHUNK, width), BF16)]
         + [pltpu.VMEM((unit, width), F32)] * 2
         + [pltpu.SemaphoreType.DMA((slots,))],
-        compiler_params=pltpu.CompilerParams(vmem_limit_bytes=LIMIT),
-        cost_estimate=pl.CostEstimate(
-            flops=4 * tokens * width * unit,
-            bytes_accessed=2 * tokens * width + 4 * width * unit,
-            transcendentals=0,
-        ),
+        compiler_params=pltpu.CompilerParams(vmem_limit_bytes=40 * MIB),
+        cost_estimate=cost(10),
         name="column_second",
     )(scal, normed, d_gate, d_up)
+
+
+FF_STEPS = 4
+
+
+def mlp_kernel(scal, n_ref, dh_ref, gate_ref, up_ref, hidden_ref, d_keep, d_give, d_acc):
+    step = pl.program_id(0)
+    gate = mm(gate_ref[...], n_ref[...], 1, 1)
+    up = mm(up_ref[...], n_ref[...], 1, 1)
+    d_hidden = dh_ref[...].astype(F32)
+    sig = 1.0 / (1.0 + jnp.exp(-gate))
+    silu = gate * sig
+    hidden_ref[...] = (silu * up).astype(BF16)
+    d_gate = (d_hidden * up * sig * (1.0 + gate * (1.0 - sig))).astype(BF16)
+    d_up = (d_hidden * silu).astype(BF16)
+    d_normed = mm(d_gate, gate_ref[...], 0, 0) + mm(d_up, up_ref[...], 0, 0)
+
+    @pl.when(step == 0)
+    def _():
+        d_acc[...] = d_normed
+
+    @pl.when(step > 0)
+    def _():
+        d_acc[...] += d_normed
+
+    @pl.when(step == FF_STEPS - 1)
+    def _():
+        halves(scal[0], d_acc, d_keep, d_give)
+
+
+def mlp(core, normed, d_hidden, gate_t, up_t):
+    rows, width = normed.shape
+    ff = gate_t.shape[0]
+    units = pl.BlockSpec((ff // FF_STEPS, width), lambda i: (i, 0))
+    tokens = pl.BlockSpec((ff // FF_STEPS, rows), lambda i: (i, 0))
+    return pl.pallas_call(
+        mlp_kernel,
+        grid=(FF_STEPS,),
+        in_specs=[SMEM, VMEM, tokens, units, units],
+        out_specs=[tokens, VMEM, VMEM],
+        out_shape=[
+            jax.ShapeDtypeStruct((ff, rows), BF16),
+            jax.ShapeDtypeStruct((rows // 2, width), F32),
+            jax.ShapeDtypeStruct((rows // 2, width), BF16),
+        ],
+        scratch_shapes=[pltpu.VMEM((rows, width), F32)],
+        compiler_params=pltpu.CompilerParams(vmem_limit_bytes=40 * MIB, dimension_semantics=("arbitrary",)),
+        cost_estimate=cost(12),
+        name="mlp",
+    )(core.reshape(1).astype(jnp.int32), normed, d_hidden, gate_t, up_t)
+
+
+def halves(core, total, keep, give):
+    half = total.shape[0] // 2
+    keep[...] = total[pl.ds(pl.multiple_of(core * half, half), half), :]
+    give[...] = total[pl.ds(pl.multiple_of((1 - core) * half, half), half), :].astype(BF16)
+
+
+def project_kernel(scal, *refs):
+    count = len(refs) - 13
+    ring, (cos_ref, sin_ref, q_ref, qw_ref, kvw_ref, h_ref, down_ref) = refs[:count], refs[count : count + 7]
+    kv_ref, d_keep, d_give, o_keep, o_give, total = refs[count + 7 :]
+    d_kv = ring[0][...].astype(F32)
+    for piece in ring[1:]:
+        d_kv += piece[...].astype(F32)
+    turned = d_kv * cos_ref[...] + pltpu.roll(d_kv, d_kv.shape[1] // 2, 1) * sin_ref[...]
+    d_kv = jnp.where(scal[0] == 0, turned, d_kv).astype(BF16)
+    kv_ref[...] = d_kv
+    total[...] = mm(q_ref[...], qw_ref[...], 1, 1) + mm(d_kv, kvw_ref[...], 1, 1)
+    halves(scal[0], total, d_keep, d_give)
+    total[...] = mm(h_ref[...], down_ref[...], 0, 0)
+    halves(scal[0], total, o_keep, o_give)
+
+
+def project(core, ring, cos, sin, d_query, q_weight, kv_cols, hidden, down):
+    rows, width = d_query.shape[0], q_weight.shape[0]
+    keep = jax.ShapeDtypeStruct((rows // 2, width), F32)
+    give = jax.ShapeDtypeStruct((rows // 2, width), BF16)
+    return pl.pallas_call(
+        project_kernel,
+        in_specs=[SMEM] + [VMEM] * (len(ring) + 7),
+        out_specs=[VMEM] * 5,
+        out_shape=[jax.ShapeDtypeStruct(ring[0].shape, BF16), keep, give, keep, give],
+        scratch_shapes=[pltpu.VMEM((rows, width), F32)],
+        compiler_params=pltpu.CompilerParams(vmem_limit_bytes=36 * MIB),
+        cost_estimate=cost(30),
+        name="project",
+    )(core.reshape(1).astype(jnp.int32), *ring, cos, sin, d_query, q_weight, kv_cols, hidden, down)
+
+
+def norm_back_kernel(x_ref, factor_ref, gain_ref, dn_ref, base_ref, dx_ref, gain_grad_ref):
+    factor = factor_ref[...]
+    w = x_ref[...].astype(F32) * factor
+    dn = dn_ref[...].astype(F32)
+    gain_grad_ref[...] = jnp.sum(dn * w, axis=0, keepdims=True)
+    dg = dn * gain_ref[...].astype(F32)
+    dx_ref[...] = base_ref[...] + factor * (dg - w * jnp.mean(dg * w, axis=-1, keepdims=True))
+
+
+def norm_back(x, factor, gain, dn, base):
+    rows, width = x.shape
+    return pl.pallas_call(
+        norm_back_kernel,
+        in_specs=[VMEM] * 5,
+        out_specs=[VMEM] * 2,
+        out_shape=[jax.ShapeDtypeStruct((rows, width), F32), jax.ShapeDtypeStruct((1, width), F32)],
+        compiler_params=pltpu.CompilerParams(vmem_limit_bytes=24 * MIB),
+        cost_estimate=cost(30),
+        name="norm_back",
+    )(x, factor, gain.reshape(1, width), dn, base)
 
 
 def assemble_kernel(nz, scal, *refs):
@@ -431,10 +522,8 @@
             value = jnp.where(dist == d, group[d][...], value)
         return value.astype(F32)
 
-    for group, target in zip(groups[:2], targets[:2]):
+    for group, target in zip(groups, targets):
         target[...] = jnp.concatenate([block(group, j) for j in range(nz)], axis=1)
-    for j in range(nz):
-        targets[2][j * unit : (j + 1) * unit, :] = block(groups[2], j).T
 
 
 def assemble(scal, gate, up, down):
@@ -445,9 +534,9 @@
         functools.partial(assemble_kernel, nz),
         in_specs=[SMEM] + [VMEM] * (3 * nz),
         out_specs=[VMEM] * 3,
-        out_shape=[jax.ShapeDtypeStruct(shape, F32) for shape in ((part, ff), (part, ff), (ff, part))],
-        compiler_params=pltpu.CompilerParams(vmem_limit_bytes=LIMIT),
-        cost_estimate=pl.CostEstimate(flops=0, bytes_accessed=18 * ff * part, transcendentals=0),
+        out_shape=[jax.ShapeDtypeStruct((part, ff), F32)] * 3,
+        compiler_params=pltpu.CompilerParams(vmem_limit_bytes=28 * MIB),
+        cost_estimate=cost(5),
         name="assemble",
     )(scal, *gate, *up, *down)
 
@@ -488,6 +577,8 @@
     factor_one = lax.rsqrt(jnp.mean(inputs * inputs, axis=-1, keepdims=True) + RMS_EPS)
     normed = (inputs * factor_one * gain_one).astype(BF16)
     cosine, sine = rope_tables(positions, hd)
+    cos_back = jnp.concatenate([cosine, cosine], axis=1)
+    sin_back = jnp.concatenate([sine, -sine], axis=1)
     query = mm(normed, q_weight, 1, 0) + q_bias.astype(F32).reshape(-1)
     query_rot = rotate(query.reshape(rows, heads, hd), cosine[:, None], sine[:, None])
     query_rot = query_rot.astype(BF16).reshape(rows, heads * hd)
@@ -503,7 +594,9 @@
     near = lax.all_to_all(
         jnp.broadcast_to(packed[None], (nz,) + packed.shape), "z", split_axis=0, concat_axis=0, tiled=True
     )
-    cot_ahead = column_start(after(cotangent, near), tp)
+    quarter = rows // ntp
+    cot_own = lax.dynamic_slice_in_dim(after(cotangent, near), tp * quarter, quarter, 0)
+    cot_ahead = [along_z(cot_own, 1)]
     far = swap(near, "x")
     kv = (near, far, swap(near, "core"), swap(far, "core"))
     kv, gate_s, up_s, down_s = lax.optimization_barrier((kv, gate_s, up_s, down_s))
@@ -518,26 +611,23 @@
     lo = lo.reshape(1, rows)
 
     attended, logs = attend(scal, query_rot, kv, lo)
+    attended, logs, cot_ahead = lax.optimization_barrier((attended, logs, cot_ahead))
+    cot_ahead += [along_z(cot_ahead[-1], 1)]
+    d_hidden = mm(down_weight, after(cotangent, attended), 1, 1).astype(BF16)
     attended_all = jnp.concatenate(gather_tp(attended, core, y), axis=1)
-    d_hidden = mm(after(cotangent, attended), down_weight, 1, 1).astype(BF16)
+    attended_all, d_hidden, cot_ahead = lax.optimization_barrier((attended_all, d_hidden, cot_ahead))
+    while len(cot_ahead) < nz - 1:
+        cot_ahead += [along_z(cot_ahead[-1], 1)]
     hidden_in = inputs + mm(attended_all, o_full, 1, 0)
 
     gain_two = mlp_gain.astype(F32)
     factor_two = lax.rsqrt(jnp.mean(hidden_in * hidden_in, axis=-1, keepdims=True) + RMS_EPS)
     normed_two = (hidden_in * factor_two * gain_two).astype(BF16)
     normed_all = column_tokens(normed_two, tp)
-    normed_two, cot_ahead = lax.optimization_barrier((normed_two, cot_ahead))
-
-    gate = mm(normed_two, gate_weight, 1, 0)
-    up = mm(normed_two, up_weight, 1, 0)
-    sig = jax.nn.sigmoid(gate)
-    hidden = (gate * sig * up).astype(BF16)
-    d_gate = (d_hidden * up * sig * (1.0 + gate * (1.0 - sig))).astype(BF16)
-    d_up = (d_hidden * gate * sig).astype(BF16)
-    d_normed_two = mm(d_gate, gate_weight, 1, 1) + mm(d_up, up_weight, 1, 1)
-    d_half = sum_core(*split_core(d_normed_two, core))
-    d_half, hidden = lax.optimization_barrier((d_half, hidden))
-    d_half = sum_y(d_half)
+
+    hidden, d_keep, d_give = mlp(core, normed_two, d_hidden, gate_weight.T, up_weight.T)
+    hidden, d_keep, d_give, cot_ahead = lax.optimization_barrier((hidden, d_keep, d_give, cot_ahead))
+    d_half = sum_y(sum_core(d_keep, d_give))
     cot_here = jnp.concatenate(after(cot_ahead, d_half), axis=0)
     cot_there = swap(cot_here, "y")
     d_normed_two = join_core(d_half, core).astype(F32)
@@ -550,35 +640,30 @@
     )
     d_attn = d_hidden_in.astype(BF16)
     d_attended = mm(d_attn, o_weight, 1, 1).astype(BF16)
-    part = width // n
+    part, small = width // n, width // (n * ntp)
     g_o = mm(d_attn, attended, 0, 0).astype(BF16).reshape(nz, 2, part, heads * hd).swapaxes(0, 1)
-    d_attended, g_o = lax.optimization_barrier((d_attended, g_o))
-    g_o = sum_x(g_o, x)
-
-    d_query_rot, keep_near, keep_far, give_near, give_far = attend_back(
-        scal, query_rot, kv, lo, attended, logs, d_attended
-    )
-    d_query_rot, g_o, cot_there = lax.optimization_barrier((d_query_rot, g_o, cot_there))
+    keep_o = lax.dynamic_index_in_dim(g_o, x, 0, keepdims=False)
+    give_o = lax.dynamic_index_in_dim(g_o, 1 - x, 0, keepdims=False)
+    d_attended, keep_o, give_o = lax.optimization_barrier((d_attended, keep_o, give_o))
+    came_o = swap(give_o, "x")
+
+    back = attend_back(scal, query_rot, kv, lo, attended, logs, d_attended, cos_back, sin_back)
+    back, came_o, cot_there = lax.optimization_barrier((back, came_o, cot_there))
+    d_query, keep_near, keep_far, give_near, give_far = back
     cots = (cotangent, cot_here, cot_there, swap(cot_here, "core"), swap(cot_there, "core"))
     d_far = (keep_far.astype(F32) + swap(give_far, "core").astype(F32)).astype(BF16)
     came_near = swap(give_near, "core")
-    came_far = swap(d_far, "x")
-    g_o = lax.all_to_all(g_o, "z", split_axis=0, concat_axis=0, tiled=True)
-    d_query_rot, hidden = after((d_query_rot, hidden), d_far)
-    mlp_part = mm(hidden, down_weight, 1, 0)
-    o_half = sum_core(*split_core(mlp_part, core))
-    d_query = rotate(d_query_rot.reshape(rows, heads, hd), cosine[:, None], -sine[:, None])
-    d_query = d_query.astype(BF16).reshape(rows, heads * hd)
-    g_q = mm(normed, d_query, 0, 0).astype(BF16).reshape(nz, 2, part, heads * hd).swapaxes(0, 1)
-    came_near, g_q, o_half, normed_all, cots = lax.optimization_barrier((came_near, g_q, o_half, normed_all, cots))
-    g_q = sum_x(g_q, x)
-    o_half = sum_y(o_half)
+    g_q = mm(normed, after(d_query, d_far), 0, 0).astype(BF16).reshape(nz, 2, part, heads * hd)
+    keep_q = lax.dynamic_index_in_dim(g_q, x, 1, keepdims=False)
+    give_q = lax.dynamic_index_in_dim(g_q, 1 - x, 1, keepdims=False)
+    came_near, d_far, keep_q, give_q, normed_all, cots = lax.optimization_barrier(
+        (came_near, d_far, keep_q, give_q, normed_all, cots)
+    )
+    came_far, came_q = swap(d_far, "x"), swap(give_q, "x")
 
     place = jnp.stack([x, z, tp]).astype(jnp.int32)
     keep_down, give_down, d_gate_c, d_up_c = column_first(place, normed_all, cots, gate_s, up_s, down_s, n)
-    came_far, g_o, g_q, o_half, d_gate_c, d_up_c, give_down = lax.optimization_barrier(
-        (came_far, g_o, g_q, o_half, d_gate_c, d_up_c, give_down)
-    )
+    came_far, came_q, d_gate_c, give_down = lax.optimization_barrier((came_far, came_q, d_gate_c, give_down))
     ring = [
         (keep_near[s].astype(F32) + came_near[s].astype(F32) + came_far[s].astype(F32)).astype(BF16)
         for s in range(nz)
@@ -586,11 +671,8 @@
     ring, give_down, d_gate_c = lax.optimization_barrier((ring, give_down, d_gate_c))
     ring = ring[:1] + [along_z(ring[s], s) for s in range(1, nz)]
     came_down = swap(give_down, "x")
-    g_q = lax.all_to_all(g_q, "z", split_axis=0, concat_axis=0, tiled=True)
     keep_gate, give_gate, keep_up, give_up = column_second(place, normed_all, d_gate_c, d_up_c, rows, n)
-    came_down, ring, g_q, give_gate, give_up = lax.optimization_barrier((came_down, ring, g_q, give_gate, give_up))
-    d_kv = sum(r.astype(F32) for r in ring)
-    d_kv = jnp.where(core == 0, rotate(d_kv, cosine, -sine), d_kv).astype(BF16)
+    came_down, ring, give_gate, give_up = lax.optimization_barrier((came_down, ring, give_gate, give_up))
 
     def sum_parts(keep, came):
         return [(keep[s].astype(F32) + came[s].astype(F32)).astype(BF16) for s in range(nz)]
@@ -598,26 +680,33 @@
     def spread(sums):
         return sums[:1] + [along_z(sums[s], s) for s in range(1, nz)]
 
-    sums, give_gate = lax.optimization_barrier((sum_parts(keep_down, came_down), give_gate))
+    sums, give_gate, ring = lax.optimization_barrier((sum_parts(keep_down, came_down), give_gate, ring))
     came_gate, g_down = swap(give_gate, "x"), spread(sums)
-    d_normed = mm(d_query, q_weight, 1, 1) + mm(d_kv, kv_cols, 1, 1)
-    d_normed = sum_core(*split_core(d_normed, core))
-    d_normed, came_gate, g_down = lax.optimization_barrier((d_normed, came_gate, g_down))
-    sums, give_up = lax.optimization_barrier((sum_parts(keep_gate, came_gate), after(give_up, d_normed)))
+    parts = project(core, ring, cos_back, sin_back, d_query, q_weight, kv_cols, hidden, down_weight)
+    parts, came_gate, g_down = lax.optimization_barrier((parts, came_gate, g_down))
+    d_kv = parts[0]
+    sums, give_up, parts = lax.optimization_barrier((sum_parts(keep_gate, came_gate), give_up, parts))
     came_up, g_gate = swap(give_up, "x"), spread(sums)
-    d_normed = sum_y(d_normed)
-    d_normed, came_up, g_gate, o_half = lax.optimization_barrier((d_normed, came_up, g_gate, o_half))
+    d_normed = sum_y(sum_core(*parts[1:3]))
+    o_half = sum_core(*parts[3:])
+    g_o = (keep_o.astype(F32) + came_o.astype(F32)).astype(BF16)
+    g_q = (keep_q.astype(F32) + came_q.astype(F32)).astype(BF16)
+    g_oq = jnp.concatenate([g_o, g_q], axis=2)
+    g_oq = [lax.dynamic_index_in_dim(g_oq, lax.rem(z + s, nz), 0, keepdims=False) for s in range(nz)]
+    g_kv = mm(normed, d_kv, 0, 0).astype(BF16).reshape(n * ntp, small, hd)
+    d_normed, came_up, g_gate, o_half, g_oq, g_kv = lax.optimization_barrier(
+        (d_normed, came_up, g_gate, o_half, g_oq, g_kv)
+    )
     sums, d_normed = lax.optimization_barrier((sum_parts(keep_up, came_up), d_normed))
     g_up = spread(sums)
-    d_normed = join_core(d_normed, core).astype(F32)
-    w_one = inputs * factor_one
-    part_attn_gain = jnp.sum(d_normed * w_one, axis=0)
-    dg_one = d_normed * gain_one
-    dx = d_hidden_in + factor_one * (dg_one - w_one * jnp.mean(dg_one * w_one, axis=-1, keepdims=True))
+    g_oq = spread(g_oq)
+    o_half = sum_y(o_half)
+    d_normed = join_core(d_normed, core)
+    dx, part_attn_gain = norm_back(layer_input, factor_one, attn_gain, d_normed, d_hidden_in)
+    dx, part_attn_gain, g_up, o_half = lax.optimization_barrier((dx, part_attn_gain, g_up, o_half))
     output = (hidden_in + join_core(o_half, core).astype(F32)).astype(BF16)
 
-    small, bias_cols = width // (n * ntp), hd // n
-    g_kv = mm(normed, d_kv, 0, 0).astype(BF16).reshape(nz, 2, ntp, small, hd)
+    bias_cols = hd // n
     q_bias_sum = jnp.sum(d_query.astype(F32), axis=0).reshape(heads, n, bias_cols).transpose(1, 0, 2)
     tail_rows = jnp.concatenate(
         [
@@ -630,13 +719,12 @@
     )
     extra = -(-tail_rows.shape[1] // (EXTRA * hd)) * EXTRA
     tail_rows = jnp.pad(tail_rows, ((0, 0), (0, extra * hd - tail_rows.shape[1]))).astype(BF16)
-    tail_rows = jnp.broadcast_to(tail_rows.reshape(nz, 2, 1, extra, hd), (nz, 2, ntp, extra, hd))
-    g_kv = sum_x(jnp.concatenate([g_kv, tail_rows], axis=3).swapaxes(0, 1), x)
+    tail_rows = jnp.broadcast_to(tail_rows.reshape(n, 1, extra, hd), (n, ntp, extra, hd)).reshape(-1, extra, hd)
     g_kv = lax.all_to_all(
-        g_kv.reshape(nz * ntp, small + extra, hd), ("z", "y", "core"), split_axis=0, concat_axis=0, tiled=True
-    )
-    g_kv, dx, output, g_up = lax.optimization_barrier((g_kv, dx, output, g_up))
-    g_kv = jnp.sum(g_kv.reshape(nz, ntp, small + extra, hd).astype(F32), axis=0)
+        jnp.concatenate([g_kv, tail_rows], axis=1), ("z", "x", "y", "core"), split_axis=0, concat_axis=0, tiled=True
+    )
+    g_kv, dx, output, g_oq = lax.optimization_barrier((g_kv, dx, output, g_oq))
+    g_kv = jnp.sum(g_kv.reshape(n, ntp, small + extra, hd).astype(F32), axis=0)
     sums = lax.dynamic_index_in_dim(g_kv[:, small:], tp, 0, keepdims=False).reshape(-1)[hd:]
     g_mlp_gain = sums[:part]
     g_attn_gain = sums[part : 2 * part]
@@ -647,8 +735,9 @@
     g_kv = g_kv[:small]
 
     g_gate, g_up, g_down = assemble(place, g_gate, g_up, g_down)
-    g_o = jnp.sum(g_o.astype(F32), axis=0).T
-    g_q = jnp.sum(g_q.astype(F32), axis=0)
+    g_down = g_down.T
+    g_oq = sum(g.astype(F32) for g in g_oq)
+    g_o, g_q = g_oq[:, : heads * hd].T, g_oq[:, heads * hd :]
 
     return (
         output,

time: 454 us -> 399 us (0.88)
  matrix products: 68.7 us -> 19.4 us
  starting transfers between devices: 107 us -> 79.1 us
  waiting for transfers between devices: 87.3 us -> 115 us
  other arithmetic: 64.4 us -> 40 us
  Pallas kernels: 54.4 us -> 77.7 us
    dot_general x15 -> x8, matrix products: 68.7 us -> 19.4 us  [mm(): lax.dot_general(a, b, (((ca,), (cb,)), ((), ())), preferred_element_type=...]
    ppermute x30 -> x29, waiting for transfers between devices: 62.8 us -> 95.8 us  [swap(): return lax.ppermute(x, axis, [(0, 1), (1, 0)])]
    pallas_call x1 -> x4, Pallas kernels: 6.77 us -> 36.9 us  [the longest x1 22.1 us: mlp(): pl.pallas_call(mlp_kernel, grid=(FF_STEPS,), in_specs=[SMEM, VMEM, tokens...]
    all_to_all x3 -> x1, starting transfers between devices: 35.9 us -> 9.93 us  [per_device(): lax.all_to_all(jnp.concatenate([g_kv, tail_rows], axis=1), ('z', 'x', 'y'...]
    ppermute x3 -> x0, starting transfers between devices: 13.6 us -> none  [column_start(): lax.ppermute(own, 'z', [(i, (i + s) % nz) for i in range(nz)])]
    ppermute x12 -> x18, waiting for transfers between devices: 17.9 us -> 8.01 us  [along_z(): lax.ppermute(block, 'z', [(i, (i + distance) % nz) for i in range(nz)])]
    ppermute x12 -> x18, starting transfers between devices: 22.8 us -> 30.5 us  [along_z(): lax.ppermute(block, 'z', [(i, (i + distance) % nz) for i in range(nz)])]
    unnamed x115 -> x228, local copies, waits for them, and re-layouts: 16.9 us -> 23.6 us
  transfers between devices with their start and end apart: 50 -> 50, of which waited for: 11 -> 17; matrix products, arithmetic and copies ran while one was open for 31% -> 17% of each run, Pallas kernels for 11% -> 20%
where the time goes in v3:
time: 399 us; the launch traced here: 392 us
  waiting for transfers between devices  115 us (29%)
  starting transfers between devices  79.1 us (20%)
  Pallas kernels  77.7 us (19%)
  local copies, waits for them, and re-layouts  43.2 us (11%)
  other arithmetic  40 us (10%)
  matrix products  19.4 us (5%)
  between operations  17.9 us (4%)
    ppermute x29, waiting for transfers between devices, swap(): return lax.ppermute(x, axis, [(0, 1), (1, 0)])  95.8 us
    ppermute x29, starting transfers between devices, swap(): return lax.ppermute(x, axis, [(0, 1), (1, 0)])  33.8 us
    ppermute x18, starting transfers between devices, along_z(): lax.ppermute(block, 'z', [(i, (i + distance) % nz) for i in range(nz)])  30.5 us
    unnamed x228, local copies, waits for them, and re-layouts  23.6 us
    pallas_call x1, Pallas kernels, column_first(): pl.pallas_call(functools.partial(column_first_kernel, quarters), in_specs...  22.6 us
    pallas_call x1, Pallas kernels, mlp(): pl.pallas_call(mlp_kernel, grid=(FF_STEPS,), in_specs=[SMEM, VMEM, tokens...  22.1 us
    dot_general x8, matrix products, mm(): lax.dot_general(a, b, (((ca,), (cb,)), ((), ())), preferred_element_type=...  19.4 us
    pallas_call x1, Pallas kernels, column_second(): pl.pallas_call(functools.partial(column_second_kernel, 4, rows), in_specs...  11.3 us
  transfers between devices with their start and end apart: 50, of which 17 were waited for; matrix products, arithmetic and copies ran while one was open for 17% of the time, Pallas kernels for 20%

profile of v3, /device:TPU:0, one launch (start us, length us, event | category | flops | bytes accessed | tf_op | source)
XLA Modules:
  0.0 391.8 jit_solution(13896322037562530036)
XLA Ops:
  17.8 4.9 %all-to-all-start = ((bf16[4,528,128]{2,1,0:T(8,128)(2,1)}), bf16[4,528,128]{2,1,0:T(8,128)(2,1)S(1)}, u32[]{:S(2)}, u32[]{:S(2)}) async-start(bf16[4,528,128]{2,1,0:T(8,128)(2,1)} %broadcast_in_dim.22), calls=%async_computation | async-start | bytes 1081344 | tf_op jit(solution)/shard_map/all_to_all | solution.py:594
  32.6 4.0 %dynamic-slice_bitcast_fusion = (bf16[560,1536]{1,0:T(8,128)(2,1)}, bf16[560,1536]{1,0:T(8,128)(2,1)}) fusion(bf16[1536,2240]{0,1:T(8,128)(2,1)} %param.25, s32[]{:T(128)S(6)} %select_n.173, bf16[1536,2240]{0,1:T(8,128)(2,1)} %param.24), kind=kLoop, calls=%fused_computation.30 | loop fusion | bytes 6881284 | tf_op jit(solution)/shard_map/dynamic_slice | solution.py:572
  43.8 7.3 %collective-permute-done.r1 = bf16[4,528,128]{2,1,0:T(8,128)(2,1)S(1)} collective-permute-done((bf16[4,528,128]{2,1,0:T(8,128)(2,1)S(1)}, bf16[4,528,128]{2,1,0:T(8,128)(2,1)S(1)}, u32[]{:S(2)}, u32[]{:S(2)}) %collective-permute-start) | collective-permute-done | bytes 540704 | tf_op jit(solution)/shard_map/ppermute | solution.py:36
  59.6 4.2 %collective-permute-start.7 = (bf16[128,1536]{1,0:T(8,128)(2,1)}, bf16[128,1536]{1,0:T(8,128)(2,1)}, u32[]{:S(2)}, u32[]{:S(2)}) collective-permute-start(bf16[128,1536]{1,0:T(8,128)(2,1)} %collective-permute-done.3), channel_id=1, source_target_pairs={{0,8},{8,16},{16,24},{24,0},{1,9},{9,17},{17,25},{25,1},{2,10},{10... | collective-permute-start | bytes 1179656 | tf_op jit(solution)/shard_map/ppermute | solution.py:80
  63.8 7.9 %fusion.8.dh_ref = bf16[2240,512]{1,0:T(8,128)(2,1)} fusion(bf16[512,1536]{1,0:T(8,128)(2,1)S(1)} %copy-done.73, bf16[2240,1536]{1,0:T(8,128)(2,1)} %refs_10_.1), kind=kOutput, calls=%fused_computation.12 | convolution fusion | flops 3524362240 | bytes 10747904 | tf_op jit(solution)/shard_map/dot_general | solution.py:19
  74.6 5.6 %collective-permute-done.7 = bf16[128,1536]{1,0:T(8,128)(2,1)} collective-permute-done((bf16[128,1536]{1,0:T(8,128)(2,1)}, bf16[128,1536]{1,0:T(8,128)(2,1)}, u32[]{:S(2)}, u32[]{:S(2)}) %collective-permute-start.7) | collective-permute-done | bytes 393248 | tf_op jit(solution)/shard_map/ppermute | solution.py:80
  87.3 22.1 %mlp.1 = (bf16[2240,512]{1,0:T(8,128)(2,1)S(1)}, f32[256,1536]{1,0:T(8,128)S(1)}, bf16[256,1536]{1,0:T(8,128)(2,1)S(1)}) custom-call(s32[1]{0:T(128)} %bitcast.7.scal, bf16[512,1536]{1,0:T(8,128)(2,1)S(1)} %multiply_convert_fusion.n_ref, bf16[2240,512]{1,0:T(8,128)(2,1)S(1)} %copy-done.59, bf16[2240,1536]{1,0:T(8,128)(2,1)} %bitcast.116, ...), custom_call_target="tpu_custom_call" | custom-call | flops 13799999488 | tf_op jit(solution)/shard_map/mlp/pallas_call | solution.py:437
  113.6 29.3 %collective-permute-done.13 = bf16[256,1536]{1,0:T(8,128)(2,1)S(1)} collective-permute-done((bf16[256,1536]{1,0:T(8,128)(2,1)S(1)}, bf16[256,1536]{1,0:T(8,128)(2,1)S(1)}, u32[]{:S(2)}, u32[]{:S(2)}) %collective-permute-start.13) | collective-permute-done | bytes 786464 | tf_op jit(solution)/shard_map/ppermute | solution.py:36
  154.4 8.2 %collective-permute-start.15 = (bf16[4,192,384]{2,1,0:T(8,128)(2,1)S(1)}, bf16[4,192,384]{2,1,0:T(8,128)(2,1)S(1)}, u32[]{:S(2)}, u32[]{:S(2)}) collective-permute-start(bf16[4,192,384]{2,1,0:T(8,128)(2,1)S(1)} %get-tuple-element.188), channel_id=1, source_target_pairs={{0,4},{4,0},{1,5},{5,1},{2,6},{6,2},{3,7},{7,3},{8,12},{12,8},{9,1... | collective-permute-start | bytes 1769480 | tf_op jit(solution)/shard_map/ppermute | solution.py:36
  162.6 5.4 %attend_back.1 = (bf16[512,384]{1,0:T(8,128)(2,1)S(1)}, bf16[4,512,128]{2,1,0:T(8,128)(2,1)S(1)}, bf16[4,512,128]{2,1,0:T(8,128)(2,1)S(1)}, bf16[4,512,128]{2,1,0:T(8,128)(2,1)S(1)}, bf16[4,512,128]{2,1,0:T(8,128)(2,1)S(1)}) custom-call(s32[4]{0:T(128)S(1)} %pad_add_fusion.1.scal, bf16[512,384]{1,0:T(8,128)(2,1)S(1)} %copy-done.19, ...), custom_call_target="tpu_custom_call" | custom-call | flops 9200000000 | tf_op jit(solution)/shard_map/attend_back/pallas_call | solution.py:261
  168.0 6.9 %collective-permute-done.16.refs_2_ = bf16[384,1536]{1,0:T(8,128)(2,1)S(1)} collective-permute-done((bf16[384,1536]{1,0:T(8,128)(2,1)S(1)}, bf16[384,1536]{1,0:T(8,128)(2,1)S(1)}, u32[]{:S(2)}, u32[]{:S(2)}) %collective-permute-start.16) | collective-permute-done | bytes 1179680 | tf_op jit(solution)/shard_map/ppermute | solution.py:36
  183.5 6.9 %collective-permute-start.21 = (bf16[4,512,128]{2,1,0:T(8,128)(2,1)}, bf16[4,512,128]{2,1,0:T(8,128)(2,1)S(1)}, u32[]{:S(2)}, u32[]{:S(2)}) collective-permute-start(bf16[4,512,128]{2,1,0:T(8,128)(2,1)} %add_convert_fusion.9), channel_id=1, source_target_pairs={{0,4},{4,0},{1,5},{5,1},{2,6},{6,2},{3,7},{7,3},{8,12},{12,8},{9,1... | collective-permute-start | bytes 1572872 | tf_op jit(solution)/shard_map/ppermute | solution.py:36
  191.8 22.6 %column_first.1 = (bf16[4,192,560]{2,1,0:T(8,128)(2,1)S(1)}, bf16[4,192,560]{2,1,0:T(8,128)(2,1)S(1)}, bf16[560,2048]{1,0:T(8,128)(2,1)}, bf16[560,2048]{1,0:T(8,128)(2,1)}) custom-call(s32[3]{0:T(128)S(1)} %pad_add_fusion.scal, bf16[2048,1536]{1,0:T(8,128)(2,1)} %all-gather.2.cloned.1.call-done.normed, bf16[512,1536]{1,0:T(8,128)(2,1)} %refs_0_, ...), custom_call_target="tpu_custom_call" | custom-call | flops 16099999744 | tf_op jit(solution)/shard_map/column_first/pallas_call | solution.py:371
  218.9 4.6 %collective-permute-start.25 = (bf16[512,128]{1,0:T(8,128)(2,1)S(1)}, bf16[512,128]{1,0:T(8,128)(2,1)S(1)}, u32[]{:S(2)}, u32[]{:S(2)}) collective-permute-start(bf16[512,128]{1,0:T(8,128)(2,1)S(1)} %get-tuple-element.226), channel_id=1, source_target_pairs={{0,16},{8,24},{16,0},{24,8},{1,17},{9,25},{17,1},{25,9},{2,18},{10... | collective-permute-start | bytes 393224 | tf_op jit(solution)/shard_map/ppermute | solution.py:80
  229.9 11.3 %column_second.1 = (bf16[4,192,560]{2,1,0:T(8,128)(2,1)S(1)}, bf16[4,192,560]{2,1,0:T(8,128)(2,1)S(1)}, bf16[4,192,560]{2,1,0:T(8,128)(2,1)S(1)}, bf16[4,192,560]{2,1,0:T(8,128)(2,1)S(1)}) custom-call(s32[3]{0:T(128)S(1)} %pad_add_fusion.scal, bf16[2048,1536]{1,0:T(8,128)(2,1)} %all-gather.2.cloned.1.call-done.normed, bf16[560,2048]{1,0:T(8,128)(2,1)S(1)} %copy-done.60, ...), custom_call_target="tpu_custom_call" | custom-call | flops 11500000256 | tf_op jit(solution)/shard_map/column_second/pallas_call | solution.py:390
  241.3 5.7 %collective-permute-done.23 = bf16[4,192,560]{2,1,0:T(8,128)(2,1)S(1)} collective-permute-done((bf16[4,192,560]{2,1,0:T(8,128)(2,1)S(1)}, bf16[4,192,560]{2,1,0:T(8,128)(2,1)S(1)}, u32[]{:S(2)}, u32[]{:S(2)}) %collective-permute-start.23) | collective-permute-done | bytes 860192 | tf_op jit(solution)/shard_map/ppermute | solution.py:36
  255.2 6.2 %project.1 = (bf16[512,128]{1,0:T(8,128)(2,1)S(1)}, f32[256,1536]{1,0:T(8,128)S(1)}, bf16[256,1536]{1,0:T(8,128)(2,1)}, f32[256,1536]{1,0:T(8,128)S(1)}, bf16[256,1536]{1,0:T(8,128)(2,1)S(1)}) custom-call(s32[1]{0:T(128)} %bitcast.7.scal, bf16[512,128]{1,0:T(8,128)(2,1)S(1)} %get-tuple-element.236.refs_0_, ...), custom_call_target="tpu_custom_call" | custom-call | flops 34500001792 | tf_op jit(solution)/shard_map/project/pallas_call | solution.py:480
  266.1 7.0 %collective-permute-done.27 = bf16[4,192,560]{2,1,0:T(8,128)(2,1)S(1)} collective-permute-done((bf16[4,192,560]{2,1,0:T(8,128)(2,1)S(1)}, bf16[4,192,560]{2,1,0:T(8,128)(2,1)S(1)}, u32[]{:S(2)}, u32[]{:S(2)}) %collective-permute-start.27) | collective-permute-done | bytes 860192 | tf_op jit(solution)/shard_map/ppermute | solution.py:36
  289.7 14.3 %collective-permute-done.32 = bf16[256,1536]{1,0:T(8,128)(2,1)S(1)} collective-permute-done((bf16[256,1536]{1,0:T(8,128)(2,1)S(1)}, bf16[256,1536]{1,0:T(8,128)(2,1)S(1)}, u32[]{:S(2)}, u32[]{:S(2)}) %collective-permute-start.32) | collective-permute-done | bytes 786464 | tf_op jit(solution)/shard_map/ppermute | solution.py:36
  305.1 6.2 %collective-permute-done.33 = bf16[4,192,560]{2,1,0:T(8,128)(2,1)S(1)} collective-permute-done((bf16[4,192,560]{2,1,0:T(8,128)(2,1)S(1)}, bf16[4,192,560]{2,1,0:T(8,128)(2,1)S(1)}, u32[]{:S(2)}, u32[]{:S(2)}) %collective-permute-start.33) | collective-permute-done | bytes 860192 | tf_op jit(solution)/shard_map/ppermute | solution.py:36
  327.4 12.9 %collective-permute-done.42 = bf16[256,1536]{1,0:T(8,128)(2,1)S(1)} collective-permute-done((bf16[256,1536]{1,0:T(8,128)(2,1)}, bf16[256,1536]{1,0:T(8,128)(2,1)S(1)}, u32[]{:S(2)}, u32[]{:S(2)}) %collective-permute-start.42) | collective-permute-done | bytes 786464 | tf_op jit(solution)/shard_map/ppermute | solution.py:36
  348.8 9.9 %all-to-all-start.1 = ((bf16[32,64,128]{2,1,0:T(8,128)(2,1)}), bf16[32,64,128]{2,1,0:T(8,128)(2,1)}, u32[]{:S(2)}, u32[]{:S(2)}) async-start(bf16[32,64,128]{2,1,0:T(8,128)(2,1)} %pad_maximum_fusion.3), calls=%async_computation.1 | async-start | bytes 1048576 | tf_op jit(solution)/shard_map/all_to_all | solution.py:723
  361.7 3.7 assemble.1
  369.1 9.5 %all-to-all-done.1 = bf16[32,64,128]{2,1,0:T(8,128)(2,1)} async-done(((bf16[32,64,128]{2,1,0:T(8,128)(2,1)}), bf16[32,64,128]{2,1,0:T(8,128)(2,1)}, u32[]{:S(2)}, u32[]{:S(2)}) %all-to-all-start.1) | async-done | bytes 524320 | tf_op jit(solution)/shard_map/all_to_all | solution.py:723
  (413 shorter events, 147.5 us)
Async XLA Ops:
  7.2 64.6 %collective-permute-start.8 = (bf16[384,1536]{1,0:T(8,128)(2,1)}, bf16[384,1536]{1,0:T(8,128)(2,1)}, u32[]{:S(2)}, u32[]{:S(2)}) collective-permute-start(bf16[384,1536]{1,0:T(8,128)(2,1)} %param.22), channel_id=1, source_target_pairs={{0,1},{1,0},{2,3},{3,2},{4,5},{5,4},{6,7},{7,6},{8,9},{9,8},{10,11... | collective-permute-start | bytes 3538952 | tf_op jit(solution)/shard_map/ppermute | solution.py:36
  7.7 35.6 %collective-permute-start.9 = (bf16[384,1536]{1,0:T(8,128)(2,1)}, bf16[384,1536]{1,0:T(8,128)(2,1)}, u32[]{:S(2)}, u32[]{:S(2)}) collective-permute-start(bf16[384,1536]{1,0:T(8,128)(2,1)} %param.22), channel_id=1, source_target_pairs={{0,2},{2,0},{1,3},{3,1},{4,6},{6,4},{5,7},{7,5},{8,10},{10,8},{9,1... | collective-permute-start | bytes 3538952 | tf_op jit(solution)/shard_map/ppermute | solution.py:36
  22.6 160.9 %all-gather.2.cloned.1.call-start = ((), (), s32[]{:S(2)}) async-start(), calls=%async_computation.2 | async-start | bytes 6684672 | tf_op jit(solution)/shard_map/all_gather | solution.py:86
  43.3 28.5 %collective-permute-start.10 = (bf16[384,1536]{1,0:T(8,128)(2,1)}, bf16[384,1536]{1,0:T(8,128)(2,1)}, u32[]{:S(2)}, u32[]{:S(2)}) collective-permute-start(bf16[384,1536]{1,0:T(8,128)(2,1)} %collective-permute-done.9), channel_id=1, source_target_pairs={{0,1},{1,0},{2,3},{3,2},{4,5},{5,4},{6,7},{7,6},{8,9},{9,8},{10,11... | collective-permute-start | bytes 3538952 | tf_op jit(solution)/shard_map/ppermute | solution.py:36
  85.6 23.9 %collective-permute-start.11 = (bf16[128,1536]{1,0:T(8,128)(2,1)}, bf16[128,1536]{1,0:T(8,128)(2,1)S(1)}, u32[]{:S(2)}, u32[]{:S(2)}) collective-permute-start(bf16[128,1536]{1,0:T(8,128)(2,1)} %collective-permute-done.7), channel_id=1, source_target_pairs={{0,8},{8,16},{16,24},{24,0},{1,9},{9,17},{17,25},{25,1},{2,10},{10... | collective-permute-start | bytes 1179656 | tf_op jit(solution)/shard_map/ppermute | solution.py:80
  112.1 30.8 %collective-permute-start.13 = (bf16[256,1536]{1,0:T(8,128)(2,1)S(1)}, bf16[256,1536]{1,0:T(8,128)(2,1)S(1)}, u32[]{:S(2)}, u32[]{:S(2)}) collective-permute-start(bf16[256,1536]{1,0:T(8,128)(2,1)S(1)} %add_convert_fusion.6), channel_id=1, source_target_pairs={{0,2},{2,0},{1,3},{3,1},{4,6},{6,4},{5,7},{7,5},{8,10},{10,8},{9,1... | collective-permute-start | bytes 2359304 | tf_op jit(solution)/shard_map/ppermute | solution.py:36
  145.8 29.2 %collective-permute-start.16 = (bf16[384,1536]{1,0:T(8,128)(2,1)S(1)}, bf16[384,1536]{1,0:T(8,128)(2,1)S(1)}, u32[]{:S(2)}, u32[]{:S(2)}) collective-permute-start(bf16[384,1536]{1,0:T(8,128)(2,1)S(1)} %constant_dynamic-update-slice_fusion.refs_1_), channel_id=1, source_target_pairs={{0,2},{2,0},{1,3},{3,1},{4,6},{6,4},{5,7},{7,5},{8,10},{10,8},{9,1... | collective-permute-start | bytes 3538952 | tf_op jit(solution)/shard_map/ppermute | solution.py:36
  154.4 22.0 %collective-permute-start.15 = (bf16[4,192,384]{2,1,0:T(8,128)(2,1)S(1)}, bf16[4,192,384]{2,1,0:T(8,128)(2,1)S(1)}, u32[]{:S(2)}, u32[]{:S(2)}) collective-permute-start(bf16[4,192,384]{2,1,0:T(8,128)(2,1)S(1)} %get-tuple-element.188), channel_id=1, source_target_pairs={{0,4},{4,0},{1,5},{5,1},{2,6},{6,2},{3,7},{7,3},{8,12},{12,8},{9,1... | collective-permute-start | bytes 1769480 | tf_op jit(solution)/shard_map/ppermute | solution.py:36
  183.5 30.9 %collective-permute-start.21 = (bf16[4,512,128]{2,1,0:T(8,128)(2,1)}, bf16[4,512,128]{2,1,0:T(8,128)(2,1)S(1)}, u32[]{:S(2)}, u32[]{:S(2)}) collective-permute-start(bf16[4,512,128]{2,1,0:T(8,128)(2,1)} %add_convert_fusion.9), channel_id=1, source_target_pairs={{0,4},{4,0},{1,5},{5,1},{2,6},{6,2},{3,7},{7,3},{8,12},{12,8},{9,1... | collective-permute-start | bytes 1572872 | tf_op jit(solution)/shard_map/ppermute | solution.py:36
  190.4 25.1 %collective-permute-start.22 = (bf16[4,192,384]{2,1,0:T(8,128)(2,1)}, bf16[4,192,384]{2,1,0:T(8,128)(2,1)S(1)}, u32[]{:S(2)}, u32[]{:S(2)}) collective-permute-start(bf16[4,192,384]{2,1,0:T(8,128)(2,1)} %get-tuple-element.205), channel_id=1, source_target_pairs={{0,4},{4,0},{1,5},{5,1},{2,6},{6,2},{3,7},{7,3},{8,12},{12,8},{9,1... | collective-permute-start | bytes 1769480 | tf_op jit(solution)/shard_map/ppermute | solution.py:36
  216.3 25.0 %collective-permute-start.24 = (bf16[512,128]{1,0:T(8,128)(2,1)S(1)}, bf16[512,128]{1,0:T(8,128)(2,1)S(1)}, u32[]{:S(2)}, u32[]{:S(2)}) collective-permute-start(bf16[512,128]{1,0:T(8,128)(2,1)S(1)} %get-tuple-element.225), channel_id=1, source_target_pairs={{0,8},{8,16},{16,24},{24,0},{1,9},{9,17},{17,25},{25,1},{2,10},{10... | collective-permute-start | bytes 393224 | tf_op jit(solution)/shard_map/ppermute | solution.py:80
  218.9 22.4 %collective-permute-start.25 = (bf16[512,128]{1,0:T(8,128)(2,1)S(1)}, bf16[512,128]{1,0:T(8,128)(2,1)S(1)}, u32[]{:S(2)}, u32[]{:S(2)}) collective-permute-start(bf16[512,128]{1,0:T(8,128)(2,1)S(1)} %get-tuple-element.226), channel_id=1, source_target_pairs={{0,16},{8,24},{16,0},{24,8},{1,17},{9,25},{17,1},{25,9},{2,18},{10... | collective-permute-start | bytes 393224 | tf_op jit(solution)/shard_map/ppermute | solution.py:80
  224.5 22.4 %collective-permute-start.23 = (bf16[4,192,560]{2,1,0:T(8,128)(2,1)S(1)}, bf16[4,192,560]{2,1,0:T(8,128)(2,1)S(1)}, u32[]{:S(2)}, u32[]{:S(2)}) collective-permute-start(bf16[4,192,560]{2,1,0:T(8,128)(2,1)S(1)} %get-tuple-element.223), channel_id=1, source_target_pairs={{0,4},{4,0},{1,5},{5,1},{2,6},{6,2},{3,7},{7,3},{8,12},{12,8},{9,1... | collective-permute-start | bytes 2580488 | tf_op jit(solution)/shard_map/ppermute | solution.py:36
  277.3 27.7 %collective-permute-start.34 = (bf16[192,560]{1,0:T(8,128)(2,1)S(1)}, bf16[192,560]{1,0:T(8,128)(2,1)S(1)}, u32[]{:S(2)}, u32[]{:S(2)}) collective-permute-start(bf16[192,560]{1,0:T(8,128)(2,1)S(1)} %copy-done.92), channel_id=1, source_target_pairs={{0,8},{8,16},{16,24},{24,0},{1,9},{9,17},{17,25},{25,1},{2,10},{10... | collective-permute-start | bytes 645128 | tf_op jit(solution)/shard_map/ppermute | solution.py:80
  277.8 27.2 %collective-permute-start.35 = (bf16[192,560]{1,0:T(8,128)(2,1)S(1)}, bf16[192,560]{1,0:T(8,128)(2,1)S(1)}, u32[]{:S(2)}, u32[]{:S(2)}) collective-permute-start(bf16[192,560]{1,0:T(8,128)(2,1)S(1)} %copy-done.91), channel_id=1, source_target_pairs={{0,16},{8,24},{16,0},{24,8},{1,17},{9,25},{17,1},{25,9},{2,18},{10... | collective-permute-start | bytes 645128 | tf_op jit(solution)/shard_map/ppermute | solution.py:80
  279.4 25.7 %collective-permute-start.36 = (bf16[192,560]{1,0:T(8,128)(2,1)S(1)}, bf16[192,560]{1,0:T(8,128)(2,1)S(1)}, u32[]{:S(2)}, u32[]{:S(2)}) collective-permute-start(bf16[192,560]{1,0:T(8,128)(2,1)S(1)} %copy-done.90), channel_id=1, source_target_pairs={{0,24},{8,0},{16,8},{24,16},{1,25},{9,1},{17,9},{25,17},{2,26},{10... | collective-permute-start | bytes 645128 | tf_op jit(solution)/shard_map/ppermute | solution.py:80
  287.3 23.9 %collective-permute-start.33 = (bf16[4,192,560]{2,1,0:T(8,128)(2,1)S(1)}, bf16[4,192,560]{2,1,0:T(8,128)(2,1)S(1)}, u32[]{:S(2)}, u32[]{:S(2)}) collective-permute-start(bf16[4,192,560]{2,1,0:T(8,128)(2,1)S(1)} %copy-done.38), channel_id=1, source_target_pairs={{0,4},{4,0},{1,5},{5,1},{2,6},{6,2},{3,7},{7,3},{8,12},{12,8},{9,1... | collective-permute-start | bytes 2580488 | tf_op jit(solution)/shard_map/ppermute | solution.py:36
  316.6 26.3 %collective-permute-start.39 = (bf16[192,560]{1,0:T(8,128)(2,1)}, bf16[192,560]{1,0:T(8,128)(2,1)S(1)}, u32[]{:S(2)}, u32[]{:S(2)}) collective-permute-start(bf16[192,560]{1,0:T(8,128)(2,1)} %get-tuple-element.279), channel_id=1, source_target_pairs={{0,8},{8,16},{16,24},{24,0},{1,9},{9,17},{17,25},{25,1},{2,10},{10... | collective-permute-start | bytes 645128 | tf_op jit(solution)/shard_map/ppermute | solution.py:80
  316.6 29.6 %collective-permute-start.40 = (bf16[192,560]{1,0:T(8,128)(2,1)}, bf16[192,560]{1,0:T(8,128)(2,1)S(1)}, u32[]{:S(2)}, u32[]{:S(2)}) collective-permute-start(bf16[192,560]{1,0:T(8,128)(2,1)} %get-tuple-element.280), channel_id=1, source_target_pairs={{0,16},{8,24},{16,0},{24,8},{1,17},{9,25},{17,1},{25,9},{2,18},{10... | collective-permute-start | bytes 645128 | tf_op jit(solution)/shard_map/ppermute | solution.py:80
  318.1 28.9 %collective-permute-start.41 = (bf16[192,560]{1,0:T(8,128)(2,1)}, bf16[192,560]{1,0:T(8,128)(2,1)S(1)}, u32[]{:S(2)}, u32[]{:S(2)}) collective-permute-start(bf16[192,560]{1,0:T(8,128)(2,1)} %get-tuple-element.281), channel_id=1, source_target_pairs={{0,24},{8,0},{16,8},{24,16},{1,25},{9,1},{17,9},{25,17},{2,26},{10... | collective-permute-start | bytes 645128 | tf_op jit(solution)/shard_map/ppermute | solution.py:80
  320.9 48.2 %collective-permute-start.44 = (bf16[192,768]{1,0:T(8,128)(2,1)}, bf16[192,768]{1,0:T(8,128)(2,1)}, u32[]{:S(2)}, u32[]{:S(2)}) collective-permute-start(bf16[192,768]{1,0:T(8,128)(2,1)} %get-tuple-element.287), channel_id=1, source_target_pairs={{0,8},{8,16},{16,24},{24,0},{1,9},{9,17},{17,25},{25,1},{2,10},{10... | collective-permute-start | bytes 884744 | tf_op jit(solution)/shard_map/ppermute | solution.py:80
  340.3 28.8 %collective-permute-start.45 = (bf16[192,768]{1,0:T(8,128)(2,1)}, bf16[192,768]{1,0:T(8,128)(2,1)}, u32[]{:S(2)}, u32[]{:S(2)}) collective-permute-start(bf16[192,768]{1,0:T(8,128)(2,1)} %get-tuple-element.288), channel_id=1, source_target_pairs={{0,16},{8,24},{16,0},{24,8},{1,17},{9,25},{17,1},{25,9},{2,18},{10... | collective-permute-start | bytes 884744 | tf_op jit(solution)/shard_map/ppermute | solution.py:80
  343.6 25.5 %collective-permute-start.46 = (bf16[192,768]{1,0:T(8,128)(2,1)}, bf16[192,768]{1,0:T(8,128)(2,1)}, u32[]{:S(2)}, u32[]{:S(2)}) collective-permute-start(bf16[192,768]{1,0:T(8,128)(2,1)} %get-tuple-element.289), channel_id=1, source_target_pairs={{0,24},{8,0},{16,8},{24,16},{1,25},{9,1},{17,9},{25,17},{2,26},{10... | collective-permute-start | bytes 884744 | tf_op jit(solution)/shard_map/ppermute | solution.py:80
  348.8 29.8 %all-to-all-start.1 = ((bf16[32,64,128]{2,1,0:T(8,128)(2,1)}), bf16[32,64,128]{2,1,0:T(8,128)(2,1)}, u32[]{:S(2)}, u32[]{:S(2)}) async-start(bf16[32,64,128]{2,1,0:T(8,128)(2,1)} %pad_maximum_fusion.3), calls=%async_computation.1 | async-start | bytes 1048576 | tf_op jit(solution)/shard_map/all_to_all | solution.py:723
  (139 other events, 1366.2 us)
Sparse Core Ops, SparseCore 0:
  85.7 78.2 all-gather.1
